TPU v7x, 128 devices: a whole 4x4x4 slice. The times are simulated.
128 devices in a mesh: req: 16 (over z, y), mlp: 8 (over x, core).
Axes of the slice: x: 4, y: 4, z: 4, core: 2. Of those that a mesh axis runs over, the one named last changes fastest.
Arguments:
- hidden: bfloat16 [8192, 3584], P('req', 'mlp'), may hold values from -6 to 6
- query_heads: bfloat16 [8192, 3584], P('req', 'mlp'), may hold values from -4 to 4
- key_heads: bfloat16 [8192, 3584], P('req', 'mlp'), may hold values from -4 to 4
- value_heads: bfloat16 [8192, 3584], P('req', 'mlp'), may hold values from -6 to 6
- segment_ids: int32 [8192], P('req'), may hold values from 0 to 63, never falling along the last dimension, each value on 1 to 1024 neighbouring positions
- page_table: int32 [16, 32], P('req'), may hold values from 0 to 31, each once within a row
- mamba_conv_input: bfloat16 [8192, 7168], P('req', 'mlp'), may hold values from -6 to 6
- mamba_output_gate: bfloat16 [8192, 7168], P('req', 'mlp'), may hold values from -6 to 6
- state_input_projection: bfloat16 [8192, 128], P('req'), may hold values from -6 to 6
- state_output_projection: bfloat16 [8192, 128], P('req'), may hold values from -6 to 6
- discrete_step_size: float32 [8192, 112], P('req', 'mlp'), may hold values from 0.24 to 100, as said below
- head_decay_rate: float32 [112], P('mlp'), may hold values from 0.00024414062 to 0.05, as said below
- skip_gain: float32 [112], P('mlp'), may hold values from 0.5 to 2
- mamba_gated_norm_gain: float32 [7168], P('mlp'), may hold values from 0.1 to 1.9
- attn_proj: bfloat16 [3584, 3584], P('mlp'), may hold values from -0.09375 to 0.09375
- mamba_output_projection: bfloat16 [7168, 3584], P('mlp'), may hold values from -0.0625 to 0.0625
- mlp_norm_gain: float32 [3584], replicated, may hold values from 0.1 to 1.9
- gate_proj: bfloat16 [3584, 7168], P('req', 'mlp'), may hold values from -0.09375 to 0.09375
- up_proj: bfloat16 [3584, 7168], P('req', 'mlp'), may hold values from -0.09375 to 0.09375
- down_proj: bfloat16 [7168, 3584], P('mlp', 'req'), may hold values from -0.0625 to 0.0625
- next_norm_gain: float32 [3584], P('mlp'), may hold values from 0.1 to 1.9
Outputs:
- new_hidden: bfloat16 [8192, 3584], P('req', 'mlp')
- next_normed: bfloat16 [8192, 3584], P('req', 'mlp')
- kv_cache: bfloat16 [2, 16, 512, 3584], P(None, 'mlp', 'req')
Inputs may be any that keep to these rules, and one draw needn't show every extreme that they name: `segment_ids`: prompt ids never fall along the stream; a prompt has 1 to 1024 tokens and one has exactly 1024. `page_table`: each request group's row names every page of its pool once. `discrete_step_size`: Positive. `head_decay_rate`: Positive.
All inputs are finite; a program needn't handle non-finite values.
Results may differ from a plain program's by a relative error of at most 0.006.
Values may be sent and summed in bfloat16 or wider, within the bound.
No kernel may reach another device: no remote copies, remote signals or barrier semaphores. Data moves between devices by JAX's collectives and lax.ppermute only.
A program may use at most 128 MiB of HBM per device.

v0:
```python
import math

import jax
import jax.numpy as jnp
from jax import lax
from jax.sharding import PartitionSpec as P

HD = 224
MAMBA_HEAD_COUNT = 112
MAMBA_HEAD_SIZE = 64
STATE_SIZE = 64
STATE_GROUPS = 2
REACH = 2
PAGE = 16


EPSILON = 1e-05
exact_mode = lax.Precision.HIGHEST


def from_behind(value, axis, steps):
    count = lax.axis_size(axis)
    leading, last = (max(0, -steps), min(count, count - steps))
    return lax.ppermute(value, axis, [(source, source + steps) for source in range(leading, last)])


def entering(x, axis, combine, identity):
    devices, mine = (lax.axis_size(axis), lax.axis_index(axis))
    everything = jax.tree.map(lambda part: lax.all_gather(part, axis), x)
    start = jax.tree.map(
        lambda part, zero: jnp.broadcast_to(jnp.asarray(zero, part.dtype), part.shape), x, identity
    )

    def step(k, before):
        reached = k < mine
        new = combine(before, jax.tree.map(lambda part: part[k], everything))
        return jax.tree.map(lambda a, b: jnp.where(reached, a, b), new, before)

    return lax.fori_loop(0, devices, step, start)


def attend_rows(
    query_rows, segment_rows, pos_rows, all_keys, all_values, key_segs, key_pos, head_count
):
    row_total = query_rows.shape[0]
    key_total = all_keys.shape[0]
    query_split = query_rows.reshape(row_total, head_count, HD)
    key_split = all_keys.reshape(key_total, head_count, HD)
    value_split = all_values.reshape(key_total, head_count, HD)
    scores = jnp.einsum(
        "qhd,khd->hqk", query_split, key_split, preferred_element_type=jnp.float32
    ) * (1.0 / math.sqrt(HD))
    allowed = (segment_rows[:, None] == key_segs[None, :]) & (key_pos[None, :] <= pos_rows[:, None])
    scores = jnp.where(allowed[None, :, :], scores, -jnp.inf)
    top_score = jnp.max(scores, axis=2, keepdims=True)
    raised = jnp.exp(scores - top_score)
    weights = (raised / jnp.sum(raised, axis=2, keepdims=True)).astype(jnp.bfloat16)
    summed = jnp.einsum("hqk,khd->qhd", weights, value_split, preferred_element_type=jnp.float32)
    return summed.astype(jnp.bfloat16).reshape(row_total, head_count * HD)


def block_contributions(
    input_token_rows,
    input_proj_rows,
    output_proj_rows,
    step_size_rows,
    head_decay_rate,
    segment_rows,
    segment_prior_state,
    group_index,
    head_width,
):
    row_count = input_token_rows.shape[0]
    head_count = step_size_rows.shape[1]
    input_float = input_token_rows.astype(jnp.float32).reshape(row_count, head_count, head_width)
    b_float = input_proj_rows.astype(jnp.float32)
    c_float = output_proj_rows.astype(jnp.float32)
    running = jnp.cumsum(-step_size_rows * head_decay_rate[None, :], axis=0)
    positions = jnp.arange(row_count, dtype=jnp.int32)
    live = (segment_rows[:, None] == segment_rows[None, :]) & (
        positions[:, None] >= positions[None, :]
    )
    spread = running.T[:, :, None] - running.T[:, None, :]
    mixing = jnp.exp(jnp.where(live[None, :, :], spread, -1e30))
    inner = jnp.einsum("tgn,ugn->gtu", c_float, b_float, precision=exact_mode)
    driven = input_float * step_size_rows[:, :, None]
    local_output = jnp.einsum(
        "htu,uhp->thp", mixing * inner[group_index], driven, precision=exact_mode
    )
    b_per_head = b_float[:, group_index, :]
    output_proj_per_head = c_float[:, group_index, :]
    tail_rows = segment_rows == segment_rows[row_count - 1]
    tail_gain = jnp.where(
        tail_rows[:, None], jnp.exp(running[row_count - 1][None, :] - running), 0.0
    )
    state_local_part = jnp.einsum(
        "uh,uhp,uhn->hpn", tail_gain, driven, b_per_head, precision=exact_mode
    )
    decay_cumulative = jnp.where(
        segment_rows[row_count - 1] == segment_prior_state, jnp.exp(running[row_count - 1]), 0.0
    )
    entry_weighting = jnp.where(
        (segment_rows == segment_prior_state)[:, None], jnp.exp(running), 0.0
    )
    return (
        local_output,
        decay_cumulative,
        state_local_part,
        entry_weighting,
        input_float,
        output_proj_per_head,
    )


def finish(local_output, entry_weighting, input_float, output_proj_per_head, carry_in, skip_gain):
    carried = jnp.einsum("hpn,thn->thp", carry_in, output_proj_per_head, precision=exact_mode)
    result = (
        local_output
        + entry_weighting[:, :, None] * carried
        + skip_gain[None, :, None] * input_float
    )
    return result.reshape(result.shape[0], result.shape[1] * result.shape[2])


def merge_states(earlier, later):
    decay_early, state_early = earlier
    decay_late, state_late = later
    return (decay_early * decay_late, decay_late[:, None, None] * state_early + state_late)


def body(
    hidden,
    query_heads,
    key_heads,
    value_heads,
    segment_ids,
    page_table,
    mamba_conv_input,
    mamba_output_gate,
    state_input_projection,
    state_output_projection,
    discrete_step_size,
    head_decay_rate,
    skip_gain,
    mamba_gated_norm_gain,
    attn_proj,
    mamba_output_projection,
    mlp_norm_gain,
    gate_proj,
    up_proj,
    down_proj,
    next_norm_gain,
):
    row_count = query_heads.shape[0]
    head_count = query_heads.shape[1] // HD
    lane_count = hidden.shape[1]
    owner_index = lax.axis_index("req")
    column = lax.axis_index("mlp")
    first_row = owner_index * row_count
    lead_rows = REACH * row_count
    shifted_ids = segment_ids + 1
    key_parts = []
    value_parts = []
    segment_parts = []
    for distance in range(REACH, 0, -1):
        moved_ids = from_behind(shifted_ids, "req", distance)
        segment_parts.append(moved_ids - 1)
        moved_keys, moved_values = from_behind((key_heads, value_heads), "req", distance)
        key_parts.append(moved_keys)
        value_parts.append(moved_values)
    key_segs = jnp.concatenate(segment_parts + [segment_ids], axis=0)
    key_pos = first_row - lead_rows + jnp.arange(lead_rows + row_count, dtype=jnp.int32)
    segment_prior_state = segment_parts[-1][row_count - 1]
    all_keys = jnp.concatenate(key_parts + [key_heads], axis=0)
    all_values = jnp.concatenate(value_parts + [value_heads], axis=0)
    block_rows = min(row_count, 512)

    def one_block(block_index):
        first_local = block_index * block_rows
        pos_rows = first_row + first_local + jnp.arange(block_rows, dtype=jnp.int32)
        return attend_rows(
            query_heads, segment_ids, pos_rows, all_keys, all_values, key_segs, key_pos, head_count
        )

    attended = lax.map(one_block, jnp.arange(row_count // block_rows, dtype=jnp.int32)).reshape(
        row_count, head_count * HD
    )
    page_count = page_table.shape[1]
    key_pages = (
        key_heads.reshape(page_count, PAGE, head_count, HD)
        .transpose(2, 0, 1, 3)
        .reshape(head_count, page_count, PAGE * HD)
    )
    value_pages = (
        value_heads.reshape(page_count, PAGE, head_count, HD)
        .transpose(2, 0, 1, 3)
        .reshape(head_count, page_count, PAGE * HD)
    )
    stacked = jnp.stack([key_pages, value_pages])
    kv_cache = jnp.zeros_like(stacked).at[:, :, page_table[0]].set(stacked)
    mamba_heads = discrete_step_size.shape[1]
    group_values = MAMBA_HEAD_COUNT // STATE_GROUPS
    b_groups = state_input_projection.reshape(row_count, STATE_GROUPS, STATE_SIZE)
    c_groups = state_output_projection.reshape(row_count, STATE_GROUPS, STATE_SIZE)
    group_index = jnp.arange(mamba_heads, dtype=jnp.int32) % STATE_GROUPS
    (
        local_output,
        decay_cumulative,
        state_local_part,
        entry_weighting,
        input_float,
        output_proj_per_head,
    ) = block_contributions(
        mamba_conv_input,
        b_groups,
        c_groups,
        discrete_step_size,
        head_decay_rate,
        segment_ids,
        segment_prior_state,
        group_index,
        MAMBA_HEAD_SIZE,
    )
    unused_decay, carry_in = entering(
        (decay_cumulative, state_local_part),
        "req",
        merge_states,
        (jnp.ones_like(decay_cumulative), jnp.zeros_like(state_local_part)),
    )
    mamba_output = finish(
        local_output, entry_weighting, input_float, output_proj_per_head, carry_in, skip_gain
    )
    gated_output = mamba_output * jax.nn.silu(mamba_output_gate.astype(jnp.float32))
    grouped_values = gated_output.reshape(
        row_count, mamba_heads // STATE_GROUPS, STATE_GROUPS, MAMBA_HEAD_SIZE
    )
    group_squares = jnp.sum(grouped_values * grouped_values, axis=(1, 3))
    running_totals = lax.psum(group_squares, "mlp")
    inverse_group = lax.rsqrt(running_totals / (group_values * MAMBA_HEAD_SIZE) + EPSILON)
    mnormed = (
        (grouped_values * inverse_group[:, None, :, None]).reshape(
            row_count, mamba_heads * MAMBA_HEAD_SIZE
        )
        * mamba_gated_norm_gain[None, :]
    ).astype(jnp.bfloat16)
    projected = jnp.dot(attended, attn_proj, preferred_element_type=jnp.float32) + jnp.dot(
        mnormed, mamba_output_projection, preferred_element_type=jnp.float32
    )
    width_total = projected.shape[1]
    offset = column * lane_count
    own_part = lax.dynamic_slice_in_dim(projected, offset, lane_count, 1) + hidden.astype(
        jnp.float32
    )
    mixed_rows = lax.psum(lax.dynamic_update_slice_in_dim(projected, own_part, offset, 1), "mlp")
    mixed_share = lax.dynamic_slice_in_dim(mixed_rows, offset, lane_count, 1)
    inverse_root_mean = lax.rsqrt(jnp.mean(mixed_rows * mixed_rows, axis=1) + EPSILON)
    normed = (mixed_rows * inverse_root_mean[:, None] * mlp_norm_gain[None, :]).astype(jnp.bfloat16)
    gate_act = jnp.dot(
        normed,
        lax.all_gather(gate_proj, "req", axis=0, tiled=True),
        preferred_element_type=jnp.float32,
    )
    up_act = jnp.dot(
        normed,
        lax.all_gather(up_proj, "req", axis=0, tiled=True),
        preferred_element_type=jnp.float32,
    )
    latent_activation = (jax.nn.silu(gate_act) * up_act).astype(jnp.bfloat16)
    partial_value = jnp.dot(
        latent_activation,
        lax.all_gather(down_proj, "req", axis=1, tiled=True),
        preferred_element_type=jnp.float32,
    )
    mlp_share = lax.psum_scatter(partial_value, "mlp", scatter_dimension=1, tiled=True)
    new_hidden = (mixed_share + mlp_share).astype(jnp.bfloat16)
    widened = new_hidden.astype(jnp.float32)
    total_sq = lax.psum(jnp.sum(widened * widened, axis=1), "mlp")
    next_normed = (
        widened * lax.rsqrt(total_sq / width_total + EPSILON)[:, None] * next_norm_gain[None, :]
    ).astype(jnp.bfloat16)
    return (new_hidden, next_normed, kv_cache)


def solution(mesh):
    return jax.shard_map(
        body,
        mesh=mesh,
        in_specs=(
            P("req", "mlp"),
            P("req", "mlp"),
            P("req", "mlp"),
            P("req", "mlp"),
            P("req"),
            P("req", None),
            P("req", "mlp"),
            P("req", "mlp"),
            P("req", None),
            P("req", None),
            P("req", "mlp"),
            P("mlp"),
            P("mlp"),
            P("mlp"),
            P("mlp", None),
            P("mlp", None),
            P(),
            P("req", "mlp"),
            P("req", "mlp"),
            P("mlp", "req"),
            P("mlp"),
        ),
        out_specs=(P("req", "mlp"), P("req", "mlp"), P(None, "mlp", "req", None)),
        check_vma=False,
    )
```

profile of v0, /device:TPU:96, one launch (start us, length us, event | category | flops | bytes accessed | tf_op | source)
XLA Modules:
  0.0 614.9 jit_solution(2052999723825984348)
XLA Ops:
  8.7 3.5 collective-permute-start.3
  16.8 2.5 copy.75
  25.5 3.5 fusion.22
  29.1 4.8 collective-permute-start.2
  47.1 8.8 %gather_fusion = f32[14,512,512]{2,1,0:T(8,128)} fusion(f32[2,512,512]{2,1,0:T(8,128)} %fusion.59, s32[1024]{0:T(1024)} %copy-done.13), kind=kCustom, calls=%fused_computation | custom fusion | bytes 29360184 | tf_op jit(solution)/shard_map/gather | solution.py:88
  60.6 44.6 %all-gather.1 = f32[16,1,14]{2,1,0:T(1,128)S(1)} all-gather(f32[1,1,14]{2,1,0:T(1,128)S(1)} %bitcast.114), channel_id=1, replica_groups=mesh['req'=16,'mlp'=8] {'req'}, dimensions={0}, use_global_device_ids=true | all-gather | bytes 952 | tf_op jit(solution)/shard_map/all_gather | solution.py:29
  105.3 2.6 pad_maximum_fusion.1
  107.9 2.4 pad_maximum_fusion
  110.2 4.1 fusion.58
  114.3 6.2 %fusion.30 = bf16[2,224,512]{2,1,0:T(8,128)(2,1)} fusion(bf16[1536,2,224]{0,2,1:T(8,128)(2,1)} %bitcast.105, f32[2,512]{1,0:T(2,128)S(1)} %fusion.58, pred[512,1536]{0,1:T(8,128)(4,1)} %compare_and_fusion, bf16[1536,2,224]{0,2,1:T(8,128)(2,1)} %bitcast.104, bf16[512,2,224]{0,2,1:T(8,128)(2,1)} %bitcast.116), kind=kOutput, calls=%fused_computation.49 | convolution fusion | flops 1417382400 | bytes 4460544 | tf_op jit(solution)/shard_map/while/body/eval_jaxpr/hqk,khd->qhd/dot_general | solution.py:58
  120.5 43.8 %while.18 = (s32[]{:T(128)}, f32[14,64,64]{2,1,0:T(8,128)}, s32[]{:T(128)}, f32[16,14]{1,0:T(8,128)S(1)}, f32[16,14,64,64]{3,2,1,0:T(8,128)}, /*index=5*/s32[]{:T(128)}, s32[]{:T(128)}) while((s32[]{:T(128)}, f32[14,64,64]{2,1,0:T(8,128)}, s32[]{:T(128)}, f32[16,14]{1,0:T(8,128)S(1)}, f32[16,14,64,64]{3,2,1,0:T(8,128)}, ...), condition=%wide.region_5.6_spmd.clone, body=%wide.region_4.5_spmd.clone.sunk | while | flops 229380 | bytes 688401 | solution.py:39
  135.6 2.0 fusion.75
  137.6 2.0 fusion.75
  139.7 2.0 fusion.75
  141.7 2.0 fusion.75
  143.8 2.0 fusion.75
  145.8 2.0 fusion.75
  147.9 2.0 fusion.75
  149.9 2.0 fusion.75
  152.0 2.0 fusion.75
  154.0 2.0 fusion.75
  156.1 2.0 fusion.75
  158.1 2.0 fusion.75
  160.2 2.0 fusion.75
  162.2 2.0 fusion.75
  164.3 2.3 fusion.37
  166.7 20.4 %fusion.21 = f32[512,14,64]{0,2,1:T(8,128)} fusion(f32[14,512,64]{1,2,0:T(8,128)S(1)} %fusion.37, f32[512,14,64]{0,2,1:T(8,128)S(1)} %bitcast.98, f32[14,512,512]{2,1,0:T(8,128)} %gather_fusion, f32[14,512]{1,0:T(8,128)S(1)} %bitcast.111, pred[512,512]{1,0:T(8,128)(4,1)S(1)} %copy-done.9, f32[14]{0:T(128)S(1)} %copy-done.18, f32[512,14]{0,1:T(8,128)S(1)} %copy-done.12, ...), kind=kOutput, calls=%fused_computation.38 | convolution fusion | flops 2831876096 | bytes 20533304 | tf_op jit(solution)/shard_map/htu,uhp->thp/dot_general | solution.py:87
  187.1 2.8 copy.80
  189.8 3.4 fusion.56
  193.3 2.8 copy.81
  197.7 13.5 %psum.21 = f32[512,2]{0,1:T(2,128)S(1)} all-reduce(f32[512,2]{0,1:T(2,128)S(1)} %reduce_sum.38), channel_id=1, replica_groups=mesh['req'=16,'mlp'=8] {'mlp'}, use_global_device_ids=true, to_apply=%region_7.8 | all-reduce | flops 1024 | bytes 8192 | tf_op jit(solution)/shard_map/psum | solution.py:238
  212.7 2.7 copy.82
  215.5 8.2 %fusion.35 = f32[512,3584]{1,0:T(8,128)S(1)} fusion(bf16[896,3584]{1,0:T(8,128)(2,1)} %param.38, f32[512,896]{1,0:T(8,128)} %copy.82, f32[896]{0:T(1024)S(1)} %copy-done.17, f32[512,896]{1,0:T(8,128)} %copy.80, bf16[512,896]{1,0:T(8,128)(2,1)} %param.30), kind=kOutput, calls=%fused_computation.57 | convolution fusion | flops 3292463104 | bytes 18353664 | tf_op jit(solution)/shard_map/dot_general | solution.py:246
  223.7 2.2 convolution_add_fusion
  225.9 3.0 copy-done.2
  229.3 5.8 dynamic_update_slice.6
  237.1 89.8 %all-reduce.2.cloned.1.call-done = f32[512,3584]{1,0:T(8,128)} async-done(((f32[512,3584]{1,0:T(8,128)}), f32[512,3584]{1,0:T(8,128)}) %all-reduce.2.cloned.1.call-update) | async-done | bytes 7340048 | tf_op jit(solution)/shard_map/psum | solution.py:254
  326.9 3.6 multiply_reduce_fusion
  330.5 60.1 %all-gather.7.cloned.1.call-done = bf16[3584,896]{1,0:T(8,128)(2,1)} async-done(((bf16[224,896]{1,0:T(8,128)(2,1)}), bf16[3584,896]{1,0:T(8,128)(2,1)}) %all-gather.7.cloned.1.call-update) | async-done | bytes 6422544 | tf_op jit(solution)/shard_map/all_gather | solution.py:260
  390.6 8.4 %fusion.57 = f32[512,896]{1,0:T(8,128)S(1)} fusion(bf16[3584,896]{1,0:T(8,128)(2,1)} %all-gather.7.cloned.1.call-done, f32[512,3584]{1,0:T(8,128)} %all-reduce.2.cloned.1.call-done, f32[3584]{0:T(1024)S(1)} %copy-done.16, f32[512]{0:T(512)S(1)} %add_rsqrt_fusion.2), kind=kOutput, calls=%fused_computation.98 | convolution fusion | flops 3293839360 | bytes 15613952 | tf_op jit(solution)/shard_map/dot_general | solution.py:258
  399.1 55.1 %all-gather.11.cloned.1.call-done = bf16[896,3584]{0,1:T(8,128)(2,1)} async-done(((bf16[896,224]{0,1:T(8,128)(2,1)}), bf16[896,3584]{0,1:T(8,128)(2,1)}) %all-gather.11.cloned.1.call-update) | async-done | bytes 6422544 | tf_op jit(solution)/shard_map/all_gather | solution.py:271
  454.2 63.6 %all-gather.9.cloned.1.call-done = bf16[3584,896]{1,0:T(8,128)(2,1)} async-done(((bf16[224,896]{1,0:T(8,128)(2,1)}), bf16[3584,896]{1,0:T(8,128)(2,1)}) %all-gather.9.cloned.1.call-update) | async-done | bytes 6422544 | tf_op jit(solution)/shard_map/all_gather | solution.py:265
  517.8 17.7 %convolution_bitcast_fusion = f32[3584,512]{1,0:T(8,128)} fusion(bf16[896,3584]{0,1:T(8,128)(2,1)} %all-gather.11.cloned.1.call-done, f32[512,896]{1,0:T(8,128)S(1)} %fusion.57, bf16[3584,896]{1,0:T(8,128)(2,1)} %all-gather.9.cloned.1.call-done, f32[512,3584]{1,0:T(8,128)} %all-reduce.2.cloned.1.call-done, f32[3584]{0:T(1024)S(1)} %copy-done.16, ...), kind=kOutput, calls=%fused_computation.19 | convolution fusion | flops 6584926208 | bytes 29376512
  541.1 2.6 scatter_fusion
  544.6 38.3 %reduce-scatter.4.cloned.1.call-done = f32[448,512]{1,0:T(8,128)} async-done(((f32[3584,512]{1,0:T(8,128)}), f32[448,512]{1,0:T(8,128)}) %reduce-scatter.4.cloned.1.call-update) | async-done | bytes 917520
  582.9 2.7 copy.96
  585.6 2.8 fusion.31
  588.4 13.2 %psum.23 = f32[512]{0:T(512)S(1)} all-reduce(f32[512]{0:T(512)S(1)} %get-tuple-element.167), channel_id=1, replica_groups=mesh['req'=16,'mlp'=8] {'mlp'}, use_global_device_ids=true, to_apply=%region_12.13 | all-reduce | flops 512 | bytes 4096 | tf_op jit(solution)/shard_map/psum | solution.py:277
  (135 shorter events, 50.8 us)
Async XLA Ops:
  7.2 216.5 %copy-start = (bf16[448,3584]{1,0:T(8,128)(2,1)S(1)}, bf16[448,3584]{1,0:T(8,128)(2,1)}, u32[]{:S(2)}) copy-start(bf16[448,3584]{1,0:T(8,128)(2,1)} %param.37) | copy-start | bytes 9633796
  7.2 113.3 %all-gather.13.cloned.1.call-start = ((), (), s32[]{:S(2)}) async-start(), calls=%async_computation.5 | async-start | bytes 7798784 | tf_op jit(solution)/shard_map/all_gather | solution.py:29
  8.7 12.2 %collective-permute-start.3 = (s32[512]{0:T(512)}, s32[512]{0:T(512)S(1)}, u32[]{:S(2)}, u32[]{:S(2)}) collective-permute-start(s32[512]{0:T(512)} %broadcast_add_fusion.3), channel_id=1, source_target_pairs={{0,8},{8,16},{16,24},{24,32},{32,40},{40,48},{48,56},{56,64},{64,7... | collective-permute-start | bytes 6152 | tf_op jit(solution)/shard_map/ppermute | solution.py:24
  14.5 6.4 %copy-start.13 = (s32[1024]{0:T(1024)}, s32[1024]{0:T(1024)S(1)}, u32[]{:S(2)}) copy-start(s32[1024]{0:T(1024)S(1)} %pad_clamp_fusion) | copy-start | bytes 12292
  19.3 3.4 copy-start.11
  19.3 6.2 %copy-start.10 = (f32[512,14]{0,1:T(8,128)S(1)}, f32[512,14]{0,1:T(8,128)}, u32[]{:S(2)}) copy-start(f32[512,14]{0,1:T(8,128)} %param.33) | copy-start | bytes 86020
  29.0 297.8 %all-reduce.2.cloned.1.call-start = ((), (), s32[]{:S(2)}) async-start(), calls=%async_computation.1 | async-start | bytes 14680064 | tf_op jit(solution)/shard_map/psum | solution.py:254
  29.1 28.9 %collective-permute-start.2 = (s32[512]{0:T(512)}, s32[512]{0:T(512)}, u32[]{:S(2)}, u32[]{:S(2)}) collective-permute-start(s32[512]{0:T(512)} %broadcast_add_fusion.3), channel_id=1, source_target_pairs={{0,16},{8,24},{16,32},{24,40},{32,48},{40,56},{48,64},{56,72},{64,... | collective-permute-start | bytes 6152 | tf_op jit(solution)/shard_map/ppermute | solution.py:24
  33.9 71.4 %collective-permute-start.4 = (bf16[512,448]{0,1:T(8,128)(2,1)}, bf16[512,448]{0,1:T(8,128)(2,1)}, u32[]{:S(2)}, u32[]{:S(2)}) collective-permute-start(bf16[512,448]{0,1:T(8,128)(2,1)} %param.25), channel_id=1, source_target_pairs={{0,16},{8,24},{16,32},{24,40},{32,48},{40,56},{48,64},{56,72},{64,... | collective-permute-start | bytes 1376264 | tf_op jit(solution)/shard_map/ppermute | solution.py:24
  35.8 69.4 %collective-permute-start.5 = (bf16[512,448]{0,1:T(8,128)(2,1)}, bf16[512,448]{0,1:T(8,128)(2,1)}, u32[]{:S(2)}, u32[]{:S(2)}) collective-permute-start(bf16[512,448]{0,1:T(8,128)(2,1)} %param.25), channel_id=1, source_target_pairs={{0,8},{8,16},{16,24},{24,32},{32,40},{40,48},{48,56},{56,64},{64,7... | collective-permute-start | bytes 1376264 | tf_op jit(solution)/shard_map/ppermute | solution.py:24
  37.8 70.1 %collective-permute-start = (bf16[512,448]{0,1:T(8,128)(2,1)}, bf16[512,448]{0,1:T(8,128)(2,1)}, u32[]{:S(2)}, u32[]{:S(2)}) collective-permute-start(bf16[512,448]{0,1:T(8,128)(2,1)} %param.26), channel_id=1, source_target_pairs={{0,16},{8,24},{16,32},{24,40},{32,48},{40,56},{48,64},{56,72},{64,... | collective-permute-start | bytes 1376264 | tf_op jit(solution)/shard_map/ppermute | solution.py:24
  39.7 68.2 %collective-permute-start.1 = (bf16[512,448]{0,1:T(8,128)(2,1)}, bf16[512,448]{0,1:T(8,128)(2,1)}, u32[]{:S(2)}, u32[]{:S(2)}) collective-permute-start(bf16[512,448]{0,1:T(8,128)(2,1)} %param.26), channel_id=1, source_target_pairs={{0,8},{8,16},{16,24},{24,32},{32,40},{40,48},{48,56},{56,64},{64,7... | collective-permute-start | bytes 1376264 | tf_op jit(solution)/shard_map/ppermute | solution.py:24
  47.1 13.5 %copy-start.15 = (f32[14]{0:T(128)S(1)}, f32[14]{0:T(128)}, u32[]{:S(2)}) copy-start(f32[14]{0:T(128)} %get-tuple-element.156) | copy-start | bytes 172
  58.0 49.9 %copy-start.6 = (bf16[512,448]{0,1:T(8,128)(2,1)S(1)}, bf16[512,448]{0,1:T(8,128)(2,1)}, u32[]{:S(2)}) copy-start(bf16[512,448]{0,1:T(8,128)(2,1)} %param.26) | copy-start | bytes 1376260
  164.3 2.3 copy-start.3
  164.3 2.3 copy-start.9
  164.3 2.4 copy-start.12
  164.3 2.4 copy-start.18
  211.3 4.2 copy-start.17
  215.5 8.2 %copy-start.8 = (bf16[2,224,512]{2,1,0:T(8,128)(2,1)S(1)}, bf16[2,224,512]{2,1,0:T(8,128)(2,1)}, u32[]{:S(2)}) copy-start(bf16[2,224,512]{2,1,0:T(8,128)(2,1)} %fusion.30) | copy-start | bytes 1376260
  223.7 5.2 copy-start.4
  225.9 3.0 copy-start.2
  235.1 155.5 %all-gather.7.cloned.1.call-start = ((), (), s32[]{:S(2)}) async-start(), calls=%async_computation.2 | async-start | bytes 6823936 | tf_op jit(solution)/shard_map/all_gather | solution.py:260
  235.8 218.4 %all-gather.11.cloned.1.call-start = ((), (), s32[]{:S(2)}) async-start(), calls=%async_computation.4 | async-start | bytes 6823936 | tf_op jit(solution)/shard_map/all_gather | solution.py:271
  236.4 281.4 %all-gather.9.cloned.1.call-start = ((), (), s32[]{:S(2)}) async-start(), calls=%async_computation.3 | async-start | bytes 6823936 | tf_op jit(solution)/shard_map/all_gather | solution.py:265
  237.0 153.6 %copy-start.16 = (f32[3584]{0:T(1024)S(1)}, f32[3584]{0:T(1024)}, u32[]{:S(2)}) copy-start(f32[3584]{0:T(1024)} %param.39) | copy-start | bytes 43012
  237.0 345.9 %reduce-scatter.4.cloned.1.call-start = ((), (), s32[]{:S(2)}) async-start(), calls=%async_computation.6 | async-start | bytes 8257536
  535.5 1.0 copy-start.5
  535.5 1.2 copy-start.7
  538.6 2.0 copy-start.19
  582.9 20.8 %copy-start.14 = (f32[448]{0:T(512)S(1)}, f32[448]{0:T(512)}, u32[]{:S(2)}) copy-start(f32[448]{0:T(512)} %param.43) | copy-start | bytes 5380
  582.9 24.8 %copy-start.1 = (bf16[448,3584]{1,0:T(8,128)(2,1)S(1)}, bf16[448,3584]{1,0:T(8,128)(2,1)}, u32[]{:S(2)}) copy-start(bf16[448,3584]{1,0:T(8,128)(2,1)} %param.37) | copy-start | bytes 9633796
Sparse Core Ops, SparseCore 0:
  29.2 87.9 all-gather.12
  235.2 91.6 all-reduce.1
  329.0 61.5 all-gather.6
  392.6 61.5 all-gather.10
  456.2 61.5 all-gather.8
  535.7 47.1 reduce-scatter.3
where the time goes:
time: 626 us; the launch traced here: 615 us
  waiting for transfers between devices  309 us (49%)
  matrix products  75 us (12%)
  blocking collectives  71.4 us (11%)
  other arithmetic  61.4 us (10%)
  local copies, waits for them, and re-layouts  55 us (9%)
  starting transfers between devices  16.2 us (3%)
  between operations  16.2 us (3%)
  loops' own time  11.1 us (2%)
    psum x1, waiting for transfers between devices, body(): lax.psum(lax.dynamic_update_slice_in_dim(projected, own_part, offset, 1),...  89.8 us
    all_gather x1, waiting for transfers between devices, body(): lax.all_gather(up_proj, 'req', axis=0, tiled=True)  63.6 us
    all_gather x1, waiting for transfers between devices, body(): lax.all_gather(gate_proj, 'req', axis=0, tiled=True)  60.1 us
    all_gather x1, waiting for transfers between devices, body(): lax.all_gather(down_proj, 'req', axis=1, tiled=True)  55.1 us
    all_gather x1, blocking collectives, entering(): everything = jax.tree.map(lambda part: lax.all_gather(part, axis), x)  44.6 us
    unnamed x7, waiting for transfers between devices  40 us
    select_n x16, other arithmetic, step(): return jax.tree.map(lambda a, b: jnp.where(reached, a, b), new, before)  32.6 us
    dot_general x1, matrix products, block_contributions(): jnp.einsum('htu,uhp->thp', mixing * inner[group_index], driven, precision...  20.4 us
  transfers between devices with their start and end apart: 12, of which 5 were waited for; matrix products, arithmetic and copies ran while one was open for 10% of the time, Pallas kernels for 0%

commit v1 on v0

v1 whole, which is shorter than its diff:
```python
import math

import jax
import jax.numpy as jnp
from jax import lax
from jax.experimental import pallas as pl
from jax.experimental.pallas import tpu as pltpu
from jax.sharding import Mesh
from jax.sharding import PartitionSpec as P

HD = 224
PAGE = 16
EPS = 1e-05
LOG2E = math.log2(math.e)
T = 512
F32 = jnp.float32
BF16 = jnp.bfloat16
REQ = ("z", "y")
MLP = ("x", "c")
VMEM = pltpu.CompilerParams(vmem_limit_bytes=56 << 20)


def dot(a, b, ca=1, cb=0):
    return lax.dot_general(a, b, (((ca,), (cb,)), ((), ())), preferred_element_type=F32)


def lanes_of(shape):
    return lax.broadcasted_iota(jnp.int32, shape, 1)


def halves(pair, i, rows, base=0):
    low = jnp.broadcast_to(pair[:, base + 2 * i : base + 2 * i + 1], (rows, 128))
    high = jnp.broadcast_to(pair[:, base + 2 * i + 1 : base + 2 * i + 2], (rows, 128))
    return jnp.where(lanes_of((rows, 128)) < 64, low, high)


def state_kernel(dt_ref, rate_ref, seg_ref, x_ref, b_ref, state_ref, row_ref, col_ref, tmp_ref):
    heads = dt_ref.shape[0]
    tiles = x_ref.shape[1] // 128
    tmp_ref[...] = jnp.zeros_like(tmp_ref)
    tmp_ref[0:heads, :] = dt_ref[...] * (rate_ref[...] * -LOG2E)
    tmp_ref[16:32, :] = jnp.ones((16, T), F32)
    tmp_ref[16 : 16 + heads, :] = dt_ref[...]
    run = tmp_ref[0:16, :]
    lane = lanes_of((16, T))
    shift = 1
    while shift < T:
        run = run + jnp.where(lane >= shift, pltpu.roll(run, shift, 1), 0.0)
        shift *= 2
    row = run - jnp.log2(tmp_ref[16:32, :])
    row_ref[...] = row
    last = jnp.sum(jnp.where(lane == T - 1, run, 0.0), axis=1, keepdims=True)
    seg = seg_ref[...]
    tail = jnp.where(seg == jnp.max(seg), 1.0, 0.0)
    tmp_ref[0:16, :] = run
    tmp_ref[16:32, :] = jnp.exp2(last - row) * tail
    col = tmp_ref[...].T
    col_ref[...] = col
    b_rows = b_ref[...].astype(F32).T.astype(BF16)
    for i in range(tiles):
        cut = slice(128 * i, 128 * i + 128)
        weighted = (x_ref[:, cut].astype(F32) * halves(col, i, T, 16)).astype(BF16)
        both = dot(b_rows, weighted)
        kept = jnp.where(lanes_of((64, 128)) < 64, both[0:64], both[64:128])
        state_ref[0:64, cut] = kept.astype(BF16)
        gone = jnp.exp2(halves(col[T - 8 : T], i, 8))[7:8]
        state_ref[64:80, cut] = jnp.broadcast_to(gone, (16, 128)).astype(BF16)


def leaving_state(dt_rows, rate, seg_row, x, b):
    width = x.shape[1]
    return pl.pallas_call(
        state_kernel,
        out_shape=(
            jax.ShapeDtypeStruct((80, width), BF16),
            jax.ShapeDtypeStruct((16, T), F32),
            jax.ShapeDtypeStruct((T, 128), F32),
        ),
        scratch_shapes=[pltpu.VMEM((128, T), F32)],
        compiler_params=VMEM,
        name="leaving_state",
    )(dt_rows, rate, seg_row, x, b)


HALF = T // 2


def mamba_kernel(
    x_ref, z_ref, b_ref, c_ref, row_ref, col_ref, segr_ref, segc_ref, near_ref, far_ref,
    ids1_ref, ids2_ref, skip_ref, out_ref, sq_ref, inner_ref,
):
    tiles = x_ref.shape[1] // 128
    b = b_ref[...]
    c = c_ref[...]
    live = (segc_ref[...] == segr_ref[...]) & (
        lax.broadcasted_iota(jnp.int32, (T, T), 0) >= lanes_of((T, T))
    )
    group = lanes_of((T, 128)) < 64
    for g in range(2):
        own = jnp.where(group == (g == 0), c, jnp.zeros_like(c))
        inner_ref[g] = jnp.where(live, dot(own, b, 1, 1), 0.0)
    last1 = jnp.max(ids1_ref[...].astype(F32))
    last2 = jnp.max(ids2_ref[...].astype(F32))
    passes = jnp.where(last1 == last2, 1.0, 0.0)
    enters = segc_ref[...].astype(F32) + 1.0 == last1
    col = col_ref[...]
    entry = jnp.where(enters, jnp.exp2(col), 0.0)
    low = lanes_of((HALF, 128)) < 64
    totals = [jnp.zeros((HALF, 128), F32) for _ in range(2)]
    for i in range(tiles):
        cut = slice(128 * i, 128 * i + 128)
        carry = (
            near_ref[0:64, cut].astype(F32)
            + near_ref[64:65, cut].astype(F32) * passes * far_ref[0:64, cut].astype(F32)
        ).astype(BF16)
        first = lanes_of((64, 128)) < 64
        nothing = jnp.zeros_like(carry)
        spread_state = jnp.concatenate(
            [jnp.where(first, carry, nothing), jnp.where(first, nothing, carry)], axis=0
        )
        for k in range(2):
            rows = slice(HALF * k, HALF * k + HALF)
            upto = HALF * (k + 1)
            parts = []
            for g in range(2):
                j = 2 * i + g
                power = jnp.minimum(col[rows, j : j + 1] - row_ref[j : j + 1, 0:upto], 126.0)
                mixing = (jnp.exp2(power) * inner_ref[g, rows, 0:upto]).astype(BF16)
                parts.append(dot(mixing, x_ref[0:upto, cut]))
            y = jnp.where(low, parts[0], parts[1])
            y = y + halves(entry[rows], i, HALF) * dot(c[rows], spread_state)
            y = y + skip_ref[:, cut] * x_ref[rows, cut].astype(F32)
            z = z_ref[rows, cut].astype(F32)
            gated = y * (z / (1.0 + jnp.exp(-z)))
            out_ref[rows, cut] = gated
            totals[k] = totals[k] + gated * gated
    for k in range(2):
        turned = totals[k].T
        even = jnp.sum(turned[0:64], axis=0, keepdims=True)
        odd = jnp.sum(turned[64:128], axis=0, keepdims=True)
        sq_ref[:, HALF * k : HALF * k + HALF] = jnp.concatenate([even, odd], axis=0)


def mamba_outputs(x, z, b, c, row, col, seg_row, seg_col, near, far, kv1, kv2, skip):
    width = x.shape[1]
    whole = lambda a: pl.BlockSpec(a.shape, lambda s: (0,) * a.ndim)
    ids = pl.BlockSpec((16, T), lambda s: (kv1.shape[0] // 16 - 1, 0))
    args = [x, z, b, c, row, col, seg_row, seg_col, near, far]
    return pl.pallas_call(
        mamba_kernel,
        grid=(1,),
        out_shape=(jax.ShapeDtypeStruct((T, width), F32), jax.ShapeDtypeStruct((2, T), F32)),
        in_specs=[*map(whole, args), ids, ids, whole(skip)],
        out_specs=(
            pl.BlockSpec((T, width), lambda s: (0, 0)), pl.BlockSpec((2, T), lambda s: (0, 0))
        ),
        scratch_shapes=[pltpu.VMEM((2, T, T), F32)],
        compiler_params=VMEM,
        name="mamba_outputs",
    )(*args, kv1, kv2, skip)


def attention_kernel(
    q_ref, k0_ref, v0_ref, k1_ref, v1_ref, k2_ref, v2_ref, ids1_ref, ids2_ref, segr_ref, segc_ref, out_ref
):
    q = q_ref[...]
    seg = segc_ref[...]
    mine = seg.astype(F32) + 1.0
    scale = LOG2E / math.sqrt(HD)
    causal = (seg == segr_ref[...]) & (
        lax.broadcasted_iota(jnp.int32, (T, T), 0) >= lanes_of((T, T))
    )
    parts = []
    for k_ref, allowed in (
        (k0_ref, causal),
        (k1_ref, mine == ids1_ref[0:1, :].astype(F32)),
        (k2_ref, mine == ids2_ref[0:1, :].astype(F32)),
    ):
        parts.append(jnp.where(allowed, dot(q, k_ref[...], 0, 0) * scale, -jnp.inf))
    top = jnp.max(jnp.maximum(jnp.maximum(parts[0], parts[1]), parts[2]), axis=1, keepdims=True)
    raised = [jnp.exp2(part - top) for part in parts]
    total = jnp.sum(raised[0] + raised[1] + raised[2], axis=1, keepdims=True)
    share = 1.0 / total
    weights = [(part * share).astype(BF16) for part in raised]
    out = dot(v0_ref[...], weights[0], 1, 1)
    out = out + dot(v1_ref[...], weights[1], 1, 1)
    out = out + dot(v2_ref[...], weights[2], 1, 1)
    out_ref[...] = out.astype(BF16)


def attend(q, k, v, kv1, kv2, seg_row, seg_col):
    width = q.shape[0]
    heads = width // HD
    head = pl.BlockSpec((HD, T), lambda h: (h, 0))
    value = pl.BlockSpec((HD, T), lambda h: (heads + h, 0))
    ids = pl.BlockSpec((16, T), lambda h: (kv1.shape[0] // 16 - 1, 0))
    return pl.pallas_call(
        attention_kernel,
        grid=(heads,),
        out_shape=jax.ShapeDtypeStruct((width, T), BF16),
        in_specs=[
            head, head, head, head, value, head, value, ids, ids,
            pl.BlockSpec((1, T), lambda h: (0, 0)), pl.BlockSpec((T, 1), lambda h: (0, 0)),
        ],
        out_specs=head,
        compiler_params=VMEM,
        name="attend",
    )(q, k, v, kv1, kv1, kv2, kv2, kv1, kv2, seg_row, seg_col)


NT = 256


def project_kernel(att_ref, gated_ref, sq_ref, gain_ref, wa_ref, wm_ref, out_ref, att_s, mam_s):
    @pl.when(pl.program_id(0) == 0)
    def _():
        att_s[...] = att_ref[...].astype(F32).T.astype(BF16)
        tiles = gated_ref.shape[1] // 128
        inverse = lax.rsqrt(sq_ref[...] / (tiles * 64 * 8) + EPS)
        spread = jnp.concatenate(
            [jnp.broadcast_to(inverse[0:1], (64, T)), jnp.broadcast_to(inverse[1:2], (64, T))], axis=0
        ).T
        for i in range(tiles):
            cut = slice(128 * i, 128 * i + 128)
            mam_s[:, cut] = (gated_ref[:, cut] * spread * gain_ref[:, cut]).astype(BF16)

    out = dot(att_s[...], wa_ref[...]) + dot(mam_s[...], wm_ref[...])
    out_ref[...] = out.T.astype(BF16)


def project(att, gated, squares, gain, wa, wm):
    total = wa.shape[1]
    same = lambda a: pl.BlockSpec(a.shape, lambda n: (0,) * a.ndim)
    return pl.pallas_call(
        project_kernel,
        grid=(total // NT,),
        out_shape=jax.ShapeDtypeStruct((total, T), BF16),
        in_specs=[
            same(att), same(gated), same(squares), same(gain),
            pl.BlockSpec((wa.shape[0], NT), lambda n: (0, n)),
            pl.BlockSpec((wm.shape[0], NT), lambda n: (0, n)),
        ],
        out_specs=pl.BlockSpec((NT, T), lambda n: (n, 0)),
        scratch_shapes=[pltpu.VMEM((T, att.shape[0]), BF16), pltpu.VMEM(gated.shape, BF16)],
        compiler_params=VMEM,
        name="project",
    )(att, gated, squares, gain, wa, wm)


def mlp_kernel(x_ref, unscale_ref, gu_ref, down_ref, out_ref, rows_s, inv_s, act_s):
    step = pl.program_id(0)
    first = act_s.shape[1] // 128

    @pl.when(step == 0)
    def _():
        width = x_ref.shape[0]
        total = jnp.zeros((T, 128), F32)
        for i in range(width // 128):
            cut = slice(128 * i, 128 * i + 128)
            turned = x_ref[cut, :].astype(F32).T
            rows_s[:, cut] = turned.astype(BF16)
            plain = turned * unscale_ref[:, cut]
            total = total + plain * plain
        inv_s[...] = jnp.broadcast_to(
            lax.rsqrt(jnp.sum(total, axis=1, keepdims=True) / width + EPS), (T, 128)
        )

    @pl.when(step < first)
    def _():
        width = x_ref.shape[0]
        gate_w = gu_ref[:, 0].reshape(width, 128)
        up_w = gu_ref[:, 1].reshape(width, 128)
        both = dot(rows_s[...], jnp.concatenate([gate_w, up_w], axis=1))
        gate = both[:, 0:128] * inv_s[...]
        up = both[:, 128:256] * inv_s[...]
        act_s[:, pl.ds(pl.multiple_of(step * 128, 128), 128)] = (
            gate / (1.0 + jnp.exp(-gate)) * up
        ).astype(BF16)

    @pl.when(step >= first)
    def _():
        w = down_ref[:, 0].reshape(out_ref.shape[0], act_s.shape[1])
        out_ref[...] = dot(w, act_s[...], 1, 1).astype(BF16)


def mlp(x, unscale, weights):
    width = x.shape[0]
    parts, _, rows, hidden = weights.shape
    first = hidden // 128
    blocks = 4
    per = parts // blocks
    return pl.pallas_call(
        mlp_kernel,
        grid=(first + blocks,),
        out_shape=jax.ShapeDtypeStruct((width, T), BF16),
        in_specs=[
            pl.BlockSpec((width, T), lambda s: (0, 0)),
            pl.BlockSpec((1, width), lambda s: (0, 0)),
            pl.BlockSpec((parts, 2, rows, 128), lambda s: (0, 0, 0, jnp.minimum(s, first - 1))),
            pl.BlockSpec((per, 1, rows, hidden), lambda s: (jnp.maximum(s - first, 0), 2, 0, 0)),
        ],
        out_specs=pl.BlockSpec((per * rows, T), lambda s: (jnp.maximum(s - first, 0), 0)),
        scratch_shapes=[
            pltpu.VMEM((T, width), BF16), pltpu.VMEM((T, 128), F32), pltpu.VMEM((T, hidden), BF16)
        ],
        compiler_params=VMEM,
        name="mlp",
    )(x, unscale, weights, weights)


def behind(value, steps):
    count = lax.axis_size(REQ)
    return lax.ppermute(value, REQ, [(i, i + steps) for i in range(count - steps)])


def along(value, steps):
    count = lax.axis_size("x")
    return lax.ppermute(value, "x", [(i, (i + steps) % count) for i in range(count)])


def swap(value):
    return lax.ppermute(value, "c", [(0, 1), (1, 0)])


def scatter_sum(partial):
    count = lax.axis_size("x")
    x, c = lax.axis_index("x"), lax.axis_index("c")
    rows = partial.shape[0] // (2 * count)
    blocks = partial.reshape(count, 2, rows, partial.shape[1])
    mine = lax.dynamic_index_in_dim(blocks, c, 1, keepdims=False)
    other = lax.dynamic_index_in_dim(blocks, 1 - c, 1, keepdims=False)
    paired = mine.astype(F32) + swap(other).astype(F32)
    total = lax.dynamic_index_in_dim(paired, x, 0, keepdims=False)
    narrow = paired.astype(BF16)
    for d in range(1, count):
        out = lax.dynamic_index_in_dim(narrow, (x + d) % count, 0, keepdims=False)
        total = total + along(out, d).astype(F32)
    return total


def gather_rows(share):
    count = lax.axis_size("x")
    x, c = lax.axis_index("x"), lax.axis_index("c")
    rows, cols = share.shape
    got = jnp.zeros((count, rows, cols), share.dtype)
    got = lax.dynamic_update_index_in_dim(got, share, x, 0)
    for d in range(1, count):
        got = lax.dynamic_update_index_in_dim(got, along(share, d), (x - d) % count, 0)
    other = swap(got)
    full = jnp.zeros((count, 2, rows, cols), share.dtype)
    full = lax.dynamic_update_index_in_dim(full, got, c, 1)
    full = lax.dynamic_update_index_in_dim(full, other, 1 - c, 1)
    return full.reshape(2 * count * rows, cols)


def body(
    hidden, query_heads, key_heads, value_heads, segment_ids, page_table, mamba_conv_input,
    mamba_output_gate, state_input_projection, state_output_projection, discrete_step_size,
    head_decay_rate, skip_gain, mamba_gated_norm_gain, attn_proj, mamba_output_projection,
    mlp_norm_gain, gate_proj, up_proj, down_proj, next_norm_gain,
):
    row_count = query_heads.shape[0]
    head_count = query_heads.shape[1] // HD
    width = hidden.shape[1]
    total_width = mlp_norm_gain.shape[0]
    owner = lax.axis_index("x") * lax.axis_size("c") + lax.axis_index("c")

    stacked_weights = jnp.stack([gate_proj, up_proj, down_proj.T])
    weights = lax.all_gather(stacked_weights, REQ, axis=0, tiled=False)

    q, k, v = query_heads.T, key_heads.T, value_heads.T
    ids = jnp.broadcast_to((segment_ids + 1).astype(BF16)[None, :], (16, row_count))
    payload = jnp.concatenate([k, v, ids], axis=0)
    kv1, kv2 = behind(payload, 1), behind(payload, 2)

    seg_row = segment_ids.reshape(1, row_count)
    seg_col = segment_ids.reshape(row_count, 1)
    state, row, col = leaving_state(
        discrete_step_size.T, head_decay_rate.reshape(-1, 1), seg_row, mamba_conv_input,
        state_input_projection,
    )
    near, far = behind(state, 1), behind(state, 2)
    skip = jnp.repeat(skip_gain, mamba_conv_input.shape[1] // skip_gain.shape[0]).reshape(1, -1)
    gated, squares = mamba_outputs(
        mamba_conv_input, mamba_output_gate, state_input_projection, state_output_projection,
        row, col, seg_row, seg_col, near, far, kv1, kv2, skip,
    )
    squares = lax.psum(squares, MLP)
    attended = attend(q, k, v, kv1, kv2, seg_row, seg_col)
    projected = project(
        attended, gated, squares, mamba_gated_norm_gain.reshape(1, -1), attn_proj,
        mamba_output_projection,
    )
    mixed = scatter_sum(projected) + hidden.T.astype(F32)
    own_gain = lax.dynamic_slice_in_dim(mlp_norm_gain, owner * width, width, 0)
    scaled = gather_rows((mixed * own_gain[:, None]).astype(BF16))
    partial = mlp(scaled, (1.0 / mlp_norm_gain).reshape(1, -1), weights)
    new_hidden = (mixed + scatter_sum(partial)).astype(BF16)
    widened = new_hidden.astype(F32)
    total_sq = lax.psum(jnp.sum(widened * widened, axis=0), MLP)
    next_normed = (
        widened * lax.rsqrt(total_sq / total_width + EPS)[None, :] * next_norm_gain[:, None]
    ).astype(BF16)

    page_count = page_table.shape[1]

    def to_pages(source):
        return (
            source.reshape(page_count, PAGE, head_count, HD)
            .transpose(2, 0, 1, 3)
            .reshape(head_count, page_count, PAGE * HD)
        )

    stacked = jnp.stack([to_pages(key_heads), to_pages(value_heads)])
    kv_cache = jnp.zeros_like(stacked).at[:, :, page_table[0]].set(stacked)
    return (new_hidden.T, next_normed.T, kv_cache)


def solution(mesh):
    split = Mesh(mesh.devices.reshape(4, 4, 4, 2), ("z", "y", "x", "c"))
    tokens = P(REQ, MLP)
    return jax.shard_map(
        body,
        mesh=split,
        in_specs=(
            tokens, tokens, tokens, tokens, P(REQ), P(REQ, None), tokens, tokens, P(REQ, None),
            P(REQ, None), tokens, P(MLP), P(MLP), P(MLP), P(MLP, None), P(MLP, None), P(), tokens,
            tokens, P(MLP, REQ), P(MLP),
        ),
        out_specs=(tokens, tokens, P(None, MLP, REQ, None)),
        check_vma=False,
    )
```

time: 626 us -> 276 us (0.44); the launches traced: 615 us -> 275 us
  waiting for transfers between devices: 309 us -> 109 us
  matrix products: 75 us -> 0 us
  Pallas kernels: 0 us -> 53.6 us
  other arithmetic: 61.4 us -> 17.8 us
  blocking collectives: 71.4 us -> 28.5 us
  local copies, waits for them, and re-layouts: 55 us -> 28.2 us
  loops' own time: 11.1 us -> 0 us
  starting transfers between devices: 16.2 us -> 23.3 us
    all_gather x4 -> x1, waiting for transfers between devices: 179 us -> 0.01 us  [body(): weights = lax.all_gather(stacked_weights, REQ, axis=0, tiled=False)]
    ppermute x6 -> x16, waiting for transfers between devices: 0.02 us -> 109 us  [the longest x9 56.2 us: along(): lax.ppermute(value, 'x', [(i, (i + steps) % count) for i in range(count)])]
    psum x1 -> x0, waiting for transfers between devices: 89.8 us -> none  [body(): lax.psum(lax.dynamic_update_slice_in_dim(projected, own_part, offset, 1),...]
    pallas_call x0 -> x5, Pallas kernels: none -> 53.6 us  [the longest x1 20.6 us: mlp(): pl.pallas_call(mlp_kernel, grid=(first + blocks,), out_shape=jax.ShapeDty...]
    dot_general x8 -> x0, matrix products: 53.1 us -> none  [the longest x1 20.4 us: block_contributions(): jnp.einsum('htu,uhp->thp', mixing * inner[group_index], driven, precision...]
    all_gather x1 -> x0, blocking collectives: 44.6 us -> none  [entering(): everything = jax.tree.map(lambda part: lax.all_gather(part, axis), x)]
    unnamed x7 -> x1, waiting for transfers between devices: 40 us -> 0.02 us
    select_n x18 -> x0, other arithmetic: 33.2 us -> none  [the longest x16 32.6 us: step(): return jax.tree.map(lambda a, b: jnp.where(reached, a, b), new, before)]
  transfers between devices with their start and end apart: 12 -> 17, of which waited for: 5 -> 11; matrix products, arithmetic and copies ran while one was open for 10% -> 10% of each run, Pallas kernels for 0% -> 12%
where the time goes in v1:
time: 276 us; the launch traced here: 275 us
  waiting for transfers between devices  109 us (39%)
  Pallas kernels  53.6 us (19%)
  blocking collectives  28.5 us (10%)
  local copies, waits for them, and re-layouts  28.2 us (10%)
  starting transfers between devices  23.3 us (8%)
  other arithmetic  17.8 us (6%)
  between operations  14.4 us (5%)
    ppermute x9, waiting for transfers between devices, along(): lax.ppermute(value, 'x', [(i, (i + steps) % count) for i in range(count)])  56.2 us
    ppermute x4, waiting for transfers between devices, behind(): lax.ppermute(value, REQ, [(i, i + steps) for i in range(count - steps)])  48.1 us
    pallas_call x1, Pallas kernels, mlp(): pl.pallas_call(mlp_kernel, grid=(first + blocks,), out_shape=jax.ShapeDty...  20.6 us
    pallas_call x1, Pallas kernels, project(): pl.pallas_call(project_kernel, grid=(total // NT,), out_shape=jax.ShapeDt...  15.9 us
    psum x1, blocking collectives, body(): total_sq = lax.psum(jnp.sum(widened * widened, axis=0), MLP)  14.6 us
    psum x1, blocking collectives, body(): squares = lax.psum(squares, MLP)  14 us
    ppermute x4, starting transfers between devices, behind(): lax.ppermute(value, REQ, [(i, i + steps) for i in range(count - steps)])  12.1 us
    ppermute x9, starting transfers between devices, along(): lax.ppermute(value, 'x', [(i, (i + steps) % count) for i in range(count)])  10.6 us
  transfers between devices with their start and end apart: 17, of which 11 were waited for; matrix products, arithmetic and copies ran while one was open for 10% of the time, Pallas kernels for 12%

profile of v1, /device:TPU:96, one launch (start us, length us, event | category | flops | bytes accessed | tf_op | source)
XLA Modules:
  0.0 275.0 jit_solution(16797473561047615088)
XLA Ops:
  7.2 2.5 pad_maximum_fusion
  9.9 1.0 pad_maximum_fusion.1
  10.9 3.5 %collective-permute-start = (bf16[912,512]{1,0:T(8,128)(2,1)}, bf16[912,512]{1,0:T(8,128)(2,1)S(1)}, u32[]{:S(2)}, u32[]{:S(2)}) collective-permute-start(bf16[912,512]{1,0:T(8,128)(2,1)} %pad_maximum_fusion.1), channel_id=1, source_target_pairs={{0,8},{8,16},{16,24},{24,32},{32,40},{40,48},{48,56},{56,64},{64,7... | collective-permute-start | bytes 2801672 | tf_op jit(solution)/shard_map/ppermute | solution.py:313
  14.3 4.8 %collective-permute-start.1 = (bf16[912,512]{1,0:T(8,128)(2,1)}, bf16[912,512]{1,0:T(8,128)(2,1)S(1)}, u32[]{:S(2)}, u32[]{:S(2)}) collective-permute-start(bf16[912,512]{1,0:T(8,128)(2,1)} %pad_maximum_fusion.1), channel_id=1, source_target_pairs={{0,16},{8,24},{16,32},{24,40},{32,48},{40,56},{48,64},{56,72},{64,... | collective-permute-start | bytes 2801672 | tf_op jit(solution)/shard_map/ppermute | solution.py:313
  19.2 0.7 copy.47.rate_ref
  19.9 4.2 %leaving_state.1 = (bf16[80,896]{1,0:T(8,128)(2,1)}, f32[16,512]{1,0:T(8,128)}, f32[512,128]{1,0:T(8,128)}) custom-call(f32[14,512]{1,0:T(8,128)} %bitcast.123, f32[14,1]{1,0:T(8,128)} %copy.47.rate_ref, s32[1,512]{1,0:T(1,128)} %bitcast.119, bf16[512,896]{1,0:T(8,128)(2,1)} %x_ref.3, bf16[512,128]{1,0:T(8,128)(2,1)} %b_ref.3), custom_call_target="tpu_custom_call" | custom-call | tf_op jit(solution)/shard_map/leaving_state/pallas_call | solution.py:72
  24.0 1.9 collective-permute-start.2
  25.9 1.9 collective-permute-start.3
  27.9 0.9 copy.46.segc_ref
  30.1 22.9 %collective-permute-done.k1_ref.v1_ref.ids1_ref = bf16[912,512]{1,0:T(8,128)(2,1)S(1)} collective-permute-done((bf16[912,512]{1,0:T(8,128)(2,1)}, bf16[912,512]{1,0:T(8,128)(2,1)S(1)}, u32[]{:S(2)}, u32[]{:S(2)}) %collective-permute-start) | collective-permute-done | bytes 933920 | tf_op jit(solution)/shard_map/ppermute | solution.py:313
  52.9 25.3 %collective-permute-done.1.k2_ref.v2_ref.ids2_ref = bf16[912,512]{1,0:T(8,128)(2,1)S(1)} collective-permute-done((bf16[912,512]{1,0:T(8,128)(2,1)}, bf16[912,512]{1,0:T(8,128)(2,1)S(1)}, u32[]{:S(2)}, u32[]{:S(2)}) %collective-permute-start.1) | collective-permute-done | bytes 933920 | tf_op jit(solution)/shard_map/ppermute | solution.py:313
  78.2 1.0 copy-done.1
  79.2 5.9 %attend.1.att_ref = bf16[448,512]{1,0:T(8,128)(2,1)} custom-call(bf16[448,512]{1,0:T(8,128)(2,1)} %bitcast.115, bf16[448,512]{1,0:T(8,128)(2,1)} %bitcast.108, bf16[448,512]{1,0:T(8,128)(2,1)} %bitcast.110, bf16[912,512]{1,0:T(8,128)(2,1)} %copy-done, bf16[912,512]{1,0:T(8,128)(2,1)} %copy-done, bf16[912,512]{1,0:T(8,128)(2,1)} %copy-done.1, ...), custom_call_target="tpu_custom_call" | custom-call | tf_op jit(solution)/shard_map/attend/pallas_call | solution.py:197
  85.8 7.0 %mamba_outputs.1 = (f32[512,896]{1,0:T(8,128)}, f32[2,512]{1,0:T(2,128)}) custom-call(bf16[512,896]{1,0:T(8,128)(2,1)} %x_ref.3, bf16[512,896]{1,0:T(8,128)(2,1)} %z_ref.1, bf16[512,128]{1,0:T(8,128)(2,1)} %b_ref.3, bf16[512,128]{1,0:T(8,128)(2,1)} %c_ref.1, f32[16,512]{1,0:T(8,128)} %get-tuple-element.8.row_ref, f32[512,128]{1,0:T(8,128)} %get-tuple-element.9.col_ref, ...), custom_call_target="tpu_custom_call" | custom-call | tf_op jit(solution)/shard_map/mamba_outputs/pallas_call | solution.py:149
  92.8 14.0 %psum.14.sq_ref = f32[2,512]{1,0:T(2,128)} all-reduce(f32[2,512]{1,0:T(2,128)} %get-tuple-element.12), channel_id=1, replica_groups=mesh['z'=4,'y'=4,'x'=4,'c'=2] {'x','c'}, use_global_device_ids=true, to_apply=%region_0.0 | all-reduce | flops 1024 | bytes 8192 | tf_op jit(solution)/shard_map/psum | solution.py:388
  106.8 15.9 %project.1 = bf16[3584,512]{1,0:T(8,128)(2,1)} custom-call(bf16[448,512]{1,0:T(8,128)(2,1)} %attend.1.att_ref, f32[512,896]{1,0:T(8,128)} %get-tuple-element.11.gated_ref, f32[2,512]{1,0:T(2,128)} %psum.14.sq_ref, f32[1,896]{1,0:T(1,128)} %reshape.75.gain_ref, bf16[448,3584]{1,0:T(8,128)(2,1)} %wa_ref.1, bf16[896,3584]{1,0:T(8,128)(2,1)} %wm_ref.1), custom_call_target="tpu_custom_call" | custom-call | tf_op jit(solution)/shard_map/project/pallas_call | solution.py:234
  122.7 2.9 %dynamic-slice_bitcast_fusion.1 = bf16[4,448,512]{2,1,0:T(8,128)(2,1)} fusion(bf16[4,2,448,512]{3,2,1,0:T(8,128)(2,1)} %bitcast.106, s32[]{:T(128)S(6)} %select_n.88), kind=kLoop, calls=%fused_computation.6 | loop fusion | bytes 3670020 | tf_op jit(solution)/shard_map/jit(dynamic_index_in_dim)/squeeze | solution.py:331
  125.6 4.0 %collective-permute-done.4 = bf16[4,448,512]{2,1,0:T(8,128)(2,1)S(1)} collective-permute-done((bf16[4,448,512]{2,1,0:T(8,128)(2,1)}, bf16[4,448,512]{2,1,0:T(8,128)(2,1)S(1)}, u32[]{:S(2)}, u32[]{:S(2)}) %collective-permute-start.4) | collective-permute-done | bytes 1835040 | tf_op jit(solution)/shard_map/ppermute | solution.py:322
  129.6 4.1 %fusion.13 = (bf16[4,448,512]{2,1,0:T(8,128)(2,1)S(1)}, f32[4,448,512]{2,1,0:T(8,128)}) fusion(bf16[4,448,512]{2,1,0:T(8,128)(2,1)S(1)} %collective-permute-done.4, bf16[4,2,448,512]{3,2,1,0:T(8,128)(2,1)} %bitcast.107, s32[]{:T(128)S(6)} %select_n.87), kind=kLoop, calls=%fused_computation.42 | loop fusion | flops 3670016 | bytes 9175044 | tf_op jit(solution)/shard_map/convert_element_type | solution.py:334
  133.8 1.6 collective-permute-start.6
  135.4 1.6 collective-permute-start.7
  137.1 20.3 %collective-permute-done.5 = bf16[448,512]{1,0:T(8,128)(2,1)S(1)} collective-permute-done((bf16[448,512]{1,0:T(8,128)(2,1)S(1)}, bf16[448,512]{1,0:T(8,128)(2,1)S(1)}, u32[]{:S(2)}, u32[]{:S(2)}) %collective-permute-start.5) | collective-permute-done | bytes 458784 | tf_op jit(solution)/shard_map/ppermute | solution.py:318
  158.0 0.8 copy-done.9
  158.9 0.9 copy-done.10
  159.8 2.2 bitcast_dynamic-update-slice_fusion.5
  162.3 3.6 %collective-permute-start.9 = (bf16[448,512]{1,0:T(8,128)(2,1)}, bf16[448,512]{1,0:T(8,128)(2,1)S(1)}, u32[]{:S(2)}, u32[]{:S(2)}) collective-permute-start(bf16[448,512]{1,0:T(8,128)(2,1)} %get-tuple-element.30), channel_id=1, source_target_pairs={{0,4},{2,6},{4,0},{6,2},{1,5},{3,7},{5,1},{7,3},{8,12},{10,14},{12... | collective-permute-start | bytes 1376264 | tf_op jit(solution)/shard_map/ppermute | solution.py:318
  165.9 9.3 %collective-permute-done.8 = bf16[448,512]{1,0:T(8,128)(2,1)} collective-permute-done((bf16[448,512]{1,0:T(8,128)(2,1)}, bf16[448,512]{1,0:T(8,128)(2,1)}, u32[]{:S(2)}, u32[]{:S(2)}) %collective-permute-start.8) | collective-permute-done | bytes 458784 | tf_op jit(solution)/shard_map/ppermute | solution.py:318
  175.2 1.0 bitcast_dynamic-update-slice_fusion.4
  176.3 9.9 %collective-permute-done.9 = bf16[448,512]{1,0:T(8,128)(2,1)S(1)} collective-permute-done((bf16[448,512]{1,0:T(8,128)(2,1)}, bf16[448,512]{1,0:T(8,128)(2,1)S(1)}, u32[]{:S(2)}, u32[]{:S(2)}) %collective-permute-start.9) | collective-permute-done | bytes 458784 | tf_op jit(solution)/shard_map/ppermute | solution.py:318
  186.9 2.2 broadcast_in_dim.44
  189.2 1.4 bitcast_dynamic-update-slice_fusion
  190.6 1.4 bitcast_dynamic-update-slice_fusion.1
  191.9 20.6 %mlp.1 = bf16[3584,512]{1,0:T(8,128)(2,1)} custom-call(bf16[3584,512]{1,0:T(8,128)(2,1)} %bitcast.22.x_ref, f32[1,3584]{1,0:T(1,128)} %reshape.78.unscale_ref, bf16[16,3,224,896]{3,2,1,0:T(8,128)(2,1)} %bitcast.102, bf16[16,3,224,896]{3,2,1,0:T(8,128)(2,1)} %bitcast.103), custom_call_target="tpu_custom_call" | custom-call | tf_op jit(solution)/shard_map/mlp/pallas_call | solution.py:292
  212.6 3.0 %dynamic-slice_bitcast_fusion = bf16[4,448,512]{2,1,0:T(8,128)(2,1)} fusion(bf16[4,2,448,512]{3,2,1,0:T(8,128)(2,1)} %bitcast.104, s32[]{:T(128)S(6)} %select_n.88), kind=kLoop, calls=%fused_computation.5 | loop fusion | bytes 3670020 | tf_op jit(solution)/shard_map/jit(dynamic_index_in_dim)/squeeze | solution.py:331
  216.9 0.9 stack_reshape.6
  218.1 0.9 stack_reshape.7
  219.0 0.8 collective-permute-done.12
  219.8 4.6 %fusion.12 = (bf16[4,448,512]{2,1,0:T(8,128)(2,1)S(1)}, f32[4,448,512]{2,1,0:T(8,128)}) fusion(bf16[4,448,512]{2,1,0:T(8,128)(2,1)} %collective-permute-done.12, bf16[4,2,448,512]{3,2,1,0:T(8,128)(2,1)} %bitcast.105, s32[]{:T(128)S(6)} %select_n.87), kind=kLoop, calls=%fused_computation.41 | loop fusion | flops 3670016 | bytes 9175044 | tf_op jit(solution)/shard_map/convert_element_type | solution.py:334
  224.3 1.1 dynamic-slice_bitcast_fusion.4
  225.7 3.3 %collective-permute-start.14 = (bf16[448,512]{1,0:T(8,128)(2,1)}, bf16[448,512]{1,0:T(8,128)(2,1)}, u32[]{:S(2)}, u32[]{:S(2)}) collective-permute-start(bf16[448,512]{1,0:T(8,128)(2,1)} %get-tuple-element.35), channel_id=1, source_target_pairs={{0,4},{2,6},{4,0},{6,2},{1,5},{3,7},{5,1},{7,3},{8,12},{10,14},{12... | collective-permute-start | bytes 1376264 | tf_op jit(solution)/shard_map/ppermute | solution.py:318
  229.1 0.9 copy.54
  230.6 2.6 scatter_fusion
  233.1 1.0 copy.55
  234.1 6.0 %collective-permute-done.13 = bf16[448,512]{1,0:T(8,128)(2,1)} collective-permute-done((bf16[448,512]{1,0:T(8,128)(2,1)}, bf16[448,512]{1,0:T(8,128)(2,1)}, u32[]{:S(2)}, u32[]{:S(2)}) %collective-permute-start.13) | collective-permute-done | bytes 458784 | tf_op jit(solution)/shard_map/ppermute | solution.py:318
  240.1 9.7 %collective-permute-done.14 = bf16[448,512]{1,0:T(8,128)(2,1)} collective-permute-done((bf16[448,512]{1,0:T(8,128)(2,1)}, bf16[448,512]{1,0:T(8,128)(2,1)}, u32[]{:S(2)}, u32[]{:S(2)}) %collective-permute-start.14) | collective-permute-done | bytes 458784 | tf_op jit(solution)/shard_map/ppermute | solution.py:318
  250.3 2.4 fusion
  252.7 14.6 %psum.15 = f32[512]{0:T(512)S(1)} all-reduce(f32[512]{0:T(512)S(1)} %get-tuple-element.25), channel_id=1, replica_groups=mesh['z'=4,'y'=4,'x'=4,'c'=2] {'x','c'}, use_global_device_ids=true, to_apply=%region_2.3 | all-reduce | flops 512 | bytes 4096 | tf_op jit(solution)/shard_map/psum | solution.py:400
  267.3 0.9 fusion.9
  (83 shorter events, 7.1 us)
Async XLA Ops:
  7.2 2.6 copy-start.15
  7.2 2.7 copy-start.2
  7.2 2.7 copy-start.4
  7.2 184.7 %all-gather.3.cloned.1.call-start = ((), (), s32[]{:S(2)}) async-start(), calls=%async_computation | async-start | bytes 20471808 | tf_op jit(solution)/shard_map/all_gather | solution.py:369
  9.8 9.4 %copy-start.20 = (f32[14]{0:T(128)S(1)}, f32[14]{0:T(128)}, u32[]{:S(2)}) copy-start(f32[14]{0:T(128)} %param.32) | copy-start | bytes 172
  9.8 18.1 %copy-start.16 = (s32[512]{0:T(512)S(1)}, s32[512]{0:T(512)}, u32[]{:S(2)}) copy-start(s32[512]{0:T(512)} %param.25) | copy-start | bytes 6148
  9.8 18.9 %copy-start.21 = (f32[14]{0:T(128)S(1)}, f32[14]{0:T(128)}, u32[]{:S(2)}) copy-start(f32[14]{0:T(128)} %param.33) | copy-start | bytes 172
  9.8 19.7 %copy-start.18 = (f32[896]{0:T(1024)S(1)}, f32[896]{0:T(1024)}, u32[]{:S(2)}) copy-start(f32[896]{0:T(1024)} %param.34) | copy-start | bytes 10756
  10.9 42.1 %collective-permute-start = (bf16[912,512]{1,0:T(8,128)(2,1)}, bf16[912,512]{1,0:T(8,128)(2,1)S(1)}, u32[]{:S(2)}, u32[]{:S(2)}) collective-permute-start(bf16[912,512]{1,0:T(8,128)(2,1)} %pad_maximum_fusion.1), channel_id=1, source_target_pairs={{0,8},{8,16},{16,24},{24,32},{32,40},{40,48},{48,56},{56,64},{64,7... | collective-permute-start | bytes 2801672 | tf_op jit(solution)/shard_map/ppermute | solution.py:313
  14.3 63.9 %collective-permute-start.1 = (bf16[912,512]{1,0:T(8,128)(2,1)}, bf16[912,512]{1,0:T(8,128)(2,1)S(1)}, u32[]{:S(2)}, u32[]{:S(2)}) collective-permute-start(bf16[912,512]{1,0:T(8,128)(2,1)} %pad_maximum_fusion.1), channel_id=1, source_target_pairs={{0,16},{8,24},{16,32},{24,40},{32,48},{40,56},{48,64},{56,72},{64,... | collective-permute-start | bytes 2801672 | tf_op jit(solution)/shard_map/ppermute | solution.py:313
  24.0 61.0 %collective-permute-start.2 = (bf16[80,896]{1,0:T(8,128)(2,1)}, bf16[80,896]{1,0:T(8,128)(2,1)S(1)}, u32[]{:S(2)}, u32[]{:S(2)}) collective-permute-start(bf16[80,896]{1,0:T(8,128)(2,1)} %get-tuple-element.10), channel_id=1, source_target_pairs={{0,8},{8,16},{16,24},{24,32},{32,40},{40,48},{48,56},{56,64},{64,7... | collective-permute-start | bytes 430088 | tf_op jit(solution)/shard_map/ppermute | solution.py:313
  25.9 59.1 %collective-permute-start.3 = (bf16[80,896]{1,0:T(8,128)(2,1)}, bf16[80,896]{1,0:T(8,128)(2,1)S(1)}, u32[]{:S(2)}, u32[]{:S(2)}) collective-permute-start(bf16[80,896]{1,0:T(8,128)(2,1)} %get-tuple-element.10), channel_id=1, source_target_pairs={{0,16},{8,24},{16,32},{24,40},{32,48},{40,56},{48,64},{56,72},{64,... | collective-permute-start | bytes 430088 | tf_op jit(solution)/shard_map/ppermute | solution.py:313
  52.9 25.3 %copy-start = (bf16[912,512]{1,0:T(8,128)(2,1)}, bf16[912,512]{1,0:T(8,128)(2,1)S(1)}, u32[]{:S(2)}) copy-start(bf16[912,512]{1,0:T(8,128)(2,1)S(1)} %collective-permute-done.k1_ref.v1_ref.ids1_ref) | copy-start | bytes 2801668
  78.2 1.0 copy-start.1
  85.0 0.7 copy-start.13
  85.1 0.7 copy-start.14
  125.6 4.0 %collective-permute-start.4 = (bf16[4,448,512]{2,1,0:T(8,128)(2,1)}, bf16[4,448,512]{2,1,0:T(8,128)(2,1)S(1)}, u32[]{:S(2)}, u32[]{:S(2)}) collective-permute-start(bf16[4,448,512]{2,1,0:T(8,128)(2,1)} %dynamic-slice_bitcast_fusion.1), channel_id=1, source_target_pairs={{0,1},{1,0},{2,3},{3,2},{4,5},{5,4},{6,7},{7,6},{8,9},{9,8},{10,11... | collective-permute-start | bytes 5505032 | tf_op jit(solution)/shard_map/ppermute | solution.py:322
  133.7 3.4 %copy-start.17 = (f32[3584]{0:T(1024)S(1)}, f32[3584]{0:T(1024)}, u32[]{:S(2)}) copy-start(f32[3584]{0:T(1024)} %param.37) | copy-start | bytes 43012
  133.7 25.3 %copy-start.6 = (bf16[512,448]{0,1:T(8,128)(2,1)S(1)}, bf16[512,448]{0,1:T(8,128)(2,1)}, u32[]{:S(2)}) copy-start(bf16[512,448]{0,1:T(8,128)(2,1)} %param.21) | copy-start | bytes 1376260
  133.8 23.6 %collective-permute-start.5 = (bf16[448,512]{1,0:T(8,128)(2,1)S(1)}, bf16[448,512]{1,0:T(8,128)(2,1)S(1)}, u32[]{:S(2)}, u32[]{:S(2)}) collective-permute-start(bf16[448,512]{1,0:T(8,128)(2,1)S(1)} %get-tuple-element.36), channel_id=1, source_target_pairs={{0,2},{2,4},{4,6},{6,0},{1,3},{3,5},{5,7},{7,1},{8,10},{10,12},{12... | collective-permute-start | bytes 1376264 | tf_op jit(solution)/shard_map/ppermute | solution.py:318
  133.8 23.6 %collective-permute-start.6 = (bf16[448,512]{1,0:T(8,128)(2,1)S(1)}, bf16[448,512]{1,0:T(8,128)(2,1)S(1)}, u32[]{:S(2)}, u32[]{:S(2)}) collective-permute-start(bf16[448,512]{1,0:T(8,128)(2,1)S(1)} %get-tuple-element.38), channel_id=1, source_target_pairs={{0,4},{2,6},{4,0},{6,2},{1,5},{3,7},{5,1},{7,3},{8,12},{10,14},{12... | collective-permute-start | bytes 1376264 | tf_op jit(solution)/shard_map/ppermute | solution.py:318
  135.4 22.6 %collective-permute-start.7 = (bf16[448,512]{1,0:T(8,128)(2,1)S(1)}, bf16[448,512]{1,0:T(8,128)(2,1)S(1)}, u32[]{:S(2)}, u32[]{:S(2)}) collective-permute-start(bf16[448,512]{1,0:T(8,128)(2,1)S(1)} %get-tuple-element.37), channel_id=1, source_target_pairs={{0,6},{2,0},{4,2},{6,4},{1,7},{3,1},{5,3},{7,5},{8,14},{10,8},{12,... | collective-permute-start | bytes 1376264 | tf_op jit(solution)/shard_map/ppermute | solution.py:318
  157.4 4.7 %copy-start.7 = (bf16[448,512]{1,0:T(8,128)(2,1)}, bf16[448,512]{1,0:T(8,128)(2,1)S(1)}, u32[]{:S(2)}) copy-start(bf16[448,512]{1,0:T(8,128)(2,1)S(1)} %collective-permute-done.6) | copy-start | bytes 1376260
  158.0 0.8 copy-start.9
  158.8 1.0 copy-start.10
  162.1 13.2 %collective-permute-start.8 = (bf16[448,512]{1,0:T(8,128)(2,1)}, bf16[448,512]{1,0:T(8,128)(2,1)}, u32[]{:S(2)}, u32[]{:S(2)}) collective-permute-start(bf16[448,512]{1,0:T(8,128)(2,1)} %get-tuple-element.30), channel_id=1, source_target_pairs={{0,2},{2,4},{4,6},{6,0},{1,3},{3,5},{5,7},{7,1},{8,10},{10,12},{12... | collective-permute-start | bytes 1376264 | tf_op jit(solution)/shard_map/ppermute | solution.py:318
  162.3 23.8 %collective-permute-start.9 = (bf16[448,512]{1,0:T(8,128)(2,1)}, bf16[448,512]{1,0:T(8,128)(2,1)S(1)}, u32[]{:S(2)}, u32[]{:S(2)}) collective-permute-start(bf16[448,512]{1,0:T(8,128)(2,1)} %get-tuple-element.30), channel_id=1, source_target_pairs={{0,4},{2,6},{4,0},{6,2},{1,5},{3,7},{5,1},{7,3},{8,12},{10,14},{12... | collective-permute-start | bytes 1376264 | tf_op jit(solution)/shard_map/ppermute | solution.py:318
  165.9 20.3 %collective-permute-start.10 = (bf16[448,512]{1,0:T(8,128)(2,1)}, bf16[448,512]{1,0:T(8,128)(2,1)S(1)}, u32[]{:S(2)}, u32[]{:S(2)}) collective-permute-start(bf16[448,512]{1,0:T(8,128)(2,1)} %get-tuple-element.30), channel_id=1, source_target_pairs={{0,6},{2,0},{4,2},{6,4},{1,7},{3,1},{5,3},{7,5},{8,14},{10,8},{12,... | collective-permute-start | bytes 1376264 | tf_op jit(solution)/shard_map/ppermute | solution.py:318
  186.2 4.3 %collective-permute-start.11 = (bf16[4,448,512]{2,1,0:T(8,128)(2,1)S(1)}, bf16[4,448,512]{2,1,0:T(8,128)(2,1)S(1)}, u32[]{:S(2)}, u32[]{:S(2)}) collective-permute-start(bf16[4,448,512]{2,1,0:T(8,128)(2,1)S(1)} %bitcast_dynamic-update-slice_fusion.2), channel_id=1, source_target_pairs={{0,1},{1,0},{2,3},{3,2},{4,5},{5,4},{6,7},{7,6},{8,9},{9,8},{10,11... | collective-permute-start | bytes 5505032 | tf_op jit(solution)/shard_map/ppermute | solution.py:322
  212.6 3.5 %copy-start.3 = (bf16[512,448]{0,1:T(8,128)(2,1)S(1)}, bf16[512,448]{0,1:T(8,128)(2,1)}, u32[]{:S(2)}) copy-start(bf16[512,448]{0,1:T(8,128)(2,1)} %param.23) | copy-start | bytes 1376260
  212.6 3.7 %copy-start.5 = (bf16[512,448]{0,1:T(8,128)(2,1)S(1)}, bf16[512,448]{0,1:T(8,128)(2,1)}, u32[]{:S(2)}) copy-start(bf16[512,448]{0,1:T(8,128)(2,1)} %param.24) | copy-start | bytes 1376260
  215.5 4.2 %collective-permute-start.12 = (bf16[4,448,512]{2,1,0:T(8,128)(2,1)}, bf16[4,448,512]{2,1,0:T(8,128)(2,1)}, u32[]{:S(2)}, u32[]{:S(2)}) collective-permute-start(bf16[4,448,512]{2,1,0:T(8,128)(2,1)} %dynamic-slice_bitcast_fusion), channel_id=1, source_target_pairs={{0,1},{1,0},{2,3},{3,2},{4,5},{5,4},{6,7},{7,6},{8,9},{9,8},{10,11... | collective-permute-start | bytes 5505032 | tf_op jit(solution)/shard_map/ppermute | solution.py:322
  225.5 14.6 %collective-permute-start.13 = (bf16[448,512]{1,0:T(8,128)(2,1)}, bf16[448,512]{1,0:T(8,128)(2,1)}, u32[]{:S(2)}, u32[]{:S(2)}) collective-permute-start(bf16[448,512]{1,0:T(8,128)(2,1)} %get-tuple-element.33), channel_id=1, source_target_pairs={{0,2},{2,4},{4,6},{6,0},{1,3},{3,5},{5,7},{7,1},{8,10},{10,12},{12... | collective-permute-start | bytes 1376264 | tf_op jit(solution)/shard_map/ppermute | solution.py:318
  225.7 24.2 %collective-permute-start.14 = (bf16[448,512]{1,0:T(8,128)(2,1)}, bf16[448,512]{1,0:T(8,128)(2,1)}, u32[]{:S(2)}, u32[]{:S(2)}) collective-permute-start(bf16[448,512]{1,0:T(8,128)(2,1)} %get-tuple-element.35), channel_id=1, source_target_pairs={{0,4},{2,6},{4,0},{6,2},{1,5},{3,7},{5,1},{7,3},{8,12},{10,14},{12... | collective-permute-start | bytes 1376264 | tf_op jit(solution)/shard_map/ppermute | solution.py:318
  229.0 1.1 copy-start.22
  229.0 21.3 %collective-permute-start.15 = (bf16[448,512]{1,0:T(8,128)(2,1)}, bf16[448,512]{1,0:T(8,128)(2,1)}, u32[]{:S(2)}, u32[]{:S(2)}) collective-permute-start(bf16[448,512]{1,0:T(8,128)(2,1)} %get-tuple-element.34), channel_id=1, source_target_pairs={{0,6},{2,0},{4,2},{6,4},{1,7},{3,1},{5,3},{7,5},{8,14},{10,8},{12,... | collective-permute-start | bytes 1376264 | tf_op jit(solution)/shard_map/ppermute | solution.py:318
  230.5 19.7 %copy-start.8 = (bf16[448,512]{1,0:T(8,128)(2,1)S(1)}, bf16[448,512]{1,0:T(8,128)(2,1)}, u32[]{:S(2)}) copy-start(bf16[448,512]{1,0:T(8,128)(2,1)} %copy-done.7) | copy-start | bytes 1376260
  233.1 17.1 %copy-start.11 = (bf16[448,512]{1,0:T(8,128)(2,1)S(1)}, bf16[448,512]{1,0:T(8,128)(2,1)}, u32[]{:S(2)}) copy-start(bf16[448,512]{1,0:T(8,128)(2,1)} %copy-done.9) | copy-start | bytes 1376260
  250.3 17.0 %copy-start.19 = (f32[448]{0:T(512)S(1)}, f32[448]{0:T(512)}, u32[]{:S(2)}) copy-start(f32[448]{0:T(512)} %param.41) | copy-start | bytes 5380
  252.7 15.5 %copy-start.12 = (bf16[448,512]{1,0:T(8,128)(2,1)}, bf16[448,512]{1,0:T(8,128)(2,1)S(1)}, u32[]{:S(2)}) copy-start(bf16[448,512]{1,0:T(8,128)(2,1)S(1)} %get-tuple-element.26) | copy-start | bytes 1376260
Sparse Core Ops, SparseCore 0:
  10.2 161.5 all-gather.2

commit v2 on v1

v2 whole, which is shorter than its diff:
```python
import math

import jax
import jax.numpy as jnp
from jax import lax
from jax.experimental import pallas as pl
from jax.experimental.pallas import tpu as pltpu
from jax.sharding import Mesh
from jax.sharding import PartitionSpec as P

HD = 224
PAGE = 16
EPS = 1e-05
LOG2E = math.log2(math.e)
T = 512
F32 = jnp.float32
BF16 = jnp.bfloat16
REQ = ("z", "y")
MLP = ("x", "c")


def vmem(mib):
    return pltpu.CompilerParams(vmem_limit_bytes=mib << 20)


def in_hbm(value):
    return pltpu.with_memory_space_constraint(value, pltpu.HBM)


def dot(a, b, ca=1, cb=0):
    return lax.dot_general(a, b, (((ca,), (cb,)), ((), ())), preferred_element_type=F32)


def lanes_of(shape):
    return lax.broadcasted_iota(jnp.int32, shape, 1)


def halves(pair, i, rows, base=0):
    low = jnp.broadcast_to(pair[:, base + 2 * i : base + 2 * i + 1], (rows, 128))
    high = jnp.broadcast_to(pair[:, base + 2 * i + 1 : base + 2 * i + 2], (rows, 128))
    return jnp.where(lanes_of((rows, 128)) < 64, low, high)


def state_kernel(dt_ref, rate_ref, seg_ref, x_ref, b_ref, state_ref, row_ref, col_ref, tmp_ref):
    heads = dt_ref.shape[0]
    tiles = x_ref.shape[1] // 128
    tmp_ref[...] = jnp.zeros_like(tmp_ref)
    tmp_ref[0:heads, :] = dt_ref[...] * (rate_ref[...] * -LOG2E)
    tmp_ref[16:32, :] = jnp.ones((16, T), F32)
    tmp_ref[16 : 16 + heads, :] = dt_ref[...]
    run = tmp_ref[0:16, :]
    lane = lanes_of((16, T))
    shift = 1
    while shift < T:
        run = run + jnp.where(lane >= shift, pltpu.roll(run, shift, 1), 0.0)
        shift *= 2
    row = run - jnp.log2(tmp_ref[16:32, :])
    row_ref[...] = row
    last = jnp.sum(jnp.where(lane == T - 1, run, 0.0), axis=1, keepdims=True)
    seg = seg_ref[...]
    tail = jnp.where(seg == jnp.max(seg), 1.0, 0.0)
    tmp_ref[0:16, :] = run
    tmp_ref[16:32, :] = jnp.exp2(last - row) * tail
    col = tmp_ref[...].T
    col_ref[...] = col
    b_rows = b_ref[...].astype(F32).T.astype(BF16)
    for i in range(tiles):
        cut = slice(128 * i, 128 * i + 128)
        weighted = (x_ref[:, cut].astype(F32) * halves(col, i, T, 16)).astype(BF16)
        both = dot(b_rows, weighted)
        kept = jnp.where(lanes_of((64, 128)) < 64, both[0:64], both[64:128])
        state_ref[0:64, cut] = kept.astype(BF16)
        gone = jnp.exp2(halves(col[T - 8 : T], i, 8))[7:8]
        final = jnp.broadcast_to((jnp.max(seg) + 1).astype(F32), (8, 128))
        state_ref[64:80, cut] = jnp.concatenate(
            [jnp.broadcast_to(gone, (8, 128)), final], axis=0
        ).astype(BF16)


def leaving_state(dt_rows, rate, seg_row, x, b):
    width = x.shape[1]
    return pl.pallas_call(
        state_kernel,
        out_shape=(
            jax.ShapeDtypeStruct((80, width), BF16),
            jax.ShapeDtypeStruct((16, T), F32),
            jax.ShapeDtypeStruct((T, 128), F32),
        ),
        scratch_shapes=[pltpu.VMEM((128, T), F32)],
        compiler_params=vmem(12),
        name="leaving_state",
    )(dt_rows, rate, seg_row, x, b)


def through_kernel(state_ref, near_ref, out_ref):
    tail = state_ref[64:80, :].astype(F32)
    before = near_ref[64:80, :].astype(F32)
    passes = jnp.where(tail[8:9] == before[8:9], tail[0:1], 0.0)
    out_ref[0:64, :] = (
        state_ref[0:64, :].astype(F32) + passes * near_ref[0:64, :].astype(F32)
    ).astype(BF16)
    out_ref[64:80, :] = state_ref[64:80, :]


def pass_through(state, near):
    return pl.pallas_call(
        through_kernel,
        out_shape=jax.ShapeDtypeStruct(state.shape, BF16),
        compiler_params=vmem(4),
        name="pass_through",
    )(state, near)


HALF = T // 2


def local_kernel(x_ref, b_ref, c_ref, row_ref, col_ref, segr_ref, segc_ref, skip_ref, out_ref, inner_ref):
    tiles = x_ref.shape[1] // 128
    b = b_ref[...]
    c = c_ref[...]
    live = (segc_ref[...] == segr_ref[...]) & (
        lax.broadcasted_iota(jnp.int32, (T, T), 0) >= lanes_of((T, T))
    )
    group = lanes_of((T, 128)) < 64
    for g in range(2):
        own = jnp.where(group == (g == 0), c, jnp.zeros_like(c))
        inner_ref[g] = jnp.where(live, dot(own, b, 1, 1), 0.0)
    col = col_ref[...]
    lane = lanes_of((T, 128))
    low = lanes_of((HALF, 128)) < 64

    def tile(i, _):
        cut = pl.ds(pl.multiple_of(i * 128, 128), 128)
        decays = [
            jnp.sum(jnp.where(lane == 2 * i + g, col, 0.0), axis=1, keepdims=True) for g in range(2)
        ]
        rows_of = [row_ref[pl.ds(2 * i + g, 1), :] for g in range(2)]
        for k in range(2):
            rows = slice(HALF * k, HALF * k + HALF)
            upto = HALF * (k + 1)
            parts = []
            for g in range(2):
                power = jnp.minimum(decays[g][rows] - rows_of[g][:, 0:upto], 126.0)
                mixing = (jnp.exp2(power) * inner_ref[g, rows, 0:upto]).astype(BF16)
                parts.append(dot(mixing, x_ref[0:upto, cut]))
            y = jnp.where(low, parts[0], parts[1])
            out_ref[rows, cut] = y + skip_ref[:, cut] * x_ref[rows, cut].astype(F32)
        return 0

    lax.fori_loop(0, tiles, tile, 0)


def mamba_local(x, b, c, row, col, seg_row, seg_col, skip):
    return pl.pallas_call(
        local_kernel,
        out_shape=jax.ShapeDtypeStruct(x.shape, F32),
        scratch_shapes=[pltpu.VMEM((2, T, T), F32)],
        compiler_params=vmem(14),
        name="mamba_local",
    )(x, b, c, row, col, seg_row, seg_col, skip)


def finish_kernel(y_ref, z_ref, c_ref, col_ref, segc_ref, carry_ref, out_ref, sq_ref):
    tiles = y_ref.shape[1] // 128
    c = c_ref[...]
    last = jnp.max(carry_ref[64:80, 0:128].astype(F32)[8:16])
    enters = segc_ref[...].astype(F32) + 1.0 == last
    entry = jnp.where(enters, jnp.exp2(col_ref[...]), 0.0)
    first = lanes_of((64, 128)) < 64
    total = jnp.zeros((T, 128), F32)
    for i in range(tiles):
        cut = slice(128 * i, 128 * i + 128)
        carry = carry_ref[0:64, cut]
        nothing = jnp.zeros_like(carry)
        spread_state = jnp.concatenate(
            [jnp.where(first, carry, nothing), jnp.where(first, nothing, carry)], axis=0
        )
        y = y_ref[:, cut] + halves(entry, i, T) * dot(c, spread_state)
        z = z_ref[:, cut].astype(F32)
        gated = y * (z / (1.0 + jnp.exp(-z)))
        out_ref[:, cut] = gated
        total = total + gated * gated
    turned = total.T
    even = jnp.sum(turned[0:64], axis=0, keepdims=True)
    odd = jnp.sum(turned[64:128], axis=0, keepdims=True)
    sq_ref[...] = jnp.concatenate([even, odd], axis=0)


def mamba_finish(y, z, c, col, seg_col, carry):
    return pl.pallas_call(
        finish_kernel,
        out_shape=(jax.ShapeDtypeStruct(y.shape, F32), jax.ShapeDtypeStruct((2, T), F32)),
        compiler_params=vmem(14),
        name="mamba_finish",
    )(y, z, c, col, seg_col, carry)


def normalize_kernel(gated_ref, sq_ref, gain_ref, out_ref):
    tiles = gated_ref.shape[1] // 128
    inverse = lax.rsqrt(sq_ref[...] / (tiles * 64 * 8) + EPS)
    spread = jnp.concatenate(
        [jnp.broadcast_to(inverse[0:1], (64, T)), jnp.broadcast_to(inverse[1:2], (64, T))], axis=0
    )
    for i in range(tiles):
        cut = slice(128 * i, 128 * i + 128)
        out_ref[cut, :] = ((gated_ref[:, cut] * gain_ref[:, cut]).T * spread).astype(BF16)


def normalize(gated, squares, gain):
    return pl.pallas_call(
        normalize_kernel,
        out_shape=jax.ShapeDtypeStruct(gated.shape[::-1], BF16),
        compiler_params=vmem(10),
        name="normalize",
    )(gated, squares, gain)


NONE = -1e30


def softmax_of(parts, values):
    top = parts[0]
    for part in parts[1:]:
        top = jnp.maximum(top, part)
    top = jnp.maximum(jnp.max(top, axis=0, keepdims=True), NONE)
    raised = [jnp.exp2(part - top) for part in parts]
    total = sum(raised)
    total = jnp.sum(total, axis=0, keepdims=True)
    some = total > 0.0
    safe = jnp.where(some, total, 1.0)
    share = jnp.where(some, 1.0 / safe, 0.0)
    out = sum(dot(value, (part * share).astype(BF16)) for part, value in zip(raised, values))
    return out, jnp.where(some, top + jnp.log2(safe), NONE)


def own_kernel(q_ref, k_ref, v_ref, segr_ref, segc_ref, out_ref, lse_ref):
    scale = LOG2E / math.sqrt(HD)
    mask = (segc_ref[...] == segr_ref[...]) & (
        lax.broadcasted_iota(jnp.int32, (T, T), 0) <= lanes_of((T, T))
    )
    lse_ref[...] = jnp.zeros_like(lse_ref)
    for h in range(q_ref.shape[0] // HD):
        at = slice(HD * h, HD * h + HD)
        part = jnp.where(mask, dot(k_ref[at, :], q_ref[at, :], 0, 0) * scale, -jnp.inf)
        out_ref[at, :], lse_ref[h : h + 1, :] = softmax_of([part], [v_ref[at, :]])


def attend_own(q, k, v, seg_row, seg_col):
    return pl.pallas_call(
        own_kernel,
        out_shape=(jax.ShapeDtypeStruct(q.shape, F32), jax.ShapeDtypeStruct((8, T), F32)),
        compiler_params=vmem(12),
        name="attend_own",
    )(q, k, v, seg_row, seg_col)


def next_kernel(q_ref, k_ref, v_ref, kv_ref, segc_ref, out_ref):
    width = k_ref.shape[0]
    scale = LOG2E / math.sqrt(HD)
    wanted = q_ref[width : width + 16, :].astype(F32)[0:1]
    ids = kv_ref[2 * width : 2 * width + 16, :].astype(F32)[0:8]
    before = jnp.concatenate([ids] * 16, axis=0).T[:, 0:1]
    masks = (segc_ref[...].astype(F32) + 1.0 == wanted, before == wanted)
    rows = []
    for h in range(width // HD):
        at = slice(HD * h, HD * h + HD)
        theirs = slice(width + HD * h, width + HD * h + HD)
        keys, values = (k_ref[at, :], kv_ref[at, :]), (v_ref[at, :], kv_ref[theirs, :])
        parts = [
            jnp.where(mask, dot(key, q_ref[at, :], 0, 0) * scale, -jnp.inf)
            for mask, key in zip(masks, keys)
        ]
        out, lse = softmax_of(parts, values)
        out_ref[at, :] = out.astype(BF16)
        for _ in range(3):
            rows.append(lse.astype(BF16).astype(F32))
            lse = lse - rows[-1]
    rows.append(jnp.ones((16 - len(rows), T), F32))
    out_ref[width : width + 16, :] = jnp.concatenate(rows, axis=0).astype(BF16)


def attend_next(q, k, v, kv, seg_col):
    return pl.pallas_call(
        next_kernel,
        out_shape=jax.ShapeDtypeStruct(q.shape, BF16),
        compiler_params=vmem(14),
        name="attend_next",
    )(q, k, v, kv, seg_col)


def merge_kernel(out_ref, lse_ref, far_ref, rows_ref):
    width = out_ref.shape[0]
    stats = far_ref[width : width + 16, :].astype(F32)
    given = stats[15:16] > 0.0
    merged = []
    for h in range(width // HD):
        at = slice(HD * h, HD * h + HD)
        lse = stats[3 * h : 3 * h + 1] + stats[3 * h + 1 : 3 * h + 2] + stats[3 * h + 2 : 3 * h + 3]
        lse = jnp.where(given, lse, NONE)
        own = lse_ref[h : h + 1, :]
        top = jnp.maximum(lse, own)
        near, far = jnp.exp2(own - top), jnp.exp2(lse - top)
        total = near + far
        merged.append(
            out_ref[at, :] * (near / total) + far_ref[at, :].astype(F32) * (far / total)
        )
    rows_ref[...] = jnp.concatenate(merged, axis=0).astype(BF16)


def merge(out, lse, far):
    return pl.pallas_call(
        merge_kernel,
        out_shape=jax.ShapeDtypeStruct(out.shape, BF16),
        compiler_params=vmem(8),
        name="merge",
    )(out, lse, far)


def project_kernel(place_ref, att_ref, mam_ref, wa_ref, wm_ref, own_ref, other_ref):
    half = own_ref.shape[0]
    out = dot(wa_ref[...], att_ref[...], 0, 0) + dot(wm_ref[...], mam_ref[...], 0, 0)
    first = place_ref[1] == 0
    own_ref[...] = jnp.where(first, out[0:half], out[half:])
    other_ref[...] = jnp.where(first, out[half:], out[0:half]).astype(BF16)


def project(place, att, mam, wa, wm):
    rows = wa.shape[0]
    once = pl.Buffered(1)
    block = pl.BlockSpec((rows, T), lambda s, p: (0, 0), pipeline_mode=once)
    return pl.pallas_call(
        project_kernel,
        grid_spec=pltpu.PrefetchScalarGridSpec(
            num_scalar_prefetch=1,
            grid=(1,),
            in_specs=[
                pl.BlockSpec(att.shape, lambda s, p: (0, 0), pipeline_mode=once),
                pl.BlockSpec(mam.shape, lambda s, p: (0, 0), pipeline_mode=once),
                pl.BlockSpec((rows, 2 * rows), lambda s, p: (0, p[0]), pipeline_mode=once),
                pl.BlockSpec((wm.shape[0], 2 * rows), lambda s, p: (0, p[0]), pipeline_mode=once),
            ],
            out_specs=(block, block),
        ),
        out_shape=(
            jax.ShapeDtypeStruct((rows, T), F32), jax.ShapeDtypeStruct((rows, T), BF16)
        ),
        compiler_params=vmem(12),
        name="project",
    )(place, att, mam, wa, wm)


def prepare_kernel(place_ref, *refs):
    z_refs, unscale_ref, rows_ref, inv_ref = refs[:-3], refs[-3], refs[-2], refs[-1]
    chips = len(z_refs) // 2
    pair = unscale_ref.shape[1]
    first = place_ref[1] == 0
    total = jnp.zeros((T, 128), F32)
    for d in range(chips):
        mine, theirs = z_refs[2 * d][...], z_refs[2 * d + 1][...]
        both = jnp.concatenate(
            [jnp.where(first, mine, theirs), jnp.where(first, theirs, mine)], axis=0
        ).T
        chip = lax.rem(place_ref[0] + chips - d, chips)
        rows_ref[:, pl.ds(pl.multiple_of(chip * pair, 128), pair)] = both
        plain = both.astype(F32) * unscale_ref[pl.ds(chip, 1), :]
        square = plain * plain
        for i in range(pair // 128):
            total = total + square[:, 128 * i : 128 * i + 128]
    inv_ref[...] = jnp.broadcast_to(
        lax.rsqrt(jnp.sum(total, axis=1, keepdims=True) / (chips * pair) + EPS), (T, 128)
    )


def prepare(place, blocks, unscale):
    smem = pl.BlockSpec(memory_space=pltpu.SMEM)
    full = pl.BlockSpec(memory_space=pltpu.VMEM)
    return pl.pallas_call(
        prepare_kernel,
        in_specs=[smem] + [full] * (len(blocks) + 1),
        out_shape=(
            jax.ShapeDtypeStruct((T, unscale.size), BF16), jax.ShapeDtypeStruct((T, 128), F32)
        ),
        compiler_params=vmem(14),
        name="prepare",
    )(place, *blocks, unscale)


def activate_kernel(rows_ref, inv_ref, gu_ref, act_ref):
    width = rows_ref.shape[1]
    w = jnp.concatenate(
        [gu_ref[:, 0].reshape(width, 128), gu_ref[:, 1].reshape(width, 128)], axis=1
    )
    both = dot(rows_ref[...], w)
    gate = both[:, 0:128] * inv_ref[...]
    up = both[:, 128:256] * inv_ref[...]
    act_ref[...] = (gate / (1.0 + jnp.exp(-gate)) * up).astype(BF16)


def activate(rows, inv, weights):
    parts, _, height, hidden = weights.shape
    once = pl.Buffered(1)
    return pl.pallas_call(
        activate_kernel,
        grid=(hidden // 128,),
        in_specs=[
            pl.BlockSpec(rows.shape, lambda s: (0, 0), pipeline_mode=once),
            pl.BlockSpec(inv.shape, lambda s: (0, 0), pipeline_mode=once),
            pl.BlockSpec((parts, 2, height, 128), lambda s: (0, 0, 0, s)),
        ],
        out_specs=pl.BlockSpec((T, 128), lambda s: (0, s)),
        out_shape=jax.ShapeDtypeStruct((T, hidden), BF16),
        compiler_params=vmem(16),
        name="activate",
    )(rows, inv, weights)


def down_kernel(place_ref, act_ref, w_ref, own_ref, other_ref):
    half, hidden = own_ref.shape[0], act_ref.shape[1]
    per = w_ref.shape[0] // 2
    act = act_ref[...]
    c = place_ref[1]
    theirs = w_ref[pl.ds(per * (1 - c), per), 0].reshape(half, hidden)
    other_ref[...] = dot(theirs, act, 1, 1).astype(BF16)
    mine = w_ref[pl.ds(per * c, per), 0].reshape(half, hidden)
    own_ref[...] = dot(mine, act, 1, 1)


def down(place, act, weights):
    parts, _, height, hidden = weights.shape
    per = parts // 4
    rows = per * height // 2
    return pl.pallas_call(
        down_kernel,
        grid_spec=pltpu.PrefetchScalarGridSpec(
            num_scalar_prefetch=1,
            grid=(1,),
            in_specs=[
                pl.BlockSpec(act.shape, lambda s, p: (0, 0)),
                pl.BlockSpec((per, 1, height, hidden), lambda s, p: (p[0], 2, 0, 0)),
            ],
            out_specs=(
                pl.BlockSpec((rows, T), lambda s, p: (0, 0)),
                pl.BlockSpec((rows, T), lambda s, p: (0, 0)),
            ),
        ),
        out_shape=(
            jax.ShapeDtypeStruct((rows, T), F32), jax.ShapeDtypeStruct((rows, T), BF16)
        ),
        compiler_params=vmem(14),
        name="down",
    )(place, act, weights)


def behind(value, steps):
    count = lax.axis_size(REQ)
    pairs = [(i, i + steps) for i in range(count) if 0 <= i + steps < count]
    return lax.ppermute(value, REQ, pairs)


def along(value, steps):
    count = lax.axis_size("x")
    return lax.ppermute(value, "x", [(i, (i + steps) % count) for i in range(count)])


def swap(value):
    return lax.ppermute(value, "c", [(0, 1), (1, 0)])


ORDER = (2, 1, 3, 0)


def scatter_sum(block_of, source):
    sent, waiting = [], []

    def send(s, own, other):
        paired = own + other.astype(F32)
        if not s:
            sent.append(paired)
            return paired
        narrow = paired.astype(BF16)
        sent.append(along(narrow, s).astype(F32))
        return narrow

    for s in ORDER:
        own, other = block_of(s, source)
        waiting.append((s, own, swap(other)))
        if s in (1, 3):
            done = [send(*item) for item in waiting][-1]
            source, _ = lax.optimization_barrier((source, done))
            waiting = []
    for item in waiting:
        send(*item)
    return sent[0] + sent[1] + sent[2] + sent[3]


def gather_rows(share):
    got = []
    for d in range(4):
        here = along(share, d) if d else share
        got += [here, swap(here)]
    return got


def group_sum(value):
    paired = value + swap(value)
    return paired + along(paired, 1) + along(paired, 2) + along(paired, 3)


def body(
    hidden, query_heads, key_heads, value_heads, segment_ids, page_table, mamba_conv_input,
    mamba_output_gate, state_input_projection, state_output_projection, discrete_step_size,
    head_decay_rate, skip_gain, mamba_gated_norm_gain, attn_proj, mamba_output_projection,
    mlp_norm_gain, gate_proj, up_proj, down_proj, next_norm_gain,
):
    row_count = query_heads.shape[0]
    head_count = query_heads.shape[1] // HD
    width = hidden.shape[1]
    total_width = mlp_norm_gain.shape[0]
    owner = lax.axis_index("x") * lax.axis_size("c") + lax.axis_index("c")

    x = lax.axis_index("x")
    core = lax.axis_index("c")

    def place(steps):
        return jnp.stack([(x + steps) % 4, core]).astype(jnp.int32)

    stacked_weights = jnp.stack([gate_proj, up_proj, down_proj.T])
    weights = in_hbm(lax.all_gather(stacked_weights, REQ, axis=0, tiled=False))

    seg_row = segment_ids.reshape(1, row_count)
    seg_col = segment_ids.reshape(row_count, 1)
    state, row, col = leaving_state(
        discrete_step_size.T, head_decay_rate.reshape(-1, 1), seg_row, mamba_conv_input,
        state_input_projection,
    )
    near = behind(state, 1)

    q, k, v = query_heads.T, key_heads.T, value_heads.T
    ids = jnp.broadcast_to((segment_ids + 1).astype(BF16)[None, :], (16, row_count))
    kv1 = behind(jnp.concatenate([k, v, ids], axis=0), 1)
    next_q = behind(jnp.concatenate([q, ids], axis=0), -1)

    page_count = page_table.shape[1]

    def to_pages(source):
        return (
            source.reshape(page_count, PAGE, head_count, HD)
            .transpose(2, 0, 1, 3)
            .reshape(head_count, page_count, PAGE * HD)
        )

    stacked = jnp.stack([to_pages(key_heads), to_pages(value_heads)])
    kv_cache = jnp.zeros_like(stacked).at[:, :, page_table[0]].set(stacked)

    own_out, own_lse = attend_own(q, k, v, seg_row, seg_col)
    skip = jnp.repeat(skip_gain, mamba_conv_input.shape[1] // skip_gain.shape[0]).reshape(1, -1)
    local = mamba_local(
        mamba_conv_input, state_input_projection, state_output_projection, row, col, seg_row,
        seg_col, skip,
    )
    waited_col, own_lse, local = lax.optimization_barrier((seg_col, own_lse, local))
    next_out = attend_next(next_q, k, v, kv1, waited_col)
    far_out = behind(next_out, 1)
    state, near, _ = lax.optimization_barrier((state, near, next_out))
    carry = behind(pass_through(state, near), 1)
    gated, squares = mamba_finish(
        in_hbm(local), mamba_output_gate, state_output_projection, col, seg_col, carry
    )
    mam = normalize(gated, group_sum(squares), mamba_gated_norm_gain.reshape(1, -1))
    own_out, mam = lax.optimization_barrier((own_out, mam))
    att = merge(in_hbm(own_out), own_lse, far_out)
    attn_proj, mamba_output_projection = in_hbm(attn_proj), in_hbm(mamba_output_projection)
    mixed = hidden.T.astype(F32) + scatter_sum(
        lambda s, rows: project(place(s), rows, mam, attn_proj, mamba_output_projection), att
    )
    own_gain = lax.dynamic_slice_in_dim(mlp_norm_gain, owner * width, width, 0)
    blocks = gather_rows((mixed * own_gain[:, None]).astype(BF16))
    rows, inv = prepare(place(0), blocks, (1.0 / mlp_norm_gain).reshape(4, -1))
    act = activate(in_hbm(rows), inv, weights)
    new_hidden = (mixed + scatter_sum(lambda s, rows: down(place(s), rows, weights), act)).astype(BF16)
    widened = new_hidden.astype(F32)
    total_sq = group_sum(jnp.sum(widened * widened, axis=0, keepdims=True))
    next_normed = (
        widened * lax.rsqrt(total_sq / total_width + EPS) * next_norm_gain[:, None]
    ).astype(BF16)

    return (new_hidden.T, next_normed.T, kv_cache)


def solution(mesh):
    split = Mesh(mesh.devices.reshape(4, 4, 4, 2), ("z", "y", "x", "c"))
    tokens = P(REQ, MLP)
    return jax.shard_map(
        body,
        mesh=split,
        in_specs=(
            tokens, tokens, tokens, tokens, P(REQ), P(REQ, None), tokens, tokens, P(REQ, None),
            P(REQ, None), tokens, P(MLP), P(MLP), P(MLP), P(MLP, None), P(MLP, None), P(), tokens,
            tokens, P(MLP, REQ), P(MLP),
        ),
        out_specs=(tokens, tokens, P(None, MLP, REQ, None)),
        check_vma=False,
    )
```

time: 276 us -> 234 us (0.85)
  blocking collectives: 28.5 us -> 0 us
  waiting for transfers between devices: 109 us -> 81 us
  starting transfers between devices: 23.3 us -> 37.4 us
  local copies, waits for them, and re-layouts: 28.2 us -> 18 us
  Pallas kernels: 53.6 us -> 62.4 us
    psum x2 -> x0, blocking collectives: 28.5 us -> none  [the longest x1 14.6 us: body(): total_sq = lax.psum(jnp.sum(widened * widened, axis=0), MLP)]
    ppermute x4 -> x5, waiting for transfers between devices: 48.1 us -> 25.3 us  [behind(): return lax.ppermute(value, REQ, pairs)]
    pallas_call x4 -> x17, Pallas kernels: 49.4 us -> 60.2 us  [the longest x4 18.4 us: project(): pl.pallas_call(project_kernel, grid_spec=pltpu.PrefetchScalarGridSpec(num...]
    ppermute x9 -> x15, starting transfers between devices: 10.6 us -> 19.8 us  [along(): lax.ppermute(value, 'x', [(i, (i + steps) % count) for i in range(count)])]
    squeeze x4 -> x0, local copies, waits for them, and re-layouts: 7.07 us -> none  [the longest x2 5.85 us: scatter_sum(): other = lax.dynamic_index_in_dim(blocks, 1 - c, 1, keepdims=False)]
    unnamed x49 -> x57, local copies, waits for them, and re-layouts: 4.79 us -> 10.2 us
    ppermute x9 -> x15, waiting for transfers between devices: 56.2 us -> 51.5 us  [along(): lax.ppermute(value, 'x', [(i, (i + steps) % count) for i in range(count)])]
    dynamic_update_slice x5 -> x0, local copies, waits for them, and re-layouts: 3.9 us -> none  [the longest x1 1.4 us: gather_rows(): full = lax.dynamic_update_index_in_dim(full, got, c, 1)]
  transfers between devices with their start and end apart: 17 -> 35, of which waited for: 11 -> 16; matrix products, arithmetic and copies ran while one was open for 10% -> 10% of each run, Pallas kernels for 12% -> 20%
where the time goes in v2:
time: 234 us; the launch traced here: 232 us
  waiting for transfers between devices  81 us (35%)
  Pallas kernels  62.4 us (27%)
  starting transfers between devices  37.4 us (16%)
  other arithmetic  18.9 us (8%)
  local copies, waits for them, and re-layouts  18 us (8%)
  between operations  14.5 us (6%)
    ppermute x15, waiting for transfers between devices, along(): lax.ppermute(value, 'x', [(i, (i + steps) % count) for i in range(count)])  51.5 us
    ppermute x5, waiting for transfers between devices, behind(): return lax.ppermute(value, REQ, pairs)  25.3 us
    ppermute x15, starting transfers between devices, along(): lax.ppermute(value, 'x', [(i, (i + steps) % count) for i in range(count)])  19.8 us
    pallas_call x4, Pallas kernels, project(): pl.pallas_call(project_kernel, grid_spec=pltpu.PrefetchScalarGridSpec(num...  18.4 us
    ppermute x5, starting transfers between devices, behind(): return lax.ppermute(value, REQ, pairs)  15.2 us
    pallas_call x4, Pallas kernels, down(): pl.pallas_call(down_kernel, grid_spec=pltpu.PrefetchScalarGridSpec(num_sc...  12.4 us
    pallas_call x1, Pallas kernels, activate(): pl.pallas_call(activate_kernel, grid=(hidden // 128,), in_specs=[pl.Block...  11.9 us
    unnamed x57, local copies, waits for them, and re-layouts  10.2 us
  transfers between devices with their start and end apart: 35, of which 16 were waited for; matrix products, arithmetic and copies ran while one was open for 10% of the time, Pallas kernels for 20%

profile of v2, /device:TPU:96, one launch (start us, length us, event | category | flops | bytes accessed | tf_op | source)
XLA Modules:
  0.0 232.2 jit_solution(11266027594481398534)
XLA Ops:
  7.2 2.5 %pad_maximum_fusion = bf16[3,224,896]{2,1,0:T(8,128)(2,1)} fusion(bf16[1,224,896]{2,1,0:T(8,128)(2,1)} %bitcast.60, bf16[1,224,896]{2,1,0:T(8,128)(2,1)} %bitcast.61, bf16[1,224,896]{2,1,0:T(8,128)(2,1)} %bitcast.62), kind=kLoop, calls=%fused_computation.1 | loop fusion | flops 1204224 | bytes 2408448 | tf_op jit(solution)/shard_map/stack | solution.py:527
  10.9 3.5 %collective-permute-start.2 = (bf16[912,512]{1,0:T(8,128)(2,1)}, bf16[912,512]{1,0:T(8,128)(2,1)}, u32[]{:S(2)}, u32[]{:S(2)}) collective-permute-start(bf16[912,512]{1,0:T(8,128)(2,1)} %pad_maximum_fusion.1), channel_id=1, source_target_pairs={{0,8},{8,16},{16,24},{24,32},{32,40},{40,48},{48,56},{56,64},{64,7... | collective-permute-start | bytes 2801672 | tf_op jit(solution)/shard_map/ppermute | solution.py:457
  15.2 4.5 %collective-permute-start.1 = (bf16[464,512]{1,0:T(8,128)(2,1)}, bf16[464,512]{1,0:T(8,128)(2,1)}, u32[]{:S(2)}, u32[]{:S(2)}) collective-permute-start(bf16[464,512]{1,0:T(8,128)(2,1)} %pad_maximum_fusion.2), channel_id=1, source_target_pairs={{8,0},{16,8},{24,16},{32,24},{40,32},{48,40},{56,48},{64,56},{72,6... | collective-permute-start | bytes 1425416 | tf_op jit(solution)/shard_map/ppermute | solution.py:457
  19.8 2.1 leaving_state.1
  21.9 1.9 collective-permute-start
  24.0 1.3 attend_own.1
  26.4 3.9 %mamba_local.1.y_ref = f32[512,896]{1,0:T(8,128)S(1)} custom-call(bf16[512,896]{1,0:T(8,128)(2,1)S(1)} %copy-done.3, bf16[512,128]{1,0:T(8,128)(2,1)S(1)} %copy-done.14, bf16[512,128]{1,0:T(8,128)(2,1)S(1)} %copy-done.15, f32[16,512]{1,0:T(8,128)S(1)} %get-tuple-element.41.row_ref, f32[512,128]{1,0:T(8,128)S(1)} %get-tuple-element.42.col_ref, ...), custom_call_target="tpu_custom_call" | custom-call | tf_op jit(solution)/shard_map/mamba_local/pallas_call | solution.py:154
  31.7 6.2 %collective-permute-done.1.q_ref = bf16[464,512]{1,0:T(8,128)(2,1)} collective-permute-done((bf16[464,512]{1,0:T(8,128)(2,1)}, bf16[464,512]{1,0:T(8,128)(2,1)}, u32[]{:S(2)}, u32[]{:S(2)}) %collective-permute-start.1) | collective-permute-done | bytes 475168 | tf_op jit(solution)/shard_map/ppermute | solution.py:457
  38.0 13.3 %collective-permute-done.2.kv_ref = bf16[912,512]{1,0:T(8,128)(2,1)} collective-permute-done((bf16[912,512]{1,0:T(8,128)(2,1)}, bf16[912,512]{1,0:T(8,128)(2,1)}, u32[]{:S(2)}, u32[]{:S(2)}) %collective-permute-start.2) | collective-permute-done | bytes 933920 | tf_op jit(solution)/shard_map/ppermute | solution.py:457
  51.2 4.5 %attend_next.1 = bf16[464,512]{1,0:T(8,128)(2,1)} custom-call(bf16[464,512]{1,0:T(8,128)(2,1)} %collective-permute-done.1.q_ref, bf16[448,512]{1,0:T(8,128)(2,1)S(1)} %bitcast.43, bf16[448,512]{1,0:T(8,128)(2,1)S(1)} %bitcast.40, bf16[912,512]{1,0:T(8,128)(2,1)} %collective-permute-done.2.kv_ref, s32[512,1]{1,0:T(8,128)S(1)} %copy.50.segc_ref), custom_call_target="tpu_custom_call" | custom-call | tf_op jit(solution)/shard_map/attend_next/pallas_call | solution.py:283
  56.2 1.9 collective-permute-start.3
  58.1 3.4 %collective-permute-start.8 = (bf16[464,512]{1,0:T(8,128)(2,1)}, bf16[464,512]{1,0:T(8,128)(2,1)}, u32[]{:S(2)}, u32[]{:S(2)}) collective-permute-start(bf16[464,512]{1,0:T(8,128)(2,1)} %attend_next.1), channel_id=1, source_target_pairs={{0,8},{8,16},{16,24},{24,32},{32,40},{40,48},{48,56},{56,64},{64,7... | collective-permute-start | bytes 1425416 | tf_op jit(solution)/shard_map/ppermute | solution.py:457
  61.5 5.4 %collective-permute-done.3.carry_ref = bf16[80,896]{1,0:T(8,128)(2,1)S(1)} collective-permute-done((bf16[80,896]{1,0:T(8,128)(2,1)S(1)}, bf16[80,896]{1,0:T(8,128)(2,1)S(1)}, u32[]{:S(2)}, u32[]{:S(2)}) %collective-permute-start.3) | collective-permute-done | bytes 143392 | tf_op jit(solution)/shard_map/ppermute | solution.py:457
  66.9 2.9 %mamba_finish.1 = (f32[512,896]{1,0:T(8,128)S(1)}, f32[2,512]{1,0:T(2,128)S(1)}) custom-call(f32[512,896]{1,0:T(8,128)} %copy-done, bf16[512,896]{1,0:T(8,128)(2,1)S(1)} %copy-done.13, bf16[512,128]{1,0:T(8,128)(2,1)S(1)} %copy-done.15, f32[512,128]{1,0:T(8,128)S(1)} %get-tuple-element.42.col_ref, s32[512,1]{1,0:T(8,128)S(1)} %copy.47.segc_ref, ...), custom_call_target="tpu_custom_call" | custom-call | tf_op jit(solution)/shard_map/mamba_finish/pallas_call | solution.py:190
  72.3 2.8 %collective-permute-start.7 = (f32[2,512]{1,0:T(2,128)S(1)}, f32[2,512]{1,0:T(2,128)S(1)}, u32[]{:S(2)}, u32[]{:S(2)}) collective-permute-start(f32[2,512]{1,0:T(2,128)S(1)} %add.137), channel_id=1, source_target_pairs={{0,6},{2,0},{4,2},{6,4},{1,7},{3,1},{5,3},{7,5},{8,14},{10,8},{12,... | collective-permute-start | bytes 12296 | tf_op jit(solution)/shard_map/ppermute | solution.py:462
  76.9 3.4 %collective-permute-done.6 = f32[2,512]{1,0:T(2,128)S(1)} collective-permute-done((f32[2,512]{1,0:T(2,128)S(1)}, f32[2,512]{1,0:T(2,128)S(1)}, u32[]{:S(2)}, u32[]{:S(2)}) %collective-permute-start.6) | collective-permute-done | bytes 4128 | tf_op jit(solution)/shard_map/ppermute | solution.py:462
  80.7 1.6 copy-done.6
  82.8 1.6 merge.1.att_ref
  84.4 4.6 %project.5 = (f32[448,512]{1,0:T(8,128)S(1)}, bf16[448,512]{1,0:T(8,128)(2,1)}) custom-call(s32[2]{0:T(128)S(1)} %get-tuple-element.92.place_ref, bf16[448,512]{1,0:T(8,128)(2,1)S(1)} %merge.1.att_ref, bf16[896,512]{1,0:T(8,128)(2,1)S(1)} %normalize.1.mam_ref, bf16[448,3584]{1,0:T(8,128)(2,1)} %wa_ref.7, bf16[896,3584]{1,0:T(8,128)(2,1)} %wm_ref.7), custom_call_target="tpu_custom_call" | custom-call | tf_op jit(solution)/shard_map/project/pallas_call | solution.py:331
  90.0 4.6 %project.4 = (f32[448,512]{1,0:T(8,128)S(1)}, bf16[448,512]{1,0:T(8,128)(2,1)}) custom-call(s32[2]{0:T(128)S(1)} %get-tuple-element.91.place_ref, bf16[448,512]{1,0:T(8,128)(2,1)S(1)} %merge.1.att_ref, bf16[896,512]{1,0:T(8,128)(2,1)S(1)} %normalize.1.mam_ref, bf16[448,3584]{1,0:T(8,128)(2,1)} %wa_ref.7, bf16[896,3584]{1,0:T(8,128)(2,1)} %wm_ref.7), custom_call_target="tpu_custom_call" | custom-call | tf_op jit(solution)/shard_map/project/pallas_call | solution.py:331
  95.1 2.0 add_convert_fusion.5
  97.1 4.6 %project.6 = (f32[448,512]{1,0:T(8,128)S(1)}, bf16[448,512]{1,0:T(8,128)(2,1)}) custom-call(s32[2]{0:T(128)S(1)} %pad_add_fusion.2.place_ref, bf16[448,512]{1,0:T(8,128)(2,1)S(1)} %merge.1.att_ref, bf16[896,512]{1,0:T(8,128)(2,1)S(1)} %normalize.1.mam_ref, bf16[448,3584]{1,0:T(8,128)(2,1)} %wa_ref.7, bf16[896,3584]{1,0:T(8,128)(2,1)} %wm_ref.7), custom_call_target="tpu_custom_call" | custom-call | tf_op jit(solution)/shard_map/project/pallas_call | solution.py:331
  102.7 2.0 add_convert_fusion.6
  104.7 1.9 collective-permute-start.10
  106.7 1.9 add_convert_fusion.4
  108.6 4.6 %project.7 = (f32[448,512]{1,0:T(8,128)S(1)}, bf16[448,512]{1,0:T(8,128)(2,1)}) custom-call(s32[2]{0:T(128)S(1)} %pad_add_fusion.3.place_ref, bf16[448,512]{1,0:T(8,128)(2,1)S(1)} %merge.1.att_ref, bf16[896,512]{1,0:T(8,128)(2,1)S(1)} %normalize.1.mam_ref, bf16[448,3584]{1,0:T(8,128)(2,1)} %wa_ref.7, bf16[896,3584]{1,0:T(8,128)(2,1)} %wm_ref.7), custom_call_target="tpu_custom_call" | custom-call | tf_op jit(solution)/shard_map/project/pallas_call | solution.py:331
  113.3 2.3 collective-permute-start.14
  115.6 11.4 %collective-permute-done.12 = bf16[448,512]{1,0:T(8,128)(2,1)} collective-permute-done((bf16[448,512]{1,0:T(8,128)(2,1)}, bf16[448,512]{1,0:T(8,128)(2,1)}, u32[]{:S(2)}, u32[]{:S(2)}) %collective-permute-start.12) | collective-permute-done | bytes 458784 | tf_op jit(solution)/shard_map/ppermute | solution.py:462
  127.0 2.4 %collective-permute-done.14 = bf16[448,512]{1,0:T(8,128)(2,1)S(1)} collective-permute-done((bf16[448,512]{1,0:T(8,128)(2,1)}, bf16[448,512]{1,0:T(8,128)(2,1)S(1)}, u32[]{:S(2)}, u32[]{:S(2)}) %collective-permute-start.14) | collective-permute-done | bytes 458784 | tf_op jit(solution)/shard_map/ppermute | solution.py:462
  129.4 2.6 %multiply_convert_fusion = (bf16[448,512]{1,0:T(8,128)(2,1)S(1)}, f32[448,512]{1,0:T(8,128)}) fusion(f32[448]{0:T(512)S(1)} %dynamic_slice.3, f32[448,512]{1,0:T(8,128)S(1)} %get-tuple-element.61, bf16[448,512]{1,0:T(8,128)(2,1)S(1)} %collective-permute-done.15, bf16[448,512]{1,0:T(8,128)(2,1)S(1)} %collective-permute-done.14, ...), kind=kLoop, calls=%fused_computation.14 | loop fusion | flops 2752512 | bytes 4589312 | tf_op jit(solution)/shard_map/convert_element_type | solution.py:577
  132.9 3.2 %collective-permute-start.19 = (bf16[448,512]{1,0:T(8,128)(2,1)S(1)}, bf16[448,512]{1,0:T(8,128)(2,1)S(1)}, u32[]{:S(2)}, u32[]{:S(2)}) collective-permute-start(bf16[448,512]{1,0:T(8,128)(2,1)S(1)} %get-tuple-element.89.refs_0_), channel_id=1, source_target_pairs={{0,4},{2,6},{4,0},{6,2},{1,5},{3,7},{5,1},{7,3},{8,12},{10,14},{12... | collective-permute-start | bytes 1376264 | tf_op jit(solution)/shard_map/ppermute | solution.py:462
  136.2 9.3 %collective-permute-done.17.refs_2_ = bf16[448,512]{1,0:T(8,128)(2,1)S(1)} collective-permute-done((bf16[448,512]{1,0:T(8,128)(2,1)S(1)}, bf16[448,512]{1,0:T(8,128)(2,1)S(1)}, u32[]{:S(2)}, u32[]{:S(2)}) %collective-permute-start.17) | collective-permute-done | bytes 458784 | tf_op jit(solution)/shard_map/ppermute | solution.py:462
  145.5 11.0 %collective-permute-done.19.refs_4_ = bf16[448,512]{1,0:T(8,128)(2,1)S(1)} collective-permute-done((bf16[448,512]{1,0:T(8,128)(2,1)S(1)}, bf16[448,512]{1,0:T(8,128)(2,1)S(1)}, u32[]{:S(2)}, u32[]{:S(2)}) %collective-permute-start.19) | collective-permute-done | bytes 458784 | tf_op jit(solution)/shard_map/ppermute | solution.py:462
  157.1 1.4 collective-permute-done.20.refs_5_
  159.1 2.8 %prepare.1 = (bf16[512,3584]{1,0:T(8,128)(2,1)S(1)}, f32[512,128]{1,0:T(8,128)S(1)}) custom-call(s32[2]{0:T(128)S(1)} %pad_add_fusion.3.place_ref, bf16[448,512]{1,0:T(8,128)(2,1)S(1)} %get-tuple-element.89.refs_0_, bf16[448,512]{1,0:T(8,128)(2,1)S(1)} %collective-permute-done.16.refs_1_, bf16[448,512]{1,0:T(8,128)(2,1)S(1)} %collective-permute-done.17.refs_2_, ...), custom_call_target="tpu_custom_call" | custom-call | tf_op jit(solution)/shard_map/prepare/pallas_call | solution.py:377
  161.9 1.8 copy-done.4
  163.7 11.9 %activate.1.act_ref = bf16[512,896]{1,0:T(8,128)(2,1)S(1)} custom-call(bf16[512,3584]{1,0:T(8,128)(2,1)} %copy-done.4, f32[512,128]{1,0:T(8,128)S(1)} %get-tuple-element.64.inv_ref, bf16[16,3,224,896]{3,2,1,0:T(8,128)(2,1)} %bitcast.52), custom_call_target="tpu_custom_call" | custom-call | tf_op jit(solution)/shard_map/activate/pallas_call | solution.py:402
  175.6 3.1 %down.5 = (f32[448,512]{1,0:T(8,128)S(1)}, bf16[448,512]{1,0:T(8,128)(2,1)S(1)}) custom-call(s32[2]{0:T(128)S(1)} %get-tuple-element.92.place_ref, bf16[512,896]{1,0:T(8,128)(2,1)S(1)} %activate.1.act_ref, bf16[16,3,224,896]{3,2,1,0:T(8,128)(2,1)} %bitcast.53), custom_call_target="tpu_custom_call" | custom-call | tf_op jit(solution)/shard_map/down/pallas_call | solution.py:432
  179.1 3.1 %down.4 = (f32[448,512]{1,0:T(8,128)S(1)}, bf16[448,512]{1,0:T(8,128)(2,1)S(1)}) custom-call(s32[2]{0:T(128)S(1)} %get-tuple-element.91.place_ref, bf16[512,896]{1,0:T(8,128)(2,1)S(1)} %activate.1.act_ref, bf16[16,3,224,896]{3,2,1,0:T(8,128)(2,1)} %bitcast.54), custom_call_target="tpu_custom_call" | custom-call | tf_op jit(solution)/shard_map/down/pallas_call | solution.py:432
  183.6 3.1 %down.6 = (f32[448,512]{1,0:T(8,128)S(1)}, bf16[448,512]{1,0:T(8,128)(2,1)S(1)}) custom-call(s32[2]{0:T(128)S(1)} %pad_add_fusion.2.place_ref, bf16[512,896]{1,0:T(8,128)(2,1)S(1)} %activate.1.act_ref, bf16[16,3,224,896]{3,2,1,0:T(8,128)(2,1)} %bitcast.55), custom_call_target="tpu_custom_call" | custom-call | tf_op jit(solution)/shard_map/down/pallas_call | solution.py:432
  187.9 2.9 %collective-permute-start.24 = (bf16[448,512]{1,0:T(8,128)(2,1)}, bf16[448,512]{1,0:T(8,128)(2,1)}, u32[]{:S(2)}, u32[]{:S(2)}) collective-permute-start(bf16[448,512]{1,0:T(8,128)(2,1)} %add_convert_fusion.3), channel_id=1, source_target_pairs={{0,4},{2,6},{4,0},{6,2},{1,5},{3,7},{5,1},{7,3},{8,12},{10,14},{12... | collective-permute-start | bytes 1376264 | tf_op jit(solution)/shard_map/ppermute | solution.py:462
  191.7 3.1 %down.7 = (f32[448,512]{1,0:T(8,128)S(1)}, bf16[448,512]{1,0:T(8,128)(2,1)S(1)}) custom-call(s32[2]{0:T(128)S(1)} %pad_add_fusion.3.place_ref, bf16[512,896]{1,0:T(8,128)(2,1)S(1)} %activate.1.act_ref, bf16[16,3,224,896]{3,2,1,0:T(8,128)(2,1)} %bitcast.56), custom_call_target="tpu_custom_call" | custom-call | tf_op jit(solution)/shard_map/down/pallas_call | solution.py:432
  196.2 1.6 stack_reshape.7
  199.1 12.0 %collective-permute-done.26 = bf16[448,512]{1,0:T(8,128)(2,1)} collective-permute-done((bf16[448,512]{1,0:T(8,128)(2,1)}, bf16[448,512]{1,0:T(8,128)(2,1)}, u32[]{:S(2)}, u32[]{:S(2)}) %collective-permute-start.26) | collective-permute-done | bytes 458784 | tf_op jit(solution)/shard_map/ppermute | solution.py:462
  211.1 1.6 collective-permute-done.28
  212.7 1.9 fusion
  215.9 2.6 %collective-permute-start.33 = (f32[1,512]{1,0:T(1,128)S(1)}, f32[1,512]{1,0:T(1,128)S(1)}, u32[]{:S(2)}, u32[]{:S(2)}) collective-permute-start(f32[1,512]{1,0:T(1,128)S(1)} %add.164), channel_id=1, source_target_pairs={{0,6},{2,0},{4,2},{6,4},{1,7},{3,1},{5,3},{7,5},{8,14},{10,8},{12,... | collective-permute-start | bytes 6152 | tf_op jit(solution)/shard_map/ppermute | solution.py:462
  220.9 2.6 %scatter_fusion = bf16[2,2,32,3584]{3,1,2,0:T(2,128)(2,1)S(1)} fusion(bf16[2,2,32,3584]{3,1,2,0:T(2,128)(2,1)S(1)} %broadcast_in_dim.21, s32[32]{0:T(128)S(1)} %fusion.4, bf16[32,2,2,3584]{3,2,1,0:T(2,128)(2,1)S(1)} %copy.56), kind=kCustom, calls=%fused_computation | custom fusion | bytes 2752640 | tf_op jit(solution)/shard_map/scatter | solution.py:553
  (139 shorter events, 27.3 us)
Async XLA Ops:
  7.2 156.5 %all-gather.3.cloned.1.call-start = ((), (), s32[]{:S(2)}) async-start(), calls=%async_computation | async-start | bytes 20471808 | tf_op jit(solution)/shard_map/all_gather | solution.py:528
  9.7 10.0 %copy-start.24 = (f32[14]{0:T(128)S(1)}, f32[14]{0:T(128)}, u32[]{:S(2)}) copy-start(f32[14]{0:T(128)} %param.32) | copy-start | bytes 172
  9.7 10.1 %copy-start.3 = (bf16[512,896]{1,0:T(8,128)(2,1)S(1)}, bf16[512,896]{1,0:T(8,128)(2,1)}, u32[]{:S(2)}) copy-start(bf16[512,896]{1,0:T(8,128)(2,1)} %x_ref.3) | copy-start | bytes 2752516
  9.7 10.1 %copy-start.14 = (bf16[512,128]{1,0:T(8,128)(2,1)S(1)}, bf16[512,128]{1,0:T(8,128)(2,1)}, u32[]{:S(2)}) copy-start(bf16[512,128]{1,0:T(8,128)(2,1)} %b_ref.3) | copy-start | bytes 393220
  9.8 10.1 %copy-start.17 = (f32[512,14]{0,1:T(8,128)S(1)}, f32[512,14]{0,1:T(8,128)}, u32[]{:S(2)}) copy-start(f32[512,14]{0,1:T(8,128)} %param.31) | copy-start | bytes 86020
  10.9 40.3 %collective-permute-start.2 = (bf16[912,512]{1,0:T(8,128)(2,1)}, bf16[912,512]{1,0:T(8,128)(2,1)}, u32[]{:S(2)}, u32[]{:S(2)}) collective-permute-start(bf16[912,512]{1,0:T(8,128)(2,1)} %pad_maximum_fusion.1), channel_id=1, source_target_pairs={{0,8},{8,16},{16,24},{24,32},{32,40},{40,48},{48,56},{56,64},{64,7... | collective-permute-start | bytes 2801672 | tf_op jit(solution)/shard_map/ppermute | solution.py:457
  14.4 11.8 %copy-start.25 = (f32[14]{0:T(128)S(1)}, f32[14]{0:T(128)}, u32[]{:S(2)}) copy-start(f32[14]{0:T(128)} %param.33) | copy-start | bytes 172
  14.4 12.0 %copy-start.15 = (bf16[512,128]{1,0:T(8,128)(2,1)S(1)}, bf16[512,128]{1,0:T(8,128)(2,1)}, u32[]{:S(2)}) copy-start(bf16[512,128]{1,0:T(8,128)(2,1)} %c_ref.3) | copy-start | bytes 393220
  15.2 22.7 %collective-permute-start.1 = (bf16[464,512]{1,0:T(8,128)(2,1)}, bf16[464,512]{1,0:T(8,128)(2,1)}, u32[]{:S(2)}, u32[]{:S(2)}) collective-permute-start(bf16[464,512]{1,0:T(8,128)(2,1)} %pad_maximum_fusion.2), channel_id=1, source_target_pairs={{8,0},{16,8},{24,16},{32,24},{40,32},{48,40},{56,48},{64,56},{72,6... | collective-permute-start | bytes 1425416 | tf_op jit(solution)/shard_map/ppermute | solution.py:457
  21.9 34.2 %collective-permute-start = (bf16[80,896]{1,0:T(8,128)(2,1)S(1)}, bf16[80,896]{1,0:T(8,128)(2,1)S(1)}, u32[]{:S(2)}, u32[]{:S(2)}) collective-permute-start(bf16[80,896]{1,0:T(8,128)(2,1)S(1)} %get-tuple-element.46.state_ref), channel_id=1, source_target_pairs={{0,8},{8,16},{16,24},{24,32},{32,40},{40,48},{48,56},{56,64},{64,7... | collective-permute-start | bytes 430088 | tf_op jit(solution)/shard_map/ppermute | solution.py:457
  31.6 35.3 %copy-start.13 = (bf16[512,896]{1,0:T(8,128)(2,1)S(1)}, bf16[512,896]{1,0:T(8,128)(2,1)}, u32[]{:S(2)}) copy-start(bf16[512,896]{1,0:T(8,128)(2,1)} %z_ref.1) | copy-start | bytes 2752516
  56.2 20.7 %copy-start.22 = (f32[896]{0:T(1024)S(1)}, f32[896]{0:T(1024)}, u32[]{:S(2)}) copy-start(f32[896]{0:T(1024)} %param.34) | copy-start | bytes 10756
  56.2 10.7 %collective-permute-start.3 = (bf16[80,896]{1,0:T(8,128)(2,1)S(1)}, bf16[80,896]{1,0:T(8,128)(2,1)S(1)}, u32[]{:S(2)}, u32[]{:S(2)}) collective-permute-start(bf16[80,896]{1,0:T(8,128)(2,1)S(1)} %pass_through.1), channel_id=1, source_target_pairs={{0,8},{8,16},{16,24},{24,32},{32,40},{40,48},{48,56},{56,64},{64,7... | collective-permute-start | bytes 430088 | tf_op jit(solution)/shard_map/ppermute | solution.py:457
  58.1 24.7 %collective-permute-start.8 = (bf16[464,512]{1,0:T(8,128)(2,1)}, bf16[464,512]{1,0:T(8,128)(2,1)}, u32[]{:S(2)}, u32[]{:S(2)}) collective-permute-start(bf16[464,512]{1,0:T(8,128)(2,1)} %attend_next.1), channel_id=1, source_target_pairs={{0,8},{8,16},{16,24},{24,32},{32,40},{40,48},{48,56},{56,64},{64,7... | collective-permute-start | bytes 1425416 | tf_op jit(solution)/shard_map/ppermute | solution.py:457
  71.1 1.2 collective-permute-start.4
  72.3 4.6 %collective-permute-start.7 = (f32[2,512]{1,0:T(2,128)S(1)}, f32[2,512]{1,0:T(2,128)S(1)}, u32[]{:S(2)}, u32[]{:S(2)}) collective-permute-start(f32[2,512]{1,0:T(2,128)S(1)} %add.137), channel_id=1, source_target_pairs={{0,6},{2,0},{4,2},{6,4},{1,7},{3,1},{5,3},{7,5},{8,14},{10,8},{12,... | collective-permute-start | bytes 12296 | tf_op jit(solution)/shard_map/ppermute | solution.py:462
  75.1 5.1 %collective-permute-start.6 = (f32[2,512]{1,0:T(2,128)S(1)}, f32[2,512]{1,0:T(2,128)S(1)}, u32[]{:S(2)}, u32[]{:S(2)}) collective-permute-start(f32[2,512]{1,0:T(2,128)S(1)} %add.137), channel_id=1, source_target_pairs={{0,4},{2,6},{4,0},{6,2},{1,5},{3,7},{5,1},{7,3},{8,12},{10,14},{12... | collective-permute-start | bytes 12296 | tf_op jit(solution)/shard_map/ppermute | solution.py:462
  75.9 4.8 %collective-permute-start.5 = (f32[2,512]{1,0:T(2,128)S(1)}, f32[2,512]{1,0:T(2,128)S(1)}, u32[]{:S(2)}, u32[]{:S(2)}) collective-permute-start(f32[2,512]{1,0:T(2,128)S(1)} %add.137), channel_id=1, source_target_pairs={{0,2},{2,4},{4,6},{6,0},{1,3},{3,5},{5,7},{7,1},{8,10},{10,12},{12... | collective-permute-start | bytes 12296 | tf_op jit(solution)/shard_map/ppermute | solution.py:462
  89.9 5.2 %collective-permute-start.11 = (bf16[448,512]{1,0:T(8,128)(2,1)}, bf16[448,512]{1,0:T(8,128)(2,1)}, u32[]{:S(2)}, u32[]{:S(2)}) collective-permute-start(bf16[448,512]{1,0:T(8,128)(2,1)} %get-tuple-element.56), channel_id=1, source_target_pairs={{0,1},{1,0},{2,3},{3,2},{4,5},{5,4},{6,7},{7,6},{8,9},{9,8},{10,11... | collective-permute-start | bytes 1376264 | tf_op jit(solution)/shard_map/ppermute | solution.py:466
  90.0 5.1 %copy-start.12 = (f32[448,512]{1,0:T(8,128)S(1)}, f32[448,512]{1,0:T(8,128)}, u32[]{:S(2)}) copy-start(f32[448,512]{1,0:T(8,128)} %copy-done.11) | copy-start | bytes 2752516
  94.6 8.1 %collective-permute-start.9 = (bf16[448,512]{1,0:T(8,128)(2,1)}, bf16[448,512]{1,0:T(8,128)(2,1)}, u32[]{:S(2)}, u32[]{:S(2)}) collective-permute-start(bf16[448,512]{1,0:T(8,128)(2,1)} %get-tuple-element.54), channel_id=1, source_target_pairs={{0,1},{1,0},{2,3},{3,2},{4,5},{5,4},{6,7},{7,6},{8,9},{9,8},{10,11... | collective-permute-start | bytes 1376264 | tf_op jit(solution)/shard_map/ppermute | solution.py:466
  102.6 4.1 %collective-permute-start.13 = (bf16[448,512]{1,0:T(8,128)(2,1)}, bf16[448,512]{1,0:T(8,128)(2,1)}, u32[]{:S(2)}, u32[]{:S(2)}) collective-permute-start(bf16[448,512]{1,0:T(8,128)(2,1)} %get-tuple-element.59), channel_id=1, source_target_pairs={{0,1},{1,0},{2,3},{3,2},{4,5},{5,4},{6,7},{7,6},{8,9},{9,8},{10,11... | collective-permute-start | bytes 1376264 | tf_op jit(solution)/shard_map/ppermute | solution.py:466
  102.7 24.3 %collective-permute-start.12 = (bf16[448,512]{1,0:T(8,128)(2,1)}, bf16[448,512]{1,0:T(8,128)(2,1)}, u32[]{:S(2)}, u32[]{:S(2)}) collective-permute-start(bf16[448,512]{1,0:T(8,128)(2,1)} %add_convert_fusion.5), channel_id=1, source_target_pairs={{0,2},{2,4},{4,6},{6,0},{1,3},{3,5},{5,7},{7,1},{8,10},{10,12},{12... | collective-permute-start | bytes 1376264 | tf_op jit(solution)/shard_map/ppermute | solution.py:462
  104.7 22.2 %collective-permute-start.10 = (bf16[448,512]{1,0:T(8,128)(2,1)}, bf16[448,512]{1,0:T(8,128)(2,1)}, u32[]{:S(2)}, u32[]{:S(2)}) collective-permute-start(bf16[448,512]{1,0:T(8,128)(2,1)} %add_convert_fusion.6), channel_id=1, source_target_pairs={{0,4},{2,6},{4,0},{6,2},{1,5},{3,7},{5,1},{7,3},{8,12},{10,14},{12... | collective-permute-start | bytes 1376264 | tf_op jit(solution)/shard_map/ppermute | solution.py:462
  108.6 6.9 %copy-start.21 = (f32[3584]{0:T(1024)S(1)}, f32[3584]{0:T(1024)}, u32[]{:S(2)}) copy-start(f32[3584]{0:T(1024)} %param.37) | copy-start | bytes 43012
  113.2 13.8 %collective-permute-start.15 = (bf16[448,512]{1,0:T(8,128)(2,1)}, bf16[448,512]{1,0:T(8,128)(2,1)S(1)}, u32[]{:S(2)}, u32[]{:S(2)}) collective-permute-start(bf16[448,512]{1,0:T(8,128)(2,1)} %get-tuple-element.62), channel_id=1, source_target_pairs={{0,1},{1,0},{2,3},{3,2},{4,5},{5,4},{6,7},{7,6},{8,9},{9,8},{10,11... | collective-permute-start | bytes 1376264 | tf_op jit(solution)/shard_map/ppermute | solution.py:466
  113.3 16.1 %collective-permute-start.14 = (bf16[448,512]{1,0:T(8,128)(2,1)}, bf16[448,512]{1,0:T(8,128)(2,1)S(1)}, u32[]{:S(2)}, u32[]{:S(2)}) collective-permute-start(bf16[448,512]{1,0:T(8,128)(2,1)} %add_convert_fusion.4), channel_id=1, source_target_pairs={{0,6},{2,0},{4,2},{6,4},{1,7},{3,1},{5,3},{7,5},{8,14},{10,8},{12,... | collective-permute-start | bytes 1376264 | tf_op jit(solution)/shard_map/ppermute | solution.py:462
  132.0 13.5 %collective-permute-start.17 = (bf16[448,512]{1,0:T(8,128)(2,1)S(1)}, bf16[448,512]{1,0:T(8,128)(2,1)S(1)}, u32[]{:S(2)}, u32[]{:S(2)}) collective-permute-start(bf16[448,512]{1,0:T(8,128)(2,1)S(1)} %get-tuple-element.89.refs_0_), channel_id=1, source_target_pairs={{0,2},{2,4},{4,6},{6,0},{1,3},{3,5},{5,7},{7,1},{8,10},{10,12},{12... | collective-permute-start | bytes 1376264 | tf_op jit(solution)/shard_map/ppermute | solution.py:462
  132.9 23.6 %collective-permute-start.19 = (bf16[448,512]{1,0:T(8,128)(2,1)S(1)}, bf16[448,512]{1,0:T(8,128)(2,1)S(1)}, u32[]{:S(2)}, u32[]{:S(2)}) collective-permute-start(bf16[448,512]{1,0:T(8,128)(2,1)S(1)} %get-tuple-element.89.refs_0_), channel_id=1, source_target_pairs={{0,4},{2,6},{4,0},{6,2},{1,5},{3,7},{5,1},{7,3},{8,12},{10,14},{12... | collective-permute-start | bytes 1376264 | tf_op jit(solution)/shard_map/ppermute | solution.py:462
  136.1 20.4 %collective-permute-start.21 = (bf16[448,512]{1,0:T(8,128)(2,1)S(1)}, bf16[448,512]{1,0:T(8,128)(2,1)S(1)}, u32[]{:S(2)}, u32[]{:S(2)}) collective-permute-start(bf16[448,512]{1,0:T(8,128)(2,1)S(1)} %get-tuple-element.89.refs_0_), channel_id=1, source_target_pairs={{0,6},{2,0},{4,2},{6,4},{1,7},{3,1},{5,3},{7,5},{8,14},{10,8},{12,... | collective-permute-start | bytes 1376264 | tf_op jit(solution)/shard_map/ppermute | solution.py:462
  136.2 20.8 %collective-permute-start.16 = (bf16[448,512]{1,0:T(8,128)(2,1)S(1)}, bf16[448,512]{1,0:T(8,128)(2,1)S(1)}, u32[]{:S(2)}, u32[]{:S(2)}) collective-permute-start(bf16[448,512]{1,0:T(8,128)(2,1)S(1)} %get-tuple-element.89.refs_0_), channel_id=1, source_target_pairs={{0,1},{1,0},{2,3},{3,2},{4,5},{5,4},{6,7},{7,6},{8,9},{9,8},{10,11... | collective-permute-start | bytes 1376264 | tf_op jit(solution)/shard_map/ppermute | solution.py:466
  145.5 11.6 %collective-permute-start.18 = (bf16[448,512]{1,0:T(8,128)(2,1)S(1)}, bf16[448,512]{1,0:T(8,128)(2,1)}, u32[]{:S(2)}, u32[]{:S(2)}) collective-permute-start(bf16[448,512]{1,0:T(8,128)(2,1)S(1)} %collective-permute-done.17.refs_2_), channel_id=1, source_target_pairs={{0,1},{1,0},{2,3},{3,2},{4,5},{5,4},{6,7},{7,6},{8,9},{9,8},{10,11... | collective-permute-start | bytes 1376264 | tf_op jit(solution)/shard_map/ppermute | solution.py:466
  156.5 1.9 collective-permute-start.20
  156.5 2.6 %collective-permute-start.22 = (bf16[448,512]{1,0:T(8,128)(2,1)S(1)}, bf16[448,512]{1,0:T(8,128)(2,1)}, u32[]{:S(2)}, u32[]{:S(2)}) collective-permute-start(bf16[448,512]{1,0:T(8,128)(2,1)S(1)} %collective-permute-done.21.refs_6_), channel_id=1, source_target_pairs={{0,1},{1,0},{2,3},{3,2},{4,5},{5,4},{6,7},{7,6},{8,9},{9,8},{10,11... | collective-permute-start | bytes 1376264 | tf_op jit(solution)/shard_map/ppermute | solution.py:466
  178.7 4.0 %collective-permute-start.25 = (bf16[448,512]{1,0:T(8,128)(2,1)S(1)}, bf16[448,512]{1,0:T(8,128)(2,1)S(1)}, u32[]{:S(2)}, u32[]{:S(2)}) collective-permute-start(bf16[448,512]{1,0:T(8,128)(2,1)S(1)} %get-tuple-element.68), channel_id=1, source_target_pairs={{0,1},{1,0},{2,3},{3,2},{4,5},{5,4},{6,7},{7,6},{8,9},{9,8},{10,11... | collective-permute-start | bytes 1376264 | tf_op jit(solution)/shard_map/ppermute | solution.py:466
  182.2 4.7 %collective-permute-start.23 = (bf16[448,512]{1,0:T(8,128)(2,1)S(1)}, bf16[448,512]{1,0:T(8,128)(2,1)S(1)}, u32[]{:S(2)}, u32[]{:S(2)}) collective-permute-start(bf16[448,512]{1,0:T(8,128)(2,1)S(1)} %get-tuple-element.66), channel_id=1, source_target_pairs={{0,1},{1,0},{2,3},{3,2},{4,5},{5,4},{6,7},{7,6},{8,9},{9,8},{10,11... | collective-permute-start | bytes 1376264 | tf_op jit(solution)/shard_map/ppermute | solution.py:466
  186.7 4.1 %collective-permute-start.27 = (bf16[448,512]{1,0:T(8,128)(2,1)S(1)}, bf16[448,512]{1,0:T(8,128)(2,1)S(1)}, u32[]{:S(2)}, u32[]{:S(2)}) collective-permute-start(bf16[448,512]{1,0:T(8,128)(2,1)S(1)} %get-tuple-element.71), channel_id=1, source_target_pairs={{0,1},{1,0},{2,3},{3,2},{4,5},{5,4},{6,7},{7,6},{8,9},{9,8},{10,11... | collective-permute-start | bytes 1376264 | tf_op jit(solution)/shard_map/ppermute | solution.py:466
  187.0 24.2 %collective-permute-start.26 = (bf16[448,512]{1,0:T(8,128)(2,1)}, bf16[448,512]{1,0:T(8,128)(2,1)}, u32[]{:S(2)}, u32[]{:S(2)}) collective-permute-start(bf16[448,512]{1,0:T(8,128)(2,1)} %add_convert_fusion.2), channel_id=1, source_target_pairs={{0,2},{2,4},{4,6},{6,0},{1,3},{3,5},{5,7},{7,1},{8,10},{10,12},{12... | collective-permute-start | bytes 1376264 | tf_op jit(solution)/shard_map/ppermute | solution.py:462
  187.9 23.2 %collective-permute-start.24 = (bf16[448,512]{1,0:T(8,128)(2,1)}, bf16[448,512]{1,0:T(8,128)(2,1)}, u32[]{:S(2)}, u32[]{:S(2)}) collective-permute-start(bf16[448,512]{1,0:T(8,128)(2,1)} %add_convert_fusion.3), channel_id=1, source_target_pairs={{0,4},{2,6},{4,0},{6,2},{1,5},{3,7},{5,1},{7,3},{8,12},{10,14},{12... | collective-permute-start | bytes 1376264 | tf_op jit(solution)/shard_map/ppermute | solution.py:462
  194.9 16.3 %collective-permute-start.29 = (bf16[448,512]{1,0:T(8,128)(2,1)S(1)}, bf16[448,512]{1,0:T(8,128)(2,1)}, u32[]{:S(2)}, u32[]{:S(2)}) collective-permute-start(bf16[448,512]{1,0:T(8,128)(2,1)S(1)} %get-tuple-element.74), channel_id=1, source_target_pairs={{0,1},{1,0},{2,3},{3,2},{4,5},{5,4},{6,7},{7,6},{8,9},{9,8},{10,11... | collective-permute-start | bytes 1376264 | tf_op jit(solution)/shard_map/ppermute | solution.py:466
  194.9 17.7 %collective-permute-start.28 = (bf16[448,512]{1,0:T(8,128)(2,1)}, bf16[448,512]{1,0:T(8,128)(2,1)}, u32[]{:S(2)}, u32[]{:S(2)}) collective-permute-start(bf16[448,512]{1,0:T(8,128)(2,1)} %add_convert_fusion.1), channel_id=1, source_target_pairs={{0,6},{2,0},{4,2},{6,4},{1,7},{3,1},{5,3},{7,5},{8,14},{10,8},{12,... | collective-permute-start | bytes 1376264 | tf_op jit(solution)/shard_map/ppermute | solution.py:462
  196.2 16.5 %copy-start.18 = (f32[448,512]{1,0:T(8,128)S(1)}, f32[448,512]{1,0:T(8,128)}, u32[]{:S(2)}) copy-start(f32[448,512]{1,0:T(8,128)} %get-tuple-element.90) | copy-start | bytes 2752516
  212.7 6.7 %copy-start.26 = (s32[1,32]{1,0:T(1,128)S(1)}, s32[1,32]{1,0:T(1,128)}, u32[]{:S(2)}) copy-start(s32[1,32]{1,0:T(1,128)} %param.26) | copy-start | bytes 388
  214.6 9.9 %copy-start.19 = (bf16[448,512]{1,0:T(8,128)(2,1)}, bf16[448,512]{1,0:T(8,128)(2,1)S(1)}, u32[]{:S(2)}) copy-start(bf16[448,512]{1,0:T(8,128)(2,1)S(1)} %get-tuple-element.88) | copy-start | bytes 1376260
  214.6 1.2 collective-permute-start.30
  215.9 8.6 %collective-permute-start.33 = (f32[1,512]{1,0:T(1,128)S(1)}, f32[1,512]{1,0:T(1,128)S(1)}, u32[]{:S(2)}, u32[]{:S(2)}) collective-permute-start(f32[1,512]{1,0:T(1,128)S(1)} %add.164), channel_id=1, source_target_pairs={{0,6},{2,0},{4,2},{6,4},{1,7},{3,1},{5,3},{7,5},{8,14},{10,8},{12,... | collective-permute-start | bytes 6152 | tf_op jit(solution)/shard_map/ppermute | solution.py:462
  218.5 6.0 %collective-permute-start.32 = (f32[1,512]{1,0:T(1,128)S(1)}, f32[1,512]{1,0:T(1,128)S(1)}, u32[]{:S(2)}, u32[]{:S(2)}) collective-permute-start(f32[1,512]{1,0:T(1,128)S(1)} %add.164), channel_id=1, source_target_pairs={{0,4},{2,6},{4,0},{6,2},{1,5},{3,7},{5,1},{7,3},{8,12},{10,14},{12... | collective-permute-start | bytes 6152 | tf_op jit(solution)/shard_map/ppermute | solution.py:462
  218.5 6.0 %collective-permute-start.31 = (f32[1,512]{1,0:T(1,128)S(1)}, f32[1,512]{1,0:T(1,128)S(1)}, u32[]{:S(2)}, u32[]{:S(2)}) collective-permute-start(f32[1,512]{1,0:T(1,128)S(1)} %add.164), channel_id=1, source_target_pairs={{0,2},{2,4},{4,6},{6,0},{1,3},{3,5},{5,7},{7,1},{8,10},{10,12},{12... | collective-permute-start | bytes 6152 | tf_op jit(solution)/shard_map/ppermute | solution.py:462
  (14 other events, 31.0 us)
Sparse Core Ops, SparseCore 0:
  10.2 140.9 all-gather.2

commit v3 on v2

--- a/solution.py
+++ b/solution.py
@@ -1,3 +1,4 @@
+import functools
 import math
 
 import jax
@@ -316,49 +317,88 @@
     )(out, lse, far)
 
 
-def project_kernel(place_ref, att_ref, mam_ref, wa_ref, wm_ref, own_ref, other_ref):
-    half = own_ref.shape[0]
+ORDER = (2, 1, 3, 0)
+
+
+def send_out(step, refs, own_s, other_s, sems):
+    for k in range(len(ORDER)):
+        pair = (
+            pltpu.make_async_copy(own_s.at[k], refs[2 * k], sems.at[0, k]),
+            pltpu.make_async_copy(other_s.at[k], refs[2 * k + 1], sems.at[1, k]),
+        )
+
+        @pl.when(step == k)
+        def _(pair=pair):
+            for copy in pair:
+                copy.start()
+
+    @pl.when(step == len(ORDER) - 1)
+    def _():
+        for k in range(len(ORDER)):
+            pltpu.make_async_copy(own_s.at[k], refs[2 * k], sems.at[0, k]).wait()
+            pltpu.make_async_copy(other_s.at[k], refs[2 * k + 1], sems.at[1, k]).wait()
+
+
+def block_outputs(rows):
+    count = len(ORDER)
+    raw = pl.BlockSpec(memory_space=pl.ANY)
+    pair = [jax.ShapeDtypeStruct((rows, T), F32), jax.ShapeDtypeStruct((rows, T), BF16)]
+    scratch = [
+        pltpu.VMEM((count, rows, T), F32),
+        pltpu.VMEM((count, rows, T), BF16),
+        pltpu.SemaphoreType.DMA((2, count)),
+    ]
+    return pair * count, [raw] * (2 * count), scratch
+
+
+def project_kernel(place_ref, att_ref, mam_ref, wa_ref, wm_ref, *refs):
+    outs, (own_s, other_s, sems) = refs[:-3], refs[-3:]
+    step = pl.program_id(0)
+    half = own_s.shape[1]
     out = dot(wa_ref[...], att_ref[...], 0, 0) + dot(wm_ref[...], mam_ref[...], 0, 0)
-    first = place_ref[1] == 0
-    own_ref[...] = jnp.where(first, out[0:half], out[half:])
-    other_ref[...] = jnp.where(first, out[half:], out[0:half]).astype(BF16)
+    first = place_ref[len(ORDER)] == 0
+    own_s[step] = jnp.where(first, out[0:half], out[half:])
+    other_s[step] = jnp.where(first, out[half:], out[0:half]).astype(BF16)
+    send_out(step, outs, own_s, other_s, sems)
 
 
 def project(place, att, mam, wa, wm):
     rows = wa.shape[0]
     once = pl.Buffered(1)
-    block = pl.BlockSpec((rows, T), lambda s, p: (0, 0), pipeline_mode=once)
+    shapes, specs, scratch = block_outputs(rows)
     return pl.pallas_call(
         project_kernel,
         grid_spec=pltpu.PrefetchScalarGridSpec(
             num_scalar_prefetch=1,
-            grid=(1,),
+            grid=(len(ORDER),),
             in_specs=[
                 pl.BlockSpec(att.shape, lambda s, p: (0, 0), pipeline_mode=once),
                 pl.BlockSpec(mam.shape, lambda s, p: (0, 0), pipeline_mode=once),
-                pl.BlockSpec((rows, 2 * rows), lambda s, p: (0, p[0]), pipeline_mode=once),
-                pl.BlockSpec((wm.shape[0], 2 * rows), lambda s, p: (0, p[0]), pipeline_mode=once),
+                pl.BlockSpec((rows, 2 * rows), lambda s, p: (0, p[s])),
+                pl.BlockSpec((wm.shape[0], 2 * rows), lambda s, p: (0, p[s])),
             ],
-            out_specs=(block, block),
+            out_specs=specs,
+            scratch_shapes=scratch,
         ),
-        out_shape=(
-            jax.ShapeDtypeStruct((rows, T), F32), jax.ShapeDtypeStruct((rows, T), BF16)
-        ),
-        compiler_params=vmem(12),
+        out_shape=shapes,
+        compiler_params=vmem(20),
         name="project",
     )(place, att, mam, wa, wm)
 
 
 def prepare_kernel(place_ref, *refs):
     z_refs, unscale_ref, rows_ref, inv_ref = refs[:-3], refs[-3], refs[-2], refs[-1]
-    chips = len(z_refs) // 2
-    pair = unscale_ref.shape[1]
+    chips, pair = unscale_ref.shape
+    mine = [ref[...] for ref in z_refs[0::2]]
+    theirs = [ref[...] for ref in z_refs[1::2]]
+    mine, theirs = (
+        [b[0], b[1], jnp.concatenate([b[2], b[3]], axis=0), b[4]] for b in (mine, theirs)
+    )
     first = place_ref[1] == 0
     total = jnp.zeros((T, 128), F32)
     for d in range(chips):
-        mine, theirs = z_refs[2 * d][...], z_refs[2 * d + 1][...]
         both = jnp.concatenate(
-            [jnp.where(first, mine, theirs), jnp.where(first, theirs, mine)], axis=0
+            [jnp.where(first, mine[d], theirs[d]), jnp.where(first, theirs[d], mine[d])], axis=0
         ).T
         chip = lax.rem(place_ref[0] + chips - d, chips)
         rows_ref[:, pl.ds(pl.multiple_of(chip * pair, 128), pair)] = both
@@ -385,70 +425,117 @@
     )(place, *blocks, unscale)
 
 
-def activate_kernel(rows_ref, inv_ref, gu_ref, act_ref):
-    width = rows_ref.shape[1]
-    w = jnp.concatenate(
-        [gu_ref[:, 0].reshape(width, 128), gu_ref[:, 1].reshape(width, 128)], axis=1
-    )
-    both = dot(rows_ref[...], w)
-    gate = both[:, 0:128] * inv_ref[...]
-    up = both[:, 128:256] * inv_ref[...]
-    act_ref[...] = (gate / (1.0 + jnp.exp(-gate)) * up).astype(BF16)
-
-
-def activate(rows, inv, weights):
+def mlp_kernel(place_ref, rows_ref, inv_ref, gu_ref, down_ref, *refs):
+    outs, (act_s, own_s, other_s, sems) = refs[:-4], refs[-4:]
+    half, hidden = own_s.shape[1], act_s.shape[1]
+    first = hidden // 128
+    step = pl.program_id(0)
+
+    @pl.when(step < first)
+    def _():
+        width = rows_ref.shape[1]
+        w = jnp.concatenate(
+            [gu_ref[:, 0].reshape(width, 128), gu_ref[:, 1].reshape(width, 128)], axis=1
+        )
+        both = dot(rows_ref[...], w)
+        gate = both[:, 0:128] * inv_ref[...]
+        up = both[:, 128:256] * inv_ref[...]
+        act_s[:, pl.ds(pl.multiple_of(step * 128, 128), 128)] = (
+            gate / (1.0 + jnp.exp(-gate)) * up
+        ).astype(BF16)
+
+    @pl.when(step >= first)
+    def _():
+        k = step - first
+        out = dot(down_ref[:, 0].reshape(2 * half, hidden), act_s[...], 1, 1)
+        lower = place_ref[len(ORDER)] == 0
+        own_s[k] = jnp.where(lower, out[0:half], out[half:])
+        other_s[k] = jnp.where(lower, out[half:], out[0:half]).astype(BF16)
+
+    send_out(step - first, outs, own_s, other_s, sems)
+
+
+def mlp(place, rows, inv, weights):
     parts, _, height, hidden = weights.shape
     once = pl.Buffered(1)
-    return pl.pallas_call(
-        activate_kernel,
-        grid=(hidden // 128,),
-        in_specs=[
-            pl.BlockSpec(rows.shape, lambda s: (0, 0), pipeline_mode=once),
-            pl.BlockSpec(inv.shape, lambda s: (0, 0), pipeline_mode=once),
-            pl.BlockSpec((parts, 2, height, 128), lambda s: (0, 0, 0, s)),
-        ],
-        out_specs=pl.BlockSpec((T, 128), lambda s: (0, s)),
-        out_shape=jax.ShapeDtypeStruct((T, hidden), BF16),
-        compiler_params=vmem(16),
-        name="activate",
-    )(rows, inv, weights)
-
-
-def down_kernel(place_ref, act_ref, w_ref, own_ref, other_ref):
-    half, hidden = own_ref.shape[0], act_ref.shape[1]
-    per = w_ref.shape[0] // 2
-    act = act_ref[...]
-    c = place_ref[1]
-    theirs = w_ref[pl.ds(per * (1 - c), per), 0].reshape(half, hidden)
-    other_ref[...] = dot(theirs, act, 1, 1).astype(BF16)
-    mine = w_ref[pl.ds(per * c, per), 0].reshape(half, hidden)
-    own_ref[...] = dot(mine, act, 1, 1)
-
-
-def down(place, act, weights):
-    parts, _, height, hidden = weights.shape
-    per = parts // 4
-    rows = per * height // 2
-    return pl.pallas_call(
-        down_kernel,
+    first = hidden // 128
+    count = len(ORDER)
+    per = parts // count
+    shapes, specs, scratch = block_outputs(per * height // 2)
+    return pl.pallas_call(
+        mlp_kernel,
         grid_spec=pltpu.PrefetchScalarGridSpec(
             num_scalar_prefetch=1,
-            grid=(1,),
+            grid=(first + count,),
             in_specs=[
-                pl.BlockSpec(act.shape, lambda s, p: (0, 0)),
-                pl.BlockSpec((per, 1, height, hidden), lambda s, p: (p[0], 2, 0, 0)),
+                pl.BlockSpec(rows.shape, lambda s, p: (0, 0), pipeline_mode=once),
+                pl.BlockSpec(inv.shape, lambda s, p: (0, 0), pipeline_mode=once),
+                pl.BlockSpec(
+                    (parts, 2, height, 128), lambda s, p: (0, 0, 0, jnp.minimum(s, first - 1))
+                ),
+                pl.BlockSpec(
+                    (per, 1, height, hidden), lambda s, p: (p[jnp.maximum(s - first, 0)], 2, 0, 0)
+                ),
             ],
-            out_specs=(
-                pl.BlockSpec((rows, T), lambda s, p: (0, 0)),
-                pl.BlockSpec((rows, T), lambda s, p: (0, 0)),
-            ),
+            out_specs=specs,
+            scratch_shapes=[pltpu.VMEM((T, hidden), BF16), *scratch],
         ),
-        out_shape=(
-            jax.ShapeDtypeStruct((rows, T), F32), jax.ShapeDtypeStruct((rows, T), BF16)
-        ),
-        compiler_params=vmem(14),
-        name="down",
-    )(place, act, weights)
+        out_shape=shapes,
+        compiler_params=vmem(26),
+        name="mlp",
+    )(place, rows, inv, weights, weights)
+
+
+def pages_kernel(table_ref, k_ref, v_ref, out_ref):
+    pages = out_ref.shape[2]
+    row = lax.broadcasted_iota(jnp.int32, (T, T), 0)
+    chosen = (table_ref[...] == lax.rem(row, pages)) & (
+        lax.rem(lanes_of((T, T)), PAGE) == row // pages
+    )
+    chosen = jnp.where(chosen, 1.0, 0.0).astype(BF16)
+    for i, ref in enumerate((k_ref, v_ref)):
+        for h in range(ref.shape[0] // HD):
+            tokens = dot(chosen, ref[HD * h : HD * h + HD, :], 1, 1).astype(BF16)
+            for j in range(PAGE):
+                out_ref[i, h, :, HD * j : HD * j + HD] = tokens[pages * j : pages * j + pages]
+
+
+def cache_pages(table, k, v):
+    heads, pages = k.shape[0] // HD, table.shape[1]
+    return pl.pallas_call(
+        pages_kernel,
+        out_shape=jax.ShapeDtypeStruct((2, heads, pages, PAGE * HD), BF16),
+        compiler_params=vmem(10),
+        name="cache_pages",
+    )(jnp.repeat(table, PAGE, axis=1), k, v)
+
+
+def stack_kernel(a_ref, b_ref, c_ref, out_ref, held_ref, sems):
+    refs = (a_ref, b_ref, c_ref)
+    loads = [pltpu.make_async_copy(r, held_ref.at[i], sems.at[0, i]) for i, r in enumerate(refs)]
+    saves = [
+        pltpu.make_async_copy(held_ref.at[i], out_ref.at[i], sems.at[1, i]) for i in range(len(refs))
+    ]
+    for load in loads:
+        load.start()
+    for load, save in zip(loads, saves):
+        load.wait()
+        save.start()
+    for save in saves:
+        save.wait()
+
+
+def stack_three(a, b, c):
+    raw = pl.BlockSpec(memory_space=pl.ANY)
+    return pl.pallas_call(
+        stack_kernel,
+        in_specs=[raw, raw, raw],
+        out_specs=raw,
+        out_shape=jax.ShapeDtypeStruct((3, *a.shape), a.dtype),
+        scratch_shapes=[pltpu.VMEM((3, *a.shape), a.dtype), pltpu.SemaphoreType.DMA((2, 3))],
+        compiler_params=vmem(4),
+        name="stack_three",
+    )(in_hbm(a), in_hbm(b), in_hbm(c))
 
 
 def behind(value, steps):
@@ -466,38 +553,57 @@
     return lax.ppermute(value, "c", [(0, 1), (1, 0)])
 
 
-ORDER = (2, 1, 3, 0)
-
-
-def scatter_sum(block_of, source):
-    sent, waiting = [], []
-
-    def send(s, own, other):
-        paired = own + other.astype(F32)
-        if not s:
-            sent.append(paired)
-            return paired
-        narrow = paired.astype(BF16)
-        sent.append(along(narrow, s).astype(F32))
-        return narrow
-
-    for s in ORDER:
-        own, other = block_of(s, source)
-        waiting.append((s, own, swap(other)))
-        if s in (1, 3):
-            done = [send(*item) for item in waiting][-1]
-            source, _ = lax.optimization_barrier((source, done))
-            waiting = []
-    for item in waiting:
-        send(*item)
-    return sent[0] + sent[1] + sent[2] + sent[3]
+def add_kernel(own_ref, other_ref, *refs, top):
+    out_ref = refs[-1]
+    half = out_ref.shape[0] // 2
+    total = own_ref[...] + other_ref[...].astype(F32)
+    first, second = total[0:half], total[half:]
+    extra = refs[0][...].astype(F32)
+    out_ref[0:half, :] = (first + extra if top else first).astype(BF16)
+    out_ref[half:, :] = (second if top else second + extra).astype(BF16)
+
+
+def add_up(own, other, extra, top):
+    return pl.pallas_call(
+        functools.partial(add_kernel, top=top),
+        out_shape=jax.ShapeDtypeStruct(own.shape, BF16),
+        compiler_params=vmem(6),
+        name="add_up",
+    )(own, other, extra)
+
+
+def halves_kernel(own_ref, other_ref, first_ref, second_ref):
+    half = first_ref.shape[0]
+    total = (own_ref[...] + other_ref[...].astype(F32)).astype(BF16)
+    first_ref[...] = total[0:half]
+    second_ref[...] = total[half:]
+
+
+def add_halves(own, other):
+    half = jax.ShapeDtypeStruct((own.shape[0] // 2, own.shape[1]), BF16)
+    return pl.pallas_call(
+        halves_kernel, out_shape=(half, half), compiler_params=vmem(6), name="add_halves"
+    )(own, other)
+
+
+def scatter_sum(blocks, base):
+    own2, other2, own1, other1, own3, other3, own0, other0 = blocks
+    up, low = add_halves(own2, swap(other2))
+    up, low = along(up, 1), along(low, 3)
+    other1, other3, other0 = swap(other1), swap(other3), swap(other0)
+    from_left = along(add_up(own1, other1, up, True), 1)
+    from_right = along(add_up(own3, other3, low, False), 3)
+    base = lax.optimization_barrier(base + own0 + other0.astype(F32))
+    return base + from_left.astype(F32) + from_right.astype(F32)
 
 
 def gather_rows(share):
+    half = share.shape[0] // 2
+    left, right = along(share, 1), along(share, 3)
+    first, second = along(left[:half], 1), along(right[half:], 3)
     got = []
-    for d in range(4):
-        here = along(share, d) if d else share
-        got += [here, swap(here)]
+    for block in (share, left, first, second, right):
+        got += [block, swap(block)]
     return got
 
 
@@ -513,7 +619,6 @@
     mlp_norm_gain, gate_proj, up_proj, down_proj, next_norm_gain,
 ):
     row_count = query_heads.shape[0]
-    head_count = query_heads.shape[1] // HD
     width = hidden.shape[1]
     total_width = mlp_norm_gain.shape[0]
     owner = lax.axis_index("x") * lax.axis_size("c") + lax.axis_index("c")
@@ -521,10 +626,9 @@
     x = lax.axis_index("x")
     core = lax.axis_index("c")
 
-    def place(steps):
-        return jnp.stack([(x + steps) % 4, core]).astype(jnp.int32)
-
-    stacked_weights = jnp.stack([gate_proj, up_proj, down_proj.T])
+    place = jnp.stack([(x + steps) % 4 for steps in ORDER] + [core]).astype(jnp.int32)
+
+    stacked_weights = stack_three(gate_proj, up_proj, down_proj.T)
     weights = in_hbm(lax.all_gather(stacked_weights, REQ, axis=0, tiled=False))
 
     seg_row = segment_ids.reshape(1, row_count)
@@ -540,25 +644,16 @@
     kv1 = behind(jnp.concatenate([k, v, ids], axis=0), 1)
     next_q = behind(jnp.concatenate([q, ids], axis=0), -1)
 
-    page_count = page_table.shape[1]
-
-    def to_pages(source):
-        return (
-            source.reshape(page_count, PAGE, head_count, HD)
-            .transpose(2, 0, 1, 3)
-            .reshape(head_count, page_count, PAGE * HD)
-        )
-
-    stacked = jnp.stack([to_pages(key_heads), to_pages(value_heads)])
-    kv_cache = jnp.zeros_like(stacked).at[:, :, page_table[0]].set(stacked)
-
+    kv_cache = cache_pages(page_table, k, v)
     own_out, own_lse = attend_own(q, k, v, seg_row, seg_col)
     skip = jnp.repeat(skip_gain, mamba_conv_input.shape[1] // skip_gain.shape[0]).reshape(1, -1)
     local = mamba_local(
         mamba_conv_input, state_input_projection, state_output_projection, row, col, seg_row,
         seg_col, skip,
     )
-    waited_col, own_lse, local = lax.optimization_barrier((seg_col, own_lse, local))
+    waited_col, own_lse, local, kv_cache = lax.optimization_barrier(
+        (seg_col, own_lse, local, kv_cache)
+    )
     next_out = attend_next(next_q, k, v, kv1, waited_col)
     far_out = behind(next_out, 1)
     state, near, _ = lax.optimization_barrier((state, near, next_out))
@@ -570,14 +665,14 @@
     own_out, mam = lax.optimization_barrier((own_out, mam))
     att = merge(in_hbm(own_out), own_lse, far_out)
     attn_proj, mamba_output_projection = in_hbm(attn_proj), in_hbm(mamba_output_projection)
-    mixed = hidden.T.astype(F32) + scatter_sum(
-        lambda s, rows: project(place(s), rows, mam, attn_proj, mamba_output_projection), att
+    mixed = scatter_sum(
+        project(place, att, mam, attn_proj, mamba_output_projection), hidden.T.astype(F32)
     )
     own_gain = lax.dynamic_slice_in_dim(mlp_norm_gain, owner * width, width, 0)
     blocks = gather_rows((mixed * own_gain[:, None]).astype(BF16))
-    rows, inv = prepare(place(0), blocks, (1.0 / mlp_norm_gain).reshape(4, -1))
-    act = activate(in_hbm(rows), inv, weights)
-    new_hidden = (mixed + scatter_sum(lambda s, rows: down(place(s), rows, weights), act)).astype(BF16)
+    here = jnp.stack([x, core]).astype(jnp.int32)
+    rows, inv = prepare(here, blocks, (1.0 / mlp_norm_gain).reshape(4, -1))
+    new_hidden = scatter_sum(mlp(place, in_hbm(rows), inv, weights), mixed).astype(BF16)
     widened = new_hidden.astype(F32)
     total_sq = group_sum(jnp.sum(widened * widened, axis=0, keepdims=True))
     next_normed = (

time: 234 us -> 216 us (0.923)
  other arithmetic: 18.9 us -> 7.06 us
  local copies, waits for them, and re-layouts: 18 us -> 6.76 us
  starting transfers between devices: 37.4 us -> 47 us
  Pallas kernels: 62.4 us -> 55.2 us
  waiting for transfers between devices: 81 us -> 84.7 us
    ppermute x15 -> x18, starting transfers between devices: 19.8 us -> 28.8 us  [along(): lax.ppermute(value, 'x', [(i, (i + steps) % count) for i in range(count)])]
    convert_element_type x6 -> x0, other arithmetic: 8.77 us -> none  [send(): narrow = paired.astype(BF16)]
    pallas_call x4 -> x1, Pallas kernels: 18.4 us -> 11.2 us  [project(): pl.pallas_call(project_kernel, grid_spec=pltpu.PrefetchScalarGridSpec(num...]
    ppermute x5, waiting for transfers between devices: 25.3 us -> 29.7 us  [behind(): return lax.ppermute(value, REQ, pairs)]
    unnamed x57 -> x52, local copies, waits for them, and re-layouts: 10.2 us -> 5.85 us
    another operation x3 -> x1, local copies, waits for them, and re-layouts: 3.42 us -> 0.08 us  [body(): jnp.stack([(x + steps) % 4 for steps in ORDER] + [core]).astype(jnp.int32)]
    another operation x5 -> x1, other arithmetic: 2.81 us -> 0.08 us  [body(): here = jnp.stack([x, core]).astype(jnp.int32)]
    add x0 -> x2, other arithmetic: none -> 2.61 us  [scatter_sum(): base = lax.optimization_barrier(base + own0 + other0.astype(F32))]
  transfers between devices with their start and end apart: 35 -> 39, of which waited for: 16 -> 19; matrix products, arithmetic and copies ran while one was open for 10% -> 3% of each run, Pallas kernels for 20% -> 15%
where the time goes in v3:
time: 216 us; the launch traced here: 215 us
  waiting for transfers between devices  84.7 us (39%)
  Pallas kernels  55.2 us (26%)
  starting transfers between devices  47 us (22%)
  between operations  14.6 us (7%)
  other arithmetic  7.06 us (3%)
  local copies, waits for them, and re-layouts  6.76 us (3%)
    ppermute x18, waiting for transfers between devices, along(): lax.ppermute(value, 'x', [(i, (i + steps) % count) for i in range(count)])  50.3 us
    ppermute x5, waiting for transfers between devices, behind(): return lax.ppermute(value, REQ, pairs)  29.7 us
    ppermute x18, starting transfers between devices, along(): lax.ppermute(value, 'x', [(i, (i + steps) % count) for i in range(count)])  28.8 us
    pallas_call x1, Pallas kernels, mlp(): pl.pallas_call(mlp_kernel, grid_spec=pltpu.PrefetchScalarGridSpec(num_sca...  20.1 us
    ppermute x5, starting transfers between devices, behind(): return lax.ppermute(value, REQ, pairs)  15.1 us
    pallas_call x1, Pallas kernels, project(): pl.pallas_call(project_kernel, grid_spec=pltpu.PrefetchScalarGridSpec(num...  11.2 us
    unnamed x52, local copies, waits for them, and re-layouts  5.85 us
    ppermute x15, waiting for transfers between devices, swap(): return lax.ppermute(value, 'c', [(0, 1), (1, 0)])  4.71 us
  transfers between devices with their start and end apart: 39, of which 19 were waited for; matrix products, arithmetic and copies ran while one was open for 3% of the time, Pallas kernels for 15%

profile of v3, /device:TPU:96, one launch (start us, length us, event | category | flops | bytes accessed | tf_op | source)
XLA Modules:
  0.0 215.3 jit_solution(7047746169661080044)
XLA Ops:
  7.2 2.2 %stack_three.1 = bf16[3,224,896]{2,1,0:T(8,128)(2,1)} custom-call(bf16[224,896]{1,0:T(8,128)(2,1)} %a_ref.1, bf16[224,896]{1,0:T(8,128)(2,1)} %b_ref.5, bf16[224,896]{1,0:T(8,128)(2,1)} %bitcast.44), custom_call_target="tpu_custom_call" | custom-call | tf_op jit(solution)/shard_map/stack_three/pallas_call | solution.py:530
  9.6 1.0 pad_maximum_fusion
  10.6 3.5 %collective-permute-start.2 = (bf16[912,512]{1,0:T(8,128)(2,1)}, bf16[912,512]{1,0:T(8,128)(2,1)}, u32[]{:S(2)}, u32[]{:S(2)}) collective-permute-start(bf16[912,512]{1,0:T(8,128)(2,1)} %pad_maximum_fusion), channel_id=1, source_target_pairs={{0,8},{8,16},{16,24},{24,32},{32,40},{40,48},{48,56},{56,64},{64,7... | collective-permute-start | bytes 2801672 | tf_op jit(solution)/shard_map/ppermute | solution.py:544
  14.9 4.5 %collective-permute-start.1 = (bf16[464,512]{1,0:T(8,128)(2,1)}, bf16[464,512]{1,0:T(8,128)(2,1)}, u32[]{:S(2)}, u32[]{:S(2)}) collective-permute-start(bf16[464,512]{1,0:T(8,128)(2,1)} %pad_maximum_fusion.1), channel_id=1, source_target_pairs={{8,0},{16,8},{24,16},{32,24},{40,32},{48,40},{56,48},{64,56},{72,6... | collective-permute-start | bytes 1425416 | tf_op jit(solution)/shard_map/ppermute | solution.py:544
  19.5 2.2 %leaving_state.1 = (bf16[80,896]{1,0:T(8,128)(2,1)S(1)}, f32[16,512]{1,0:T(8,128)S(1)}, f32[512,128]{1,0:T(8,128)S(1)}) custom-call(f32[14,512]{1,0:T(8,128)S(1)} %bitcast.40, f32[14,1]{1,0:T(8,128)S(1)} %copy.31.rate_ref, s32[1,512]{1,0:T(1,128)S(1)} %bitcast.35, bf16[512,896]{1,0:T(8,128)(2,1)S(1)} %copy-done.3, bf16[512,128]{1,0:T(8,128)(2,1)S(1)} %copy-done.8), custom_call_target="tpu_custom_call" | custom-call | tf_op jit(solution)/shard_map/leaving_state/pallas_call | solution.py:83
  21.6 1.9 collective-permute-start
  24.0 1.7 cache_pages.1
  25.8 1.3 attend_own.1
  27.1 1.0 copy-done.6
  28.1 3.9 %mamba_local.1.y_ref = f32[512,896]{1,0:T(8,128)S(1)} custom-call(bf16[512,896]{1,0:T(8,128)(2,1)S(1)} %copy-done.3, bf16[512,128]{1,0:T(8,128)(2,1)S(1)} %copy-done.8, bf16[512,128]{1,0:T(8,128)(2,1)S(1)} %copy-done.9, f32[16,512]{1,0:T(8,128)S(1)} %get-tuple-element.42.row_ref, f32[512,128]{1,0:T(8,128)S(1)} %get-tuple-element.43.col_ref, ...), custom_call_target="tpu_custom_call" | custom-call | tf_op jit(solution)/shard_map/mamba_local/pallas_call | solution.py:155
  32.0 1.3 copy-done
  33.5 3.8 %collective-permute-done.1.q_ref = bf16[464,512]{1,0:T(8,128)(2,1)} collective-permute-done((bf16[464,512]{1,0:T(8,128)(2,1)}, bf16[464,512]{1,0:T(8,128)(2,1)}, u32[]{:S(2)}, u32[]{:S(2)}) %collective-permute-start.1) | collective-permute-done | bytes 475168 | tf_op jit(solution)/shard_map/ppermute | solution.py:544
  37.3 13.3 %collective-permute-done.2.kv_ref = bf16[912,512]{1,0:T(8,128)(2,1)} collective-permute-done((bf16[912,512]{1,0:T(8,128)(2,1)}, bf16[912,512]{1,0:T(8,128)(2,1)}, u32[]{:S(2)}, u32[]{:S(2)}) %collective-permute-start.2) | collective-permute-done | bytes 933920 | tf_op jit(solution)/shard_map/ppermute | solution.py:544
  50.6 4.5 %attend_next.1 = bf16[464,512]{1,0:T(8,128)(2,1)} custom-call(bf16[464,512]{1,0:T(8,128)(2,1)} %collective-permute-done.1.q_ref, bf16[448,512]{1,0:T(8,128)(2,1)S(1)} %bitcast.28, bf16[448,512]{1,0:T(8,128)(2,1)S(1)} %bitcast.32, bf16[912,512]{1,0:T(8,128)(2,1)} %collective-permute-done.2.kv_ref, s32[512,1]{1,0:T(8,128)S(1)} %copy.33.segc_ref), custom_call_target="tpu_custom_call" | custom-call | tf_op jit(solution)/shard_map/attend_next/pallas_call | solution.py:284
  55.1 1.9 collective-permute-start.8
  57.0 3.4 %collective-permute-start.3 = (bf16[80,896]{1,0:T(8,128)(2,1)S(1)}, bf16[80,896]{1,0:T(8,128)(2,1)S(1)}, u32[]{:S(2)}, u32[]{:S(2)}) collective-permute-start(bf16[80,896]{1,0:T(8,128)(2,1)S(1)} %pass_through.1), channel_id=1, source_target_pairs={{0,8},{8,16},{16,24},{24,32},{32,40},{40,48},{48,56},{56,64},{64,7... | collective-permute-start | bytes 430088 | tf_op jit(solution)/shard_map/ppermute | solution.py:544
  60.4 12.6 %collective-permute-done.3.carry_ref = bf16[80,896]{1,0:T(8,128)(2,1)S(1)} collective-permute-done((bf16[80,896]{1,0:T(8,128)(2,1)S(1)}, bf16[80,896]{1,0:T(8,128)(2,1)S(1)}, u32[]{:S(2)}, u32[]{:S(2)}) %collective-permute-start.3) | collective-permute-done | bytes 143392 | tf_op jit(solution)/shard_map/ppermute | solution.py:544
  73.0 3.0 %mamba_finish.1 = (f32[512,896]{1,0:T(8,128)S(1)}, f32[2,512]{1,0:T(2,128)S(1)}) custom-call(f32[512,896]{1,0:T(8,128)} %copy-done, bf16[512,896]{1,0:T(8,128)(2,1)S(1)} %copy-done.7, bf16[512,128]{1,0:T(8,128)(2,1)S(1)} %copy-done.9, f32[512,128]{1,0:T(8,128)S(1)} %get-tuple-element.43.col_ref, s32[512,1]{1,0:T(8,128)S(1)} %copy.30.segc_ref, ...), custom_call_target="tpu_custom_call" | custom-call | tf_op jit(solution)/shard_map/mamba_finish/pallas_call | solution.py:191
  76.0 1.2 collective-permute-done.4
  77.2 2.8 %collective-permute-start.7 = (f32[2,512]{1,0:T(2,128)S(1)}, f32[2,512]{1,0:T(2,128)S(1)}, u32[]{:S(2)}, u32[]{:S(2)}) collective-permute-start(f32[2,512]{1,0:T(2,128)S(1)} %add.97), channel_id=1, source_target_pairs={{0,6},{2,0},{4,2},{6,4},{1,7},{3,1},{5,3},{7,5},{8,14},{10,8},{12,... | collective-permute-start | bytes 12296 | tf_op jit(solution)/shard_map/ppermute | solution.py:549
  81.7 3.3 %collective-permute-done.6 = f32[2,512]{1,0:T(2,128)S(1)} collective-permute-done((f32[2,512]{1,0:T(2,128)S(1)}, f32[2,512]{1,0:T(2,128)S(1)}, u32[]{:S(2)}, u32[]{:S(2)}) %collective-permute-start.6) | collective-permute-done | bytes 4128 | tf_op jit(solution)/shard_map/ppermute | solution.py:549
  86.1 1.4 merge.1.att_ref
  87.5 11.2 %project.1 = (f32[448,512]{1,0:T(8,128)S(1)}, bf16[448,512]{1,0:T(8,128)(2,1)S(1)}, f32[448,512]{1,0:T(8,128)S(1)}, bf16[448,512]{1,0:T(8,128)(2,1)S(1)}, f32[44...) custom-call(s32[5]{0:T(128)S(1)} %stack.30.place_ref, ...), custom_call_target="tpu_custom_call" | custom-call | tf_op jit(solution)/shard_map/project/pallas_call | solution.py:369
  100.8 3.2 %collective-permute-start.15 = (bf16[224,512]{1,0:T(8,128)(2,1)S(1)}, bf16[224,512]{1,0:T(8,128)(2,1)S(1)}, u32[]{:S(2)}, u32[]{:S(2)}) collective-permute-start(bf16[224,512]{1,0:T(8,128)(2,1)S(1)} %get-tuple-element.63), channel_id=1, source_target_pairs={{0,6},{2,0},{4,2},{6,4},{1,7},{3,1},{5,3},{7,5},{8,14},{10,8},{12,... | collective-permute-start | bytes 688136 | tf_op jit(solution)/shard_map/ppermute | solution.py:549
  104.0 5.6 %collective-permute-done.12.refs_0_ = bf16[224,512]{1,0:T(8,128)(2,1)S(1)} collective-permute-done((bf16[224,512]{1,0:T(8,128)(2,1)S(1)}, bf16[224,512]{1,0:T(8,128)(2,1)S(1)}, u32[]{:S(2)}, u32[]{:S(2)}) %collective-permute-start.12) | collective-permute-done | bytes 229408 | tf_op jit(solution)/shard_map/ppermute | solution.py:549
  110.0 3.3 %collective-permute-start.16 = (bf16[448,512]{1,0:T(8,128)(2,1)S(1)}, bf16[448,512]{1,0:T(8,128)(2,1)}, u32[]{:S(2)}, u32[]{:S(2)}) collective-permute-start(bf16[448,512]{1,0:T(8,128)(2,1)S(1)} %add_up.5), channel_id=1, source_target_pairs={{0,6},{2,0},{4,2},{6,4},{1,7},{3,1},{5,3},{7,5},{8,14},{10,8},{12,... | collective-permute-start | bytes 1376264 | tf_op jit(solution)/shard_map/ppermute | solution.py:549
  113.3 1.2 fusion.3
  114.6 8.3 %collective-permute-done.13 = bf16[448,512]{1,0:T(8,128)(2,1)S(1)} collective-permute-done((bf16[448,512]{1,0:T(8,128)(2,1)S(1)}, bf16[448,512]{1,0:T(8,128)(2,1)S(1)}, u32[]{:S(2)}, u32[]{:S(2)}) %collective-permute-start.13) | collective-permute-done | bytes 458784 | tf_op jit(solution)/shard_map/ppermute | solution.py:549
  122.9 1.4 multiply_convert_fusion.refs_0_
  124.3 3.1 %collective-permute-start.22 = (bf16[448,512]{1,0:T(8,128)(2,1)S(1)}, bf16[448,512]{1,0:T(8,128)(2,1)S(1)}, u32[]{:S(2)}, u32[]{:S(2)}) collective-permute-start(bf16[448,512]{1,0:T(8,128)(2,1)S(1)} %multiply_convert_fusion.refs_0_), channel_id=1, source_target_pairs={{0,6},{2,0},{4,2},{6,4},{1,7},{3,1},{5,3},{7,5},{8,14},{10,8},{12,... | collective-permute-start | bytes 1376264 | tf_op jit(solution)/shard_map/ppermute | solution.py:549
  127.4 8.2 %collective-permute-done.22.refs_8_ = bf16[448,512]{1,0:T(8,128)(2,1)S(1)} collective-permute-done((bf16[448,512]{1,0:T(8,128)(2,1)S(1)}, bf16[448,512]{1,0:T(8,128)(2,1)S(1)}, u32[]{:S(2)}, u32[]{:S(2)}) %collective-permute-start.22) | collective-permute-done | bytes 458784 | tf_op jit(solution)/shard_map/ppermute | solution.py:549
  135.6 3.8 %collective-permute-start.23 = (bf16[224,512]{1,0:T(8,128)(2,1)S(1)}, bf16[224,512]{1,0:T(8,128)(2,1)S(1)}, u32[]{:S(2)}, u32[]{:S(2)}) collective-permute-start(bf16[224,512]{1,0:T(8,128)(2,1)S(1)} %slice.9), channel_id=1, source_target_pairs={{0,6},{2,0},{4,2},{6,4},{1,7},{3,1},{5,3},{7,5},{8,14},{10,8},{12,... | collective-permute-start | bytes 688136 | tf_op jit(solution)/shard_map/ppermute | solution.py:549
  140.2 2.7 %collective-permute-done.23.refs_6_ = bf16[224,512]{1,0:T(8,128)(2,1)S(1)} collective-permute-done((bf16[224,512]{1,0:T(8,128)(2,1)S(1)}, bf16[224,512]{1,0:T(8,128)(2,1)S(1)}, u32[]{:S(2)}, u32[]{:S(2)}) %collective-permute-start.23) | collective-permute-done | bytes 229408 | tf_op jit(solution)/shard_map/ppermute | solution.py:549
  142.9 3.8 %collective-permute-done.20.refs_4_ = bf16[224,512]{1,0:T(8,128)(2,1)S(1)} collective-permute-done((bf16[224,512]{1,0:T(8,128)(2,1)S(1)}, bf16[224,512]{1,0:T(8,128)(2,1)S(1)}, u32[]{:S(2)}, u32[]{:S(2)}) %collective-permute-start.20) | collective-permute-done | bytes 229408 | tf_op jit(solution)/shard_map/ppermute | solution.py:549
  148.3 0.9 copy-done.11
  149.2 2.5 %prepare.1 = (bf16[512,3584]{1,0:T(8,128)(2,1)S(1)}, f32[512,128]{1,0:T(8,128)S(1)}) custom-call(s32[2]{0:T(128)S(1)} %pad_add_fusion.place_ref, bf16[448,512]{1,0:T(8,128)(2,1)S(1)} %multiply_convert_fusion.refs_0_, bf16[448,512]{1,0:T(8,128)(2,1)S(1)} %collective-permute-done.17.refs_1_, bf16[448,512]{1,0:T(8,128)(2,1)S(1)} %collective-permute-done.18.refs_2_, ...), custom_call_target="tpu_custom_call" | custom-call | tf_op jit(solution)/shard_map/prepare/pallas_call | solution.py:417
  151.8 1.9 copy-done.4
  153.6 20.1 %mlp.1 = (f32[448,512]{1,0:T(8,128)S(1)}, bf16[448,512]{1,0:T(8,128)(2,1)S(1)}, f32[448,512]{1,0:T(8,128)S(1)}, bf16[448,512]{1,0:T(8,128)(2,1)S(1)}, f32[448,51...) custom-call(s32[5]{0:T(128)S(1)} %stack.30.place_ref, ...), custom_call_target="tpu_custom_call" | custom-call | tf_op jit(solution)/shard_map/mlp/pallas_call | solution.py:465
  175.8 3.2 %collective-permute-start.32 = (bf16[224,512]{1,0:T(8,128)(2,1)S(1)}, bf16[224,512]{1,0:T(8,128)(2,1)S(1)}, u32[]{:S(2)}, u32[]{:S(2)}) collective-permute-start(bf16[224,512]{1,0:T(8,128)(2,1)S(1)} %get-tuple-element.75), channel_id=1, source_target_pairs={{0,6},{2,0},{4,2},{6,4},{1,7},{3,1},{5,3},{7,5},{8,14},{10,8},{12,... | collective-permute-start | bytes 688136 | tf_op jit(solution)/shard_map/ppermute | solution.py:549
  179.1 5.6 %collective-permute-done.29.refs_0_ = bf16[224,512]{1,0:T(8,128)(2,1)S(1)} collective-permute-done((bf16[224,512]{1,0:T(8,128)(2,1)S(1)}, bf16[224,512]{1,0:T(8,128)(2,1)S(1)}, u32[]{:S(2)}, u32[]{:S(2)}) %collective-permute-start.29) | collective-permute-done | bytes 229408 | tf_op jit(solution)/shard_map/ppermute | solution.py:549
  185.0 3.3 %collective-permute-start.33 = (bf16[448,512]{1,0:T(8,128)(2,1)S(1)}, bf16[448,512]{1,0:T(8,128)(2,1)S(1)}, u32[]{:S(2)}, u32[]{:S(2)}) collective-permute-start(bf16[448,512]{1,0:T(8,128)(2,1)S(1)} %add_up.7), channel_id=1, source_target_pairs={{0,6},{2,0},{4,2},{6,4},{1,7},{3,1},{5,3},{7,5},{8,14},{10,8},{12,... | collective-permute-start | bytes 1376264 | tf_op jit(solution)/shard_map/ppermute | solution.py:549
  188.3 1.4 convert_add_fusion
  189.7 8.1 %collective-permute-done.30 = bf16[448,512]{1,0:T(8,128)(2,1)S(1)} collective-permute-done((bf16[448,512]{1,0:T(8,128)(2,1)S(1)}, bf16[448,512]{1,0:T(8,128)(2,1)S(1)}, u32[]{:S(2)}, u32[]{:S(2)}) %collective-permute-start.30) | collective-permute-done | bytes 458784 | tf_op jit(solution)/shard_map/ppermute | solution.py:549
  198.2 1.1 collective-permute-done.34
  199.3 3.1 %collective-permute-start.37 = (f32[1,512]{1,0:T(1,128)S(1)}, f32[1,512]{1,0:T(1,128)S(1)}, u32[]{:S(2)}, u32[]{:S(2)}) collective-permute-start(f32[1,512]{1,0:T(1,128)S(1)} %add.111), channel_id=1, source_target_pairs={{0,6},{2,0},{4,2},{6,4},{1,7},{3,1},{5,3},{7,5},{8,14},{10,8},{12,... | collective-permute-start | bytes 6152 | tf_op jit(solution)/shard_map/ppermute | solution.py:549
  202.5 0.9 collective-permute-start.35
  203.8 3.8 %collective-permute-done.36 = f32[1,512]{1,0:T(1,128)S(1)} collective-permute-done((f32[1,512]{1,0:T(1,128)S(1)}, f32[1,512]{1,0:T(1,128)S(1)}, u32[]{:S(2)}, u32[]{:S(2)}) %collective-permute-start.36) | collective-permute-done | bytes 2080 | tf_op jit(solution)/shard_map/ppermute | solution.py:549
  207.6 0.9 fusion.4
  (130 shorter events, 12.5 us)
Async XLA Ops:
  7.2 146.4 %all-gather.3.cloned.1.call-start = ((), (), s32[]{:S(2)}) async-start(), calls=%async_computation | async-start | bytes 20471808 | tf_op jit(solution)/shard_map/all_gather | solution.py:632
  9.4 10.0 %copy-start.3 = (bf16[512,896]{1,0:T(8,128)(2,1)S(1)}, bf16[512,896]{1,0:T(8,128)(2,1)}, u32[]{:S(2)}) copy-start(bf16[512,896]{1,0:T(8,128)(2,1)} %x_ref.3) | copy-start | bytes 2752516
  9.5 14.0 %copy-start.24 = (f32[14]{0:T(128)S(1)}, f32[14]{0:T(128)}, u32[]{:S(2)}) copy-start(f32[14]{0:T(128)} %param.33) | copy-start | bytes 172
  9.6 14.2 %copy-start.25 = (s32[1,32]{1,0:T(1,128)S(1)}, s32[1,32]{1,0:T(1,128)}, u32[]{:S(2)}) copy-start(s32[1,32]{1,0:T(1,128)} %param.26) | copy-start | bytes 388
  10.6 40.0 %collective-permute-start.2 = (bf16[912,512]{1,0:T(8,128)(2,1)}, bf16[912,512]{1,0:T(8,128)(2,1)}, u32[]{:S(2)}, u32[]{:S(2)}) collective-permute-start(bf16[912,512]{1,0:T(8,128)(2,1)} %pad_maximum_fusion), channel_id=1, source_target_pairs={{0,8},{8,16},{16,24},{24,32},{32,40},{40,48},{48,56},{56,64},{64,7... | collective-permute-start | bytes 2801672 | tf_op jit(solution)/shard_map/ppermute | solution.py:544
  14.9 22.4 %collective-permute-start.1 = (bf16[464,512]{1,0:T(8,128)(2,1)}, bf16[464,512]{1,0:T(8,128)(2,1)}, u32[]{:S(2)}, u32[]{:S(2)}) collective-permute-start(bf16[464,512]{1,0:T(8,128)(2,1)} %pad_maximum_fusion.1), channel_id=1, source_target_pairs={{8,0},{16,8},{24,16},{32,24},{40,32},{48,40},{56,48},{64,56},{72,6... | collective-permute-start | bytes 1425416 | tf_op jit(solution)/shard_map/ppermute | solution.py:544
  21.6 35.3 %collective-permute-start = (bf16[80,896]{1,0:T(8,128)(2,1)S(1)}, bf16[80,896]{1,0:T(8,128)(2,1)S(1)}, u32[]{:S(2)}, u32[]{:S(2)}) collective-permute-start(bf16[80,896]{1,0:T(8,128)(2,1)S(1)} %get-tuple-element.47.state_ref), channel_id=1, source_target_pairs={{0,8},{8,16},{16,24},{24,32},{32,40},{40,48},{48,56},{56,64},{64,7... | collective-permute-start | bytes 430088 | tf_op jit(solution)/shard_map/ppermute | solution.py:544
  33.5 39.5 %copy-start.7 = (bf16[512,896]{1,0:T(8,128)(2,1)S(1)}, bf16[512,896]{1,0:T(8,128)(2,1)}, u32[]{:S(2)}) copy-start(bf16[512,896]{1,0:T(8,128)(2,1)} %z_ref.1) | copy-start | bytes 2752516
  55.1 31.1 %collective-permute-start.8 = (bf16[464,512]{1,0:T(8,128)(2,1)}, bf16[464,512]{1,0:T(8,128)(2,1)S(1)}, u32[]{:S(2)}, u32[]{:S(2)}) collective-permute-start(bf16[464,512]{1,0:T(8,128)(2,1)} %attend_next.1), channel_id=1, source_target_pairs={{0,8},{8,16},{16,24},{24,32},{32,40},{40,48},{48,56},{56,64},{64,7... | collective-permute-start | bytes 1425416 | tf_op jit(solution)/shard_map/ppermute | solution.py:544
  57.0 24.6 %copy-start.21 = (f32[896]{0:T(1024)S(1)}, f32[896]{0:T(1024)}, u32[]{:S(2)}) copy-start(f32[896]{0:T(1024)} %param.34) | copy-start | bytes 10756
  57.0 15.9 %collective-permute-start.3 = (bf16[80,896]{1,0:T(8,128)(2,1)S(1)}, bf16[80,896]{1,0:T(8,128)(2,1)S(1)}, u32[]{:S(2)}, u32[]{:S(2)}) collective-permute-start(bf16[80,896]{1,0:T(8,128)(2,1)S(1)} %pass_through.1), channel_id=1, source_target_pairs={{0,8},{8,16},{16,24},{24,32},{32,40},{40,48},{48,56},{56,64},{64,7... | collective-permute-start | bytes 430088 | tf_op jit(solution)/shard_map/ppermute | solution.py:544
  75.9 1.2 collective-permute-start.4
  77.2 4.5 %collective-permute-start.7 = (f32[2,512]{1,0:T(2,128)S(1)}, f32[2,512]{1,0:T(2,128)S(1)}, u32[]{:S(2)}, u32[]{:S(2)}) collective-permute-start(f32[2,512]{1,0:T(2,128)S(1)} %add.97), channel_id=1, source_target_pairs={{0,6},{2,0},{4,2},{6,4},{1,7},{3,1},{5,3},{7,5},{8,14},{10,8},{12,... | collective-permute-start | bytes 12296 | tf_op jit(solution)/shard_map/ppermute | solution.py:549
  79.9 5.1 %collective-permute-start.6 = (f32[2,512]{1,0:T(2,128)S(1)}, f32[2,512]{1,0:T(2,128)S(1)}, u32[]{:S(2)}, u32[]{:S(2)}) collective-permute-start(f32[2,512]{1,0:T(2,128)S(1)} %add.97), channel_id=1, source_target_pairs={{0,4},{2,6},{4,0},{6,2},{1,5},{3,7},{5,1},{7,3},{8,12},{10,14},{12... | collective-permute-start | bytes 12296 | tf_op jit(solution)/shard_map/ppermute | solution.py:549
  80.7 4.8 %collective-permute-start.5 = (f32[2,512]{1,0:T(2,128)S(1)}, f32[2,512]{1,0:T(2,128)S(1)}, u32[]{:S(2)}, u32[]{:S(2)}) collective-permute-start(f32[2,512]{1,0:T(2,128)S(1)} %add.97), channel_id=1, source_target_pairs={{0,2},{2,4},{4,6},{6,0},{1,3},{3,5},{5,7},{7,1},{8,10},{10,12},{12... | collective-permute-start | bytes 12296 | tf_op jit(solution)/shard_map/ppermute | solution.py:549
  98.7 1.9 collective-permute-start.11
  98.8 5.2 %collective-permute-start.10 = (bf16[448,512]{1,0:T(8,128)(2,1)S(1)}, bf16[448,512]{1,0:T(8,128)(2,1)S(1)}, u32[]{:S(2)}, u32[]{:S(2)}) collective-permute-start(bf16[448,512]{1,0:T(8,128)(2,1)S(1)} %get-tuple-element.57), channel_id=1, source_target_pairs={{0,1},{1,0},{2,3},{3,2},{4,5},{5,4},{6,7},{7,6},{8,9},{9,8},{10,11... | collective-permute-start | bytes 1376264 | tf_op jit(solution)/shard_map/ppermute | solution.py:553
  99.3 10.5 %collective-permute-start.14 = (bf16[448,512]{1,0:T(8,128)(2,1)S(1)}, bf16[448,512]{1,0:T(8,128)(2,1)S(1)}, u32[]{:S(2)}, u32[]{:S(2)}) collective-permute-start(bf16[448,512]{1,0:T(8,128)(2,1)S(1)} %get-tuple-element.62), channel_id=1, source_target_pairs={{0,1},{1,0},{2,3},{3,2},{4,5},{5,4},{6,7},{7,6},{8,9},{9,8},{10,11... | collective-permute-start | bytes 1376264 | tf_op jit(solution)/shard_map/ppermute | solution.py:553
  99.4 13.9 %collective-permute-start.9 = (bf16[448,512]{1,0:T(8,128)(2,1)S(1)}, bf16[448,512]{1,0:T(8,128)(2,1)}, u32[]{:S(2)}, u32[]{:S(2)}) collective-permute-start(bf16[448,512]{1,0:T(8,128)(2,1)S(1)} %get-tuple-element.55), channel_id=1, source_target_pairs={{0,1},{1,0},{2,3},{3,2},{4,5},{5,4},{6,7},{7,6},{8,9},{9,8},{10,11... | collective-permute-start | bytes 1376264 | tf_op jit(solution)/shard_map/ppermute | solution.py:553
  100.7 8.9 %collective-permute-start.12 = (bf16[224,512]{1,0:T(8,128)(2,1)S(1)}, bf16[224,512]{1,0:T(8,128)(2,1)S(1)}, u32[]{:S(2)}, u32[]{:S(2)}) collective-permute-start(bf16[224,512]{1,0:T(8,128)(2,1)S(1)} %get-tuple-element.60), channel_id=1, source_target_pairs={{0,2},{2,4},{4,6},{6,0},{1,3},{3,5},{5,7},{7,1},{8,10},{10,12},{12... | collective-permute-start | bytes 688136 | tf_op jit(solution)/shard_map/ppermute | solution.py:549
  100.8 9.1 %collective-permute-start.15 = (bf16[224,512]{1,0:T(8,128)(2,1)S(1)}, bf16[224,512]{1,0:T(8,128)(2,1)S(1)}, u32[]{:S(2)}, u32[]{:S(2)}) collective-permute-start(bf16[224,512]{1,0:T(8,128)(2,1)S(1)} %get-tuple-element.63), channel_id=1, source_target_pairs={{0,6},{2,0},{4,2},{6,4},{1,7},{3,1},{5,3},{7,5},{8,14},{10,8},{12,... | collective-permute-start | bytes 688136 | tf_op jit(solution)/shard_map/ppermute | solution.py:549
  109.8 13.1 %collective-permute-start.13 = (bf16[448,512]{1,0:T(8,128)(2,1)S(1)}, bf16[448,512]{1,0:T(8,128)(2,1)S(1)}, u32[]{:S(2)}, u32[]{:S(2)}) collective-permute-start(bf16[448,512]{1,0:T(8,128)(2,1)S(1)} %add_up.4), channel_id=1, source_target_pairs={{0,2},{2,4},{4,6},{6,0},{1,3},{3,5},{5,7},{7,1},{8,10},{10,12},{12... | collective-permute-start | bytes 1376264 | tf_op jit(solution)/shard_map/ppermute | solution.py:549
  110.0 12.9 %collective-permute-start.16 = (bf16[448,512]{1,0:T(8,128)(2,1)S(1)}, bf16[448,512]{1,0:T(8,128)(2,1)}, u32[]{:S(2)}, u32[]{:S(2)}) collective-permute-start(bf16[448,512]{1,0:T(8,128)(2,1)S(1)} %add_up.5), channel_id=1, source_target_pairs={{0,6},{2,0},{4,2},{6,4},{1,7},{3,1},{5,3},{7,5},{8,14},{10,8},{12,... | collective-permute-start | bytes 1376264 | tf_op jit(solution)/shard_map/ppermute | solution.py:549
  114.6 24.9 %copy-start.14 = (f32[448,512]{1,0:T(8,128)}, f32[448,512]{1,0:T(8,128)S(1)}, u32[]{:S(2)}) copy-start(f32[448,512]{1,0:T(8,128)S(1)} %fusion.3) | copy-start | bytes 2752516
  122.9 12.7 %copy-start.17 = (bf16[448,512]{1,0:T(8,128)(2,1)}, bf16[448,512]{1,0:T(8,128)(2,1)S(1)}, u32[]{:S(2)}) copy-start(bf16[448,512]{1,0:T(8,128)(2,1)S(1)} %collective-permute-done.13) | copy-start | bytes 1376260
  124.3 11.3 %collective-permute-start.22 = (bf16[448,512]{1,0:T(8,128)(2,1)S(1)}, bf16[448,512]{1,0:T(8,128)(2,1)S(1)}, u32[]{:S(2)}, u32[]{:S(2)}) collective-permute-start(bf16[448,512]{1,0:T(8,128)(2,1)S(1)} %multiply_convert_fusion.refs_0_), channel_id=1, source_target_pairs={{0,6},{2,0},{4,2},{6,4},{1,7},{3,1},{5,3},{7,5},{8,14},{10,8},{12,... | collective-permute-start | bytes 1376264 | tf_op jit(solution)/shard_map/ppermute | solution.py:549
  127.4 12.0 %collective-permute-start.18 = (bf16[448,512]{1,0:T(8,128)(2,1)S(1)}, bf16[448,512]{1,0:T(8,128)(2,1)S(1)}, u32[]{:S(2)}, u32[]{:S(2)}) collective-permute-start(bf16[448,512]{1,0:T(8,128)(2,1)S(1)} %multiply_convert_fusion.refs_0_), channel_id=1, source_target_pairs={{0,2},{2,4},{4,6},{6,0},{1,3},{3,5},{5,7},{7,1},{8,10},{10,12},{12... | collective-permute-start | bytes 1376264 | tf_op jit(solution)/shard_map/ppermute | solution.py:549
  135.6 7.3 %collective-permute-start.23 = (bf16[224,512]{1,0:T(8,128)(2,1)S(1)}, bf16[224,512]{1,0:T(8,128)(2,1)S(1)}, u32[]{:S(2)}, u32[]{:S(2)}) collective-permute-start(bf16[224,512]{1,0:T(8,128)(2,1)S(1)} %slice.9), channel_id=1, source_target_pairs={{0,6},{2,0},{4,2},{6,4},{1,7},{3,1},{5,3},{7,5},{8,14},{10,8},{12,... | collective-permute-start | bytes 688136 | tf_op jit(solution)/shard_map/ppermute | solution.py:549
  139.4 7.3 %collective-permute-start.20 = (bf16[224,512]{1,0:T(8,128)(2,1)S(1)}, bf16[224,512]{1,0:T(8,128)(2,1)S(1)}, u32[]{:S(2)}, u32[]{:S(2)}) collective-permute-start(bf16[224,512]{1,0:T(8,128)(2,1)S(1)} %slice.8), channel_id=1, source_target_pairs={{0,2},{2,4},{4,6},{6,0},{1,3},{3,5},{5,7},{7,1},{8,10},{10,12},{12... | collective-permute-start | bytes 688136 | tf_op jit(solution)/shard_map/ppermute | solution.py:549
  139.5 7.3 %collective-permute-start.17 = (bf16[448,512]{1,0:T(8,128)(2,1)S(1)}, bf16[448,512]{1,0:T(8,128)(2,1)S(1)}, u32[]{:S(2)}, u32[]{:S(2)}) collective-permute-start(bf16[448,512]{1,0:T(8,128)(2,1)S(1)} %multiply_convert_fusion.refs_0_), channel_id=1, source_target_pairs={{0,1},{1,0},{2,3},{3,2},{4,5},{5,4},{6,7},{7,6},{8,9},{9,8},{10,11... | collective-permute-start | bytes 1376264 | tf_op jit(solution)/shard_map/ppermute | solution.py:553
  139.6 7.2 %collective-permute-start.25 = (bf16[448,512]{1,0:T(8,128)(2,1)S(1)}, bf16[448,512]{1,0:T(8,128)(2,1)S(1)}, u32[]{:S(2)}, u32[]{:S(2)}) collective-permute-start(bf16[448,512]{1,0:T(8,128)(2,1)S(1)} %collective-permute-done.22.refs_8_), channel_id=1, source_target_pairs={{0,1},{1,0},{2,3},{3,2},{4,5},{5,4},{6,7},{7,6},{8,9},{9,8},{10,11... | collective-permute-start | bytes 1376264 | tf_op jit(solution)/shard_map/ppermute | solution.py:553
  140.1 6.7 %collective-permute-start.19 = (bf16[448,512]{1,0:T(8,128)(2,1)S(1)}, bf16[448,512]{1,0:T(8,128)(2,1)S(1)}, u32[]{:S(2)}, u32[]{:S(2)}) collective-permute-start(bf16[448,512]{1,0:T(8,128)(2,1)S(1)} %collective-permute-done.18.refs_2_), channel_id=1, source_target_pairs={{0,1},{1,0},{2,3},{3,2},{4,5},{5,4},{6,7},{7,6},{8,9},{9,8},{10,11... | collective-permute-start | bytes 1376264 | tf_op jit(solution)/shard_map/ppermute | solution.py:553
  142.9 3.9 %collective-permute-start.24 = (bf16[224,512]{1,0:T(8,128)(2,1)S(1)}, bf16[224,512]{1,0:T(8,128)(2,1)S(1)}, u32[]{:S(2)}, u32[]{:S(2)}) collective-permute-start(bf16[224,512]{1,0:T(8,128)(2,1)S(1)} %collective-permute-done.23.refs_6_), channel_id=1, source_target_pairs={{0,1},{1,0},{2,3},{3,2},{4,5},{5,4},{6,7},{7,6},{8,9},{9,8},{10,11... | collective-permute-start | bytes 688136 | tf_op jit(solution)/shard_map/ppermute | solution.py:553
  146.7 1.6 collective-permute-start.21
  173.8 1.9 collective-permute-start.28
  174.0 5.1 %collective-permute-start.27 = (bf16[448,512]{1,0:T(8,128)(2,1)S(1)}, bf16[448,512]{1,0:T(8,128)(2,1)S(1)}, u32[]{:S(2)}, u32[]{:S(2)}) collective-permute-start(bf16[448,512]{1,0:T(8,128)(2,1)S(1)} %get-tuple-element.69), channel_id=1, source_target_pairs={{0,1},{1,0},{2,3},{3,2},{4,5},{5,4},{6,7},{7,6},{8,9},{9,8},{10,11... | collective-permute-start | bytes 1376264 | tf_op jit(solution)/shard_map/ppermute | solution.py:553
  174.4 10.5 %collective-permute-start.31 = (bf16[448,512]{1,0:T(8,128)(2,1)S(1)}, bf16[448,512]{1,0:T(8,128)(2,1)S(1)}, u32[]{:S(2)}, u32[]{:S(2)}) collective-permute-start(bf16[448,512]{1,0:T(8,128)(2,1)S(1)} %get-tuple-element.74), channel_id=1, source_target_pairs={{0,1},{1,0},{2,3},{3,2},{4,5},{5,4},{6,7},{7,6},{8,9},{9,8},{10,11... | collective-permute-start | bytes 1376264 | tf_op jit(solution)/shard_map/ppermute | solution.py:553
  174.7 13.6 %collective-permute-start.26 = (bf16[448,512]{1,0:T(8,128)(2,1)S(1)}, bf16[448,512]{1,0:T(8,128)(2,1)S(1)}, u32[]{:S(2)}, u32[]{:S(2)}) collective-permute-start(bf16[448,512]{1,0:T(8,128)(2,1)S(1)} %get-tuple-element.67), channel_id=1, source_target_pairs={{0,1},{1,0},{2,3},{3,2},{4,5},{5,4},{6,7},{7,6},{8,9},{9,8},{10,11... | collective-permute-start | bytes 1376264 | tf_op jit(solution)/shard_map/ppermute | solution.py:553
  175.7 8.9 %collective-permute-start.29 = (bf16[224,512]{1,0:T(8,128)(2,1)S(1)}, bf16[224,512]{1,0:T(8,128)(2,1)S(1)}, u32[]{:S(2)}, u32[]{:S(2)}) collective-permute-start(bf16[224,512]{1,0:T(8,128)(2,1)S(1)} %get-tuple-element.72), channel_id=1, source_target_pairs={{0,2},{2,4},{4,6},{6,0},{1,3},{3,5},{5,7},{7,1},{8,10},{10,12},{12... | collective-permute-start | bytes 688136 | tf_op jit(solution)/shard_map/ppermute | solution.py:549
  175.8 9.1 %collective-permute-start.32 = (bf16[224,512]{1,0:T(8,128)(2,1)S(1)}, bf16[224,512]{1,0:T(8,128)(2,1)S(1)}, u32[]{:S(2)}, u32[]{:S(2)}) collective-permute-start(bf16[224,512]{1,0:T(8,128)(2,1)S(1)} %get-tuple-element.75), channel_id=1, source_target_pairs={{0,6},{2,0},{4,2},{6,4},{1,7},{3,1},{5,3},{7,5},{8,14},{10,8},{12,... | collective-permute-start | bytes 688136 | tf_op jit(solution)/shard_map/ppermute | solution.py:549
  184.8 13.0 %collective-permute-start.30 = (bf16[448,512]{1,0:T(8,128)(2,1)S(1)}, bf16[448,512]{1,0:T(8,128)(2,1)S(1)}, u32[]{:S(2)}, u32[]{:S(2)}) collective-permute-start(bf16[448,512]{1,0:T(8,128)(2,1)S(1)} %add_up.6), channel_id=1, source_target_pairs={{0,2},{2,4},{4,6},{6,0},{1,3},{3,5},{5,7},{7,1},{8,10},{10,12},{12... | collective-permute-start | bytes 1376264 | tf_op jit(solution)/shard_map/ppermute | solution.py:549
  185.0 12.8 %collective-permute-start.33 = (bf16[448,512]{1,0:T(8,128)(2,1)S(1)}, bf16[448,512]{1,0:T(8,128)(2,1)S(1)}, u32[]{:S(2)}, u32[]{:S(2)}) collective-permute-start(bf16[448,512]{1,0:T(8,128)(2,1)S(1)} %add_up.7), channel_id=1, source_target_pairs={{0,6},{2,0},{4,2},{6,4},{1,7},{3,1},{5,3},{7,5},{8,14},{10,8},{12,... | collective-permute-start | bytes 1376264 | tf_op jit(solution)/shard_map/ppermute | solution.py:549
  189.7 17.9 %copy-start.22 = (f32[448]{0:T(512)S(1)}, f32[448]{0:T(512)}, u32[]{:S(2)}) copy-start(f32[448]{0:T(512)} %param.41) | copy-start | bytes 5380
  198.1 10.4 %copy-start.16 = (bf16[448,512]{1,0:T(8,128)(2,1)}, bf16[448,512]{1,0:T(8,128)(2,1)S(1)}, u32[]{:S(2)}) copy-start(bf16[448,512]{1,0:T(8,128)(2,1)S(1)} %get-tuple-element.78) | copy-start | bytes 1376260
  198.1 1.2 collective-permute-start.34
  199.3 4.5 %collective-permute-start.37 = (f32[1,512]{1,0:T(1,128)S(1)}, f32[1,512]{1,0:T(1,128)S(1)}, u32[]{:S(2)}, u32[]{:S(2)}) collective-permute-start(f32[1,512]{1,0:T(1,128)S(1)} %add.111), channel_id=1, source_target_pairs={{0,6},{2,0},{4,2},{6,4},{1,7},{3,1},{5,3},{7,5},{8,14},{10,8},{12,... | collective-permute-start | bytes 6152 | tf_op jit(solution)/shard_map/ppermute | solution.py:549
  202.5 5.1 %collective-permute-start.36 = (f32[1,512]{1,0:T(1,128)S(1)}, f32[1,512]{1,0:T(1,128)S(1)}, u32[]{:S(2)}, u32[]{:S(2)}) collective-permute-start(f32[1,512]{1,0:T(1,128)S(1)} %add.111), channel_id=1, source_target_pairs={{0,4},{2,6},{4,0},{6,2},{1,5},{3,7},{5,1},{7,3},{8,12},{10,14},{12... | collective-permute-start | bytes 6152 | tf_op jit(solution)/shard_map/ppermute | solution.py:549
  202.5 5.1 %collective-permute-start.35 = (f32[1,512]{1,0:T(1,128)S(1)}, f32[1,512]{1,0:T(1,128)S(1)}, u32[]{:S(2)}, u32[]{:S(2)}) collective-permute-start(f32[1,512]{1,0:T(1,128)S(1)} %add.111), channel_id=1, source_target_pairs={{0,2},{2,4},{4,6},{6,0},{1,3},{3,5},{5,7},{7,1},{8,10},{10,12},{12... | collective-permute-start | bytes 6152 | tf_op jit(solution)/shard_map/ppermute | solution.py:549
  (17 other events, 66.2 us)
Sparse Core Ops, SparseCore 0:
  10.2 140.5 all-gather.2

commit v4 on v3

--- a/solution.py
+++ b/solution.py
@@ -553,23 +553,82 @@
     return lax.ppermute(value, "c", [(0, 1), (1, 0)])
 
 
-def add_kernel(own_ref, other_ref, *refs, top):
+def half_kernel(own_ref, other_ref, *refs, top):
     out_ref = refs[-1]
-    half = out_ref.shape[0] // 2
-    total = own_ref[...] + other_ref[...].astype(F32)
-    first, second = total[0:half], total[half:]
-    extra = refs[0][...].astype(F32)
-    out_ref[0:half, :] = (first + extra if top else first).astype(BF16)
-    out_ref[half:, :] = (second if top else second + extra).astype(BF16)
-
-
-def add_up(own, other, extra, top):
-    return pl.pallas_call(
-        functools.partial(add_kernel, top=top),
-        out_shape=jax.ShapeDtypeStruct(own.shape, BF16),
+    half = out_ref.shape[0]
+    at = slice(0, half) if top else slice(half, 2 * half)
+    total = own_ref[at, :] + other_ref[at, :].astype(F32)
+    if len(refs) == 2:
+        total = total + refs[0][...].astype(F32)
+    out_ref[...] = total.astype(BF16)
+
+
+def add_half(own, other, *extra, top):
+    return pl.pallas_call(
+        functools.partial(half_kernel, top=top),
+        out_shape=jax.ShapeDtypeStruct((own.shape[0] // 2, own.shape[1]), BF16),
         compiler_params=vmem(6),
-        name="add_up",
-    )(own, other, extra)
+        name="add_half",
+    )(own, other, *extra)
+
+
+def base_kernel(base_ref, own_ref, other_ref, top_ref, low_ref, out_ref):
+    half = top_ref.shape[0]
+    total = base_ref[...].astype(F32) + own_ref[...] + other_ref[...].astype(F32)
+    out_ref[0:half, :] = total[0:half] + top_ref[...].astype(F32)
+    out_ref[half:, :] = total[half:] + low_ref[...].astype(F32)
+
+
+def add_base(base, own, other, top, low):
+    return pl.pallas_call(
+        base_kernel,
+        out_shape=jax.ShapeDtypeStruct(own.shape, F32),
+        compiler_params=vmem(8),
+        name="add_base",
+    )(base, own, other, top, low)
+
+
+def mixed_kernel(base_ref, top_ref, low_ref, gain_ref, mixed_ref, scaled_ref):
+    half = top_ref.shape[0]
+    for at, ref in ((slice(0, half), top_ref), (slice(half, 2 * half), low_ref)):
+        mixed = base_ref[at, :] + ref[...].astype(F32)
+        mixed_ref[at, :] = mixed
+        scaled_ref[at, :] = (mixed * gain_ref[at, :]).astype(BF16)
+
+
+def finish_mixed(base, top, low, gain):
+    return pl.pallas_call(
+        mixed_kernel,
+        out_shape=(
+            jax.ShapeDtypeStruct(base.shape, F32), jax.ShapeDtypeStruct(base.shape, BF16)
+        ),
+        compiler_params=vmem(8),
+        name="finish_mixed",
+    )(base, top, low, gain)
+
+
+def hidden_kernel(base_ref, top_ref, low_ref, new_ref, kept_ref, sq_ref):
+    half = top_ref.shape[0]
+    total = jnp.zeros(sq_ref.shape, F32)
+    for at, ref in ((slice(0, half), top_ref), (slice(half, 2 * half), low_ref)):
+        new = (base_ref[at, :] + ref[...].astype(F32)).astype(BF16)
+        new_ref[at, :] = new
+        kept_ref[at, :] = new
+        wide = new.astype(F32)
+        total = total + jnp.sum(wide * wide, axis=0, keepdims=True)
+    sq_ref[...] = total
+
+
+def finish_hidden(base, top, low):
+    return pl.pallas_call(
+        hidden_kernel,
+        out_shape=(
+            jax.ShapeDtypeStruct(base.shape, BF16), jax.ShapeDtypeStruct(base.shape, BF16),
+            jax.ShapeDtypeStruct((1, T), F32),
+        ),
+        compiler_params=vmem(8),
+        name="finish_hidden",
+    )(base, top, low)
 
 
 def halves_kernel(own_ref, other_ref, first_ref, second_ref):
@@ -591,10 +650,11 @@
     up, low = add_halves(own2, swap(other2))
     up, low = along(up, 1), along(low, 3)
     other1, other3, other0 = swap(other1), swap(other3), swap(other0)
-    from_left = along(add_up(own1, other1, up, True), 1)
-    from_right = along(add_up(own3, other3, low, False), 3)
-    base = lax.optimization_barrier(base + own0 + other0.astype(F32))
-    return base + from_left.astype(F32) + from_right.astype(F32)
+    left_low = along(add_half(own1, other1, top=False), 1)
+    right_top = along(add_half(own3, other3, top=True), 3)
+    left_top = along(add_half(own1, other1, up, top=True), 1)
+    right_low = along(add_half(own3, other3, low, top=False), 3)
+    return add_base(base, own0, other0, right_top, left_low), left_top, right_low
 
 
 def gather_rows(share):
@@ -665,16 +725,19 @@
     own_out, mam = lax.optimization_barrier((own_out, mam))
     att = merge(in_hbm(own_out), own_lse, far_out)
     attn_proj, mamba_output_projection = in_hbm(attn_proj), in_hbm(mamba_output_projection)
-    mixed = scatter_sum(
-        project(place, att, mam, attn_proj, mamba_output_projection), hidden.T.astype(F32)
-    )
     own_gain = lax.dynamic_slice_in_dim(mlp_norm_gain, owner * width, width, 0)
-    blocks = gather_rows((mixed * own_gain[:, None]).astype(BF16))
+    mixed, scaled = finish_mixed(
+        *scatter_sum(project(place, att, mam, attn_proj, mamba_output_projection), hidden.T),
+        own_gain[:, None],
+    )
+    blocks = gather_rows(scaled)
     here = jnp.stack([x, core]).astype(jnp.int32)
     rows, inv = prepare(here, blocks, (1.0 / mlp_norm_gain).reshape(4, -1))
-    new_hidden = scatter_sum(mlp(place, in_hbm(rows), inv, weights), mixed).astype(BF16)
-    widened = new_hidden.astype(F32)
-    total_sq = group_sum(jnp.sum(widened * widened, axis=0, keepdims=True))
+    new_hidden, kept, squares = finish_hidden(
+        *scatter_sum(mlp(place, in_hbm(rows), inv, weights), mixed)
+    )
+    widened = kept.astype(F32)
+    total_sq = group_sum(squares)
     next_normed = (
         widened * lax.rsqrt(total_sq / total_width + EPS) * next_norm_gain[:, None]
     ).astype(BF16)

time: 216 us -> 212 us (0.981)
  waiting for transfers between devices: 84.7 us -> 76.3 us
  other arithmetic: 7.06 us -> 2.82 us
  Pallas kernels: 55.2 us -> 58.9 us
  starting transfers between devices: 47 us -> 50.5 us
    ppermute x18 -> x22, waiting for transfers between devices: 50.3 us -> 40.6 us  [along(): lax.ppermute(value, 'x', [(i, (i + steps) % count) for i in range(count)])]
    ppermute x18 -> x22, starting transfers between devices: 28.8 us -> 32.3 us  [along(): lax.ppermute(value, 'x', [(i, (i + steps) % count) for i in range(count)])]
    pallas_call x4 -> x12, Pallas kernels: 0.46 us -> 3.64 us  [the longest x8 1.2 us: add_half(): pl.pallas_call(functools.partial(half_kernel, top=top), out_shape=jax.Sha...]
    add x2 -> x0, other arithmetic: 2.61 us -> none  [scatter_sum(): base = lax.optimization_barrier(base + own0 + other0.astype(F32))]
    unnamed x52 -> x42, local copies, waits for them, and re-layouts: 5.85 us -> 5.76 us
  transfers between devices with their start and end apart: 39 -> 43, of which waited for: 19 -> 23; matrix products, arithmetic and copies ran while one was open for 3% -> 1% of each run, Pallas kernels for 15% -> 17%
where the time goes in v4:
time: 212 us; the launch traced here: 210 us
  waiting for transfers between devices  76.3 us (36%)
  Pallas kernels  58.9 us (28%)
  starting transfers between devices  50.5 us (24%)
  between operations  14.6 us (7%)
  local copies, waits for them, and re-layouts  6.8 us (3%)
  other arithmetic  2.82 us (1%)
    ppermute x22, waiting for transfers between devices, along(): lax.ppermute(value, 'x', [(i, (i + steps) % count) for i in range(count)])  40.6 us
    ppermute x22, starting transfers between devices, along(): lax.ppermute(value, 'x', [(i, (i + steps) % count) for i in range(count)])  32.3 us
    ppermute x5, waiting for transfers between devices, behind(): return lax.ppermute(value, REQ, pairs)  29.7 us
    pallas_call x1, Pallas kernels, mlp(): pl.pallas_call(mlp_kernel, grid_spec=pltpu.PrefetchScalarGridSpec(num_sca...  20.1 us
    ppermute x5, starting transfers between devices, behind(): return lax.ppermute(value, REQ, pairs)  15.2 us
    pallas_call x1, Pallas kernels, project(): pl.pallas_call(project_kernel, grid_spec=pltpu.PrefetchScalarGridSpec(num...  11.6 us
    unnamed x42, local copies, waits for them, and re-layouts  5.76 us
    ppermute x15, waiting for transfers between devices, swap(): return lax.ppermute(value, 'c', [(0, 1), (1, 0)])  5.63 us
  transfers between devices with their start and end apart: 43, of which 23 were waited for; matrix products, arithmetic and copies ran while one was open for 1% of the time, Pallas kernels for 17%

profile of v4, /device:TPU:96, one launch (start us, length us, event | category | flops | bytes accessed | tf_op | source)
XLA Modules:
  0.0 209.9 jit_solution(8544588503450846180)
XLA Ops:
  7.2 2.1 %stack_three.1 = bf16[3,224,896]{2,1,0:T(8,128)(2,1)} custom-call(bf16[224,896]{1,0:T(8,128)(2,1)} %a_ref.1, bf16[224,896]{1,0:T(8,128)(2,1)} %b_ref.5, bf16[224,896]{1,0:T(8,128)(2,1)} %bitcast.41), custom_call_target="tpu_custom_call" | custom-call | tf_op jit(solution)/shard_map/stack_three/pallas_call | solution.py:530
  9.6 1.0 pad_maximum_fusion
  10.6 3.5 %collective-permute-start.2 = (bf16[912,512]{1,0:T(8,128)(2,1)}, bf16[912,512]{1,0:T(8,128)(2,1)}, u32[]{:S(2)}, u32[]{:S(2)}) collective-permute-start(bf16[912,512]{1,0:T(8,128)(2,1)} %pad_maximum_fusion), channel_id=1, source_target_pairs={{0,8},{8,16},{16,24},{24,32},{32,40},{40,48},{48,56},{56,64},{64,7... | collective-permute-start | bytes 2801672 | tf_op jit(solution)/shard_map/ppermute | solution.py:544
  14.9 4.5 %collective-permute-start.1 = (bf16[464,512]{1,0:T(8,128)(2,1)}, bf16[464,512]{1,0:T(8,128)(2,1)}, u32[]{:S(2)}, u32[]{:S(2)}) collective-permute-start(bf16[464,512]{1,0:T(8,128)(2,1)} %pad_maximum_fusion.1), channel_id=1, source_target_pairs={{8,0},{16,8},{24,16},{32,24},{40,32},{48,40},{56,48},{64,56},{72,6... | collective-permute-start | bytes 1425416 | tf_op jit(solution)/shard_map/ppermute | solution.py:544
  19.4 2.1 %leaving_state.1 = (bf16[80,896]{1,0:T(8,128)(2,1)S(1)}, f32[16,512]{1,0:T(8,128)S(1)}, f32[512,128]{1,0:T(8,128)S(1)}) custom-call(f32[14,512]{1,0:T(8,128)S(1)} %bitcast.38, f32[14,1]{1,0:T(8,128)S(1)} %copy.32.rate_ref, s32[1,512]{1,0:T(1,128)S(1)} %bitcast.33, bf16[512,896]{1,0:T(8,128)(2,1)S(1)} %copy-done.3, bf16[512,128]{1,0:T(8,128)(2,1)S(1)} %copy-done.8), custom_call_target="tpu_custom_call" | custom-call | tf_op jit(solution)/shard_map/leaving_state/pallas_call | solution.py:83
  21.6 1.9 collective-permute-start
  24.0 1.7 cache_pages.1
  25.7 1.3 attend_own.1
  27.0 1.0 copy-done.6
  28.0 4.0 %mamba_local.1.y_ref = f32[512,896]{1,0:T(8,128)S(1)} custom-call(bf16[512,896]{1,0:T(8,128)(2,1)S(1)} %copy-done.3, bf16[512,128]{1,0:T(8,128)(2,1)S(1)} %copy-done.8, bf16[512,128]{1,0:T(8,128)(2,1)S(1)} %copy-done.9, f32[16,512]{1,0:T(8,128)S(1)} %get-tuple-element.47.row_ref, f32[512,128]{1,0:T(8,128)S(1)} %get-tuple-element.48.col_ref, ...), custom_call_target="tpu_custom_call" | custom-call | tf_op jit(solution)/shard_map/mamba_local/pallas_call | solution.py:155
  31.9 1.3 copy-done
  33.4 3.9 %collective-permute-done.1.q_ref = bf16[464,512]{1,0:T(8,128)(2,1)} collective-permute-done((bf16[464,512]{1,0:T(8,128)(2,1)}, bf16[464,512]{1,0:T(8,128)(2,1)}, u32[]{:S(2)}, u32[]{:S(2)}) %collective-permute-start.1) | collective-permute-done | bytes 475168 | tf_op jit(solution)/shard_map/ppermute | solution.py:544
  37.2 13.3 %collective-permute-done.2.kv_ref = bf16[912,512]{1,0:T(8,128)(2,1)} collective-permute-done((bf16[912,512]{1,0:T(8,128)(2,1)}, bf16[912,512]{1,0:T(8,128)(2,1)}, u32[]{:S(2)}, u32[]{:S(2)}) %collective-permute-start.2) | collective-permute-done | bytes 933920 | tf_op jit(solution)/shard_map/ppermute | solution.py:544
  50.5 4.5 %attend_next.1 = bf16[464,512]{1,0:T(8,128)(2,1)} custom-call(bf16[464,512]{1,0:T(8,128)(2,1)} %collective-permute-done.1.q_ref, bf16[448,512]{1,0:T(8,128)(2,1)S(1)} %bitcast.25, bf16[448,512]{1,0:T(8,128)(2,1)S(1)} %bitcast.29, bf16[912,512]{1,0:T(8,128)(2,1)} %collective-permute-done.2.kv_ref, s32[512,1]{1,0:T(8,128)S(1)} %copy.34.segc_ref), custom_call_target="tpu_custom_call" | custom-call | tf_op jit(solution)/shard_map/attend_next/pallas_call | solution.py:284
  55.0 1.9 collective-permute-start.8
  57.0 3.4 %collective-permute-start.3 = (bf16[80,896]{1,0:T(8,128)(2,1)S(1)}, bf16[80,896]{1,0:T(8,128)(2,1)S(1)}, u32[]{:S(2)}, u32[]{:S(2)}) collective-permute-start(bf16[80,896]{1,0:T(8,128)(2,1)S(1)} %pass_through.1), channel_id=1, source_target_pairs={{0,8},{8,16},{16,24},{24,32},{32,40},{40,48},{48,56},{56,64},{64,7... | collective-permute-start | bytes 430088 | tf_op jit(solution)/shard_map/ppermute | solution.py:544
  60.4 12.5 %collective-permute-done.3.carry_ref = bf16[80,896]{1,0:T(8,128)(2,1)S(1)} collective-permute-done((bf16[80,896]{1,0:T(8,128)(2,1)S(1)}, bf16[80,896]{1,0:T(8,128)(2,1)S(1)}, u32[]{:S(2)}, u32[]{:S(2)}) %collective-permute-start.3) | collective-permute-done | bytes 143392 | tf_op jit(solution)/shard_map/ppermute | solution.py:544
  72.9 2.9 %mamba_finish.1 = (f32[512,896]{1,0:T(8,128)S(1)}, f32[2,512]{1,0:T(2,128)S(1)}) custom-call(f32[512,896]{1,0:T(8,128)} %copy-done, bf16[512,896]{1,0:T(8,128)(2,1)S(1)} %copy-done.7, bf16[512,128]{1,0:T(8,128)(2,1)S(1)} %copy-done.9, f32[512,128]{1,0:T(8,128)S(1)} %get-tuple-element.48.col_ref, s32[512,1]{1,0:T(8,128)S(1)} %copy.31.segc_ref, ...), custom_call_target="tpu_custom_call" | custom-call | tf_op jit(solution)/shard_map/mamba_finish/pallas_call | solution.py:191
  76.0 1.2 collective-permute-done.4
  77.1 2.8 %collective-permute-start.7 = (f32[2,512]{1,0:T(2,128)S(1)}, f32[2,512]{1,0:T(2,128)S(1)}, u32[]{:S(2)}, u32[]{:S(2)}) collective-permute-start(f32[2,512]{1,0:T(2,128)S(1)} %add.73), channel_id=1, source_target_pairs={{0,6},{2,0},{4,2},{6,4},{1,7},{3,1},{5,3},{7,5},{8,14},{10,8},{12,... | collective-permute-start | bytes 12296 | tf_op jit(solution)/shard_map/ppermute | solution.py:549
  81.7 3.3 %collective-permute-done.6 = f32[2,512]{1,0:T(2,128)S(1)} collective-permute-done((f32[2,512]{1,0:T(2,128)S(1)}, f32[2,512]{1,0:T(2,128)S(1)}, u32[]{:S(2)}, u32[]{:S(2)}) %collective-permute-start.6) | collective-permute-done | bytes 4128 | tf_op jit(solution)/shard_map/ppermute | solution.py:549
  86.1 1.4 merge.1.att_ref
  87.5 11.6 %project.1 = (f32[448,512]{1,0:T(8,128)S(1)}, bf16[448,512]{1,0:T(8,128)(2,1)S(1)}, f32[448,512]{1,0:T(8,128)S(1)}, bf16[448,512]{1,0:T(8,128)(2,1)S(1)}, f32[44...) custom-call(s32[5]{0:T(128)S(1)} %stack.30.place_ref, ...), custom_call_target="tpu_custom_call" | custom-call | tf_op jit(solution)/shard_map/project/pallas_call | solution.py:369
  101.2 3.2 %collective-permute-start.17 = (bf16[224,512]{1,0:T(8,128)(2,1)S(1)}, bf16[224,512]{1,0:T(8,128)(2,1)S(1)}, u32[]{:S(2)}, u32[]{:S(2)}) collective-permute-start(bf16[224,512]{1,0:T(8,128)(2,1)S(1)} %get-tuple-element.68), channel_id=1, source_target_pairs={{0,6},{2,0},{4,2},{6,4},{1,7},{3,1},{5,3},{7,5},{8,14},{10,8},{12,... | collective-permute-start | bytes 688136 | tf_op jit(solution)/shard_map/ppermute | solution.py:549
  104.6 2.1 collective-permute-start.13
  106.7 4.1 %collective-permute-done.15.refs_0_ = bf16[224,512]{1,0:T(8,128)(2,1)S(1)} collective-permute-done((bf16[224,512]{1,0:T(8,128)(2,1)S(1)}, bf16[224,512]{1,0:T(8,128)(2,1)S(1)}, u32[]{:S(2)}, u32[]{:S(2)}) %collective-permute-start.15) | collective-permute-done | bytes 229408 | tf_op jit(solution)/shard_map/ppermute | solution.py:549
  111.8 3.2 %collective-permute-start.18 = (bf16[224,512]{1,0:T(8,128)(2,1)}, bf16[224,512]{1,0:T(8,128)(2,1)}, u32[]{:S(2)}, u32[]{:S(2)}) collective-permute-start(bf16[224,512]{1,0:T(8,128)(2,1)} %add_half.11), channel_id=1, source_target_pairs={{0,6},{2,0},{4,2},{6,4},{1,7},{3,1},{5,3},{7,5},{8,14},{10,8},{12,... | collective-permute-start | bytes 688136 | tf_op jit(solution)/shard_map/ppermute | solution.py:549
  115.9 3.9 %collective-permute-done.16.top_ref = bf16[224,512]{1,0:T(8,128)(2,1)S(1)} collective-permute-done((bf16[224,512]{1,0:T(8,128)(2,1)S(1)}, bf16[224,512]{1,0:T(8,128)(2,1)S(1)}, u32[]{:S(2)}, u32[]{:S(2)}) %collective-permute-start.16) | collective-permute-done | bytes 229408 | tf_op jit(solution)/shard_map/ppermute | solution.py:549
  119.8 1.1 finish_mixed.1
  120.9 3.1 %collective-permute-start.24 = (bf16[448,512]{1,0:T(8,128)(2,1)S(1)}, bf16[448,512]{1,0:T(8,128)(2,1)S(1)}, u32[]{:S(2)}, u32[]{:S(2)}) collective-permute-start(bf16[448,512]{1,0:T(8,128)(2,1)S(1)} %get-tuple-element.70.refs_0_), channel_id=1, source_target_pairs={{0,6},{2,0},{4,2},{6,4},{1,7},{3,1},{5,3},{7,5},{8,14},{10,8},{12,... | collective-permute-start | bytes 1376264 | tf_op jit(solution)/shard_map/ppermute | solution.py:549
  124.1 8.7 %collective-permute-done.24.refs_8_ = bf16[448,512]{1,0:T(8,128)(2,1)S(1)} collective-permute-done((bf16[448,512]{1,0:T(8,128)(2,1)S(1)}, bf16[448,512]{1,0:T(8,128)(2,1)S(1)}, u32[]{:S(2)}, u32[]{:S(2)}) %collective-permute-start.24) | collective-permute-done | bytes 458784 | tf_op jit(solution)/shard_map/ppermute | solution.py:549
  132.8 3.0 %collective-permute-start.25 = (bf16[224,512]{1,0:T(8,128)(2,1)S(1)}, bf16[224,512]{1,0:T(8,128)(2,1)S(1)}, u32[]{:S(2)}, u32[]{:S(2)}) collective-permute-start(bf16[224,512]{1,0:T(8,128)(2,1)S(1)} %slice.9), channel_id=1, source_target_pairs={{0,6},{2,0},{4,2},{6,4},{1,7},{3,1},{5,3},{7,5},{8,14},{10,8},{12,... | collective-permute-start | bytes 688136 | tf_op jit(solution)/shard_map/ppermute | solution.py:549
  136.5 2.7 %collective-permute-done.25.refs_6_ = bf16[224,512]{1,0:T(8,128)(2,1)S(1)} collective-permute-done((bf16[224,512]{1,0:T(8,128)(2,1)S(1)}, bf16[224,512]{1,0:T(8,128)(2,1)S(1)}, u32[]{:S(2)}, u32[]{:S(2)}) %collective-permute-start.25) | collective-permute-done | bytes 229408 | tf_op jit(solution)/shard_map/ppermute | solution.py:549
  140.0 3.2 %collective-permute-done.22.refs_4_ = bf16[224,512]{1,0:T(8,128)(2,1)} collective-permute-done((bf16[224,512]{1,0:T(8,128)(2,1)S(1)}, bf16[224,512]{1,0:T(8,128)(2,1)}, u32[]{:S(2)}, u32[]{:S(2)}) %collective-permute-start.22) | collective-permute-done | bytes 229408 | tf_op jit(solution)/shard_map/ppermute | solution.py:549
  143.3 1.7 collective-permute-done.23.refs_5_
  146.0 2.7 %prepare.1 = (bf16[512,3584]{1,0:T(8,128)(2,1)S(1)}, f32[512,128]{1,0:T(8,128)S(1)}) custom-call(s32[2]{0:T(128)S(1)} %pad_add_fusion.place_ref, bf16[448,512]{1,0:T(8,128)(2,1)S(1)} %get-tuple-element.70.refs_0_, bf16[448,512]{1,0:T(8,128)(2,1)S(1)} %collective-permute-done.19.refs_1_, bf16[448,512]{1,0:T(8,128)(2,1)S(1)} %collective-permute-done.20.refs_2_, ...), custom_call_target="tpu_custom_call" | custom-call | tf_op jit(solution)/shard_map/prepare/pallas_call | solution.py:417
  148.7 1.8 copy-done.4
  150.8 20.1 %mlp.1 = (f32[448,512]{1,0:T(8,128)S(1)}, bf16[448,512]{1,0:T(8,128)(2,1)S(1)}, f32[448,512]{1,0:T(8,128)S(1)}, bf16[448,512]{1,0:T(8,128)(2,1)S(1)}, f32[448,51...) custom-call(s32[5]{0:T(128)S(1)} %stack.30.place_ref, ...), custom_call_target="tpu_custom_call" | custom-call | tf_op jit(solution)/shard_map/mlp/pallas_call | solution.py:465
  172.9 1.6 collective-permute-start.34
  174.5 1.7 collective-permute-start.36
  176.3 1.6 collective-permute-start.30
  178.5 4.0 %collective-permute-done.34.refs_0_ = bf16[224,512]{1,0:T(8,128)(2,1)S(1)} collective-permute-done((bf16[224,512]{1,0:T(8,128)(2,1)S(1)}, bf16[224,512]{1,0:T(8,128)(2,1)S(1)}, u32[]{:S(2)}, u32[]{:S(2)}) %collective-permute-start.34) | collective-permute-done | bytes 229408 | tf_op jit(solution)/shard_map/ppermute | solution.py:549
  183.1 2.9 %collective-permute-start.37 = (bf16[224,512]{1,0:T(8,128)(2,1)S(1)}, bf16[224,512]{1,0:T(8,128)(2,1)S(1)}, u32[]{:S(2)}, u32[]{:S(2)}) collective-permute-start(bf16[224,512]{1,0:T(8,128)(2,1)S(1)} %add_half.15), channel_id=1, source_target_pairs={{0,6},{2,0},{4,2},{6,4},{1,7},{3,1},{5,3},{7,5},{8,14},{10,8},{12,... | collective-permute-start | bytes 688136 | tf_op jit(solution)/shard_map/ppermute | solution.py:549
  186.1 1.8 collective-permute-done.30.top_ref
  188.1 3.6 %collective-permute-done.35.top_ref = bf16[224,512]{1,0:T(8,128)(2,1)S(1)} collective-permute-done((bf16[224,512]{1,0:T(8,128)(2,1)S(1)}, bf16[224,512]{1,0:T(8,128)(2,1)S(1)}, u32[]{:S(2)}, u32[]{:S(2)}) %collective-permute-start.35) | collective-permute-done | bytes 229408 | tf_op jit(solution)/shard_map/ppermute | solution.py:549
  192.6 1.2 collective-permute-done.38
  193.8 3.0 %collective-permute-start.41 = (f32[1,512]{1,0:T(1,128)S(1)}, f32[1,512]{1,0:T(1,128)S(1)}, u32[]{:S(2)}, u32[]{:S(2)}) collective-permute-start(f32[1,512]{1,0:T(1,128)S(1)} %add.79), channel_id=1, source_target_pairs={{0,6},{2,0},{4,2},{6,4},{1,7},{3,1},{5,3},{7,5},{8,14},{10,8},{12,... | collective-permute-start | bytes 6152 | tf_op jit(solution)/shard_map/ppermute | solution.py:549
  198.0 3.8 %collective-permute-done.40 = f32[1,512]{1,0:T(1,128)S(1)} collective-permute-done((f32[1,512]{1,0:T(1,128)S(1)}, f32[1,512]{1,0:T(1,128)S(1)}, u32[]{:S(2)}, u32[]{:S(2)}) %collective-permute-start.40) | collective-permute-done | bytes 2080 | tf_op jit(solution)/shard_map/ppermute | solution.py:549
  (133 shorter events, 18.4 us)
Async XLA Ops:
  7.2 143.6 %all-gather.3.cloned.1.call-start = ((), (), s32[]{:S(2)}) async-start(), calls=%async_computation | async-start | bytes 20471808 | tf_op jit(solution)/shard_map/all_gather | solution.py:692
  9.5 14.0 %copy-start.19 = (f32[14]{0:T(128)S(1)}, f32[14]{0:T(128)}, u32[]{:S(2)}) copy-start(f32[14]{0:T(128)} %param.33) | copy-start | bytes 172
  9.6 14.1 %copy-start.20 = (s32[1,32]{1,0:T(1,128)S(1)}, s32[1,32]{1,0:T(1,128)}, u32[]{:S(2)}) copy-start(s32[1,32]{1,0:T(1,128)} %param.26) | copy-start | bytes 388
  10.6 40.0 %collective-permute-start.2 = (bf16[912,512]{1,0:T(8,128)(2,1)}, bf16[912,512]{1,0:T(8,128)(2,1)}, u32[]{:S(2)}, u32[]{:S(2)}) collective-permute-start(bf16[912,512]{1,0:T(8,128)(2,1)} %pad_maximum_fusion), channel_id=1, source_target_pairs={{0,8},{8,16},{16,24},{24,32},{32,40},{40,48},{48,56},{56,64},{64,7... | collective-permute-start | bytes 2801672 | tf_op jit(solution)/shard_map/ppermute | solution.py:544
  14.9 22.4 %collective-permute-start.1 = (bf16[464,512]{1,0:T(8,128)(2,1)}, bf16[464,512]{1,0:T(8,128)(2,1)}, u32[]{:S(2)}, u32[]{:S(2)}) collective-permute-start(bf16[464,512]{1,0:T(8,128)(2,1)} %pad_maximum_fusion.1), channel_id=1, source_target_pairs={{8,0},{16,8},{24,16},{32,24},{40,32},{48,40},{56,48},{64,56},{72,6... | collective-permute-start | bytes 1425416 | tf_op jit(solution)/shard_map/ppermute | solution.py:544
  21.6 35.3 %collective-permute-start = (bf16[80,896]{1,0:T(8,128)(2,1)S(1)}, bf16[80,896]{1,0:T(8,128)(2,1)S(1)}, u32[]{:S(2)}, u32[]{:S(2)}) collective-permute-start(bf16[80,896]{1,0:T(8,128)(2,1)S(1)} %get-tuple-element.52.state_ref), channel_id=1, source_target_pairs={{0,8},{8,16},{16,24},{24,32},{32,40},{40,48},{48,56},{56,64},{64,7... | collective-permute-start | bytes 430088 | tf_op jit(solution)/shard_map/ppermute | solution.py:544
  33.4 39.6 %copy-start.7 = (bf16[512,896]{1,0:T(8,128)(2,1)S(1)}, bf16[512,896]{1,0:T(8,128)(2,1)}, u32[]{:S(2)}) copy-start(bf16[512,896]{1,0:T(8,128)(2,1)} %z_ref.1) | copy-start | bytes 2752516
  55.0 31.1 %collective-permute-start.8 = (bf16[464,512]{1,0:T(8,128)(2,1)}, bf16[464,512]{1,0:T(8,128)(2,1)S(1)}, u32[]{:S(2)}, u32[]{:S(2)}) collective-permute-start(bf16[464,512]{1,0:T(8,128)(2,1)} %attend_next.1), channel_id=1, source_target_pairs={{0,8},{8,16},{16,24},{24,32},{32,40},{40,48},{48,56},{56,64},{64,7... | collective-permute-start | bytes 1425416 | tf_op jit(solution)/shard_map/ppermute | solution.py:544
  57.0 24.6 %copy-start.16 = (f32[896]{0:T(1024)S(1)}, f32[896]{0:T(1024)}, u32[]{:S(2)}) copy-start(f32[896]{0:T(1024)} %param.34) | copy-start | bytes 10756
  57.0 16.0 %collective-permute-start.3 = (bf16[80,896]{1,0:T(8,128)(2,1)S(1)}, bf16[80,896]{1,0:T(8,128)(2,1)S(1)}, u32[]{:S(2)}, u32[]{:S(2)}) collective-permute-start(bf16[80,896]{1,0:T(8,128)(2,1)S(1)} %pass_through.1), channel_id=1, source_target_pairs={{0,8},{8,16},{16,24},{24,32},{32,40},{40,48},{48,56},{56,64},{64,7... | collective-permute-start | bytes 430088 | tf_op jit(solution)/shard_map/ppermute | solution.py:544
  75.9 1.2 collective-permute-start.4
  77.1 4.5 %collective-permute-start.7 = (f32[2,512]{1,0:T(2,128)S(1)}, f32[2,512]{1,0:T(2,128)S(1)}, u32[]{:S(2)}, u32[]{:S(2)}) collective-permute-start(f32[2,512]{1,0:T(2,128)S(1)} %add.73), channel_id=1, source_target_pairs={{0,6},{2,0},{4,2},{6,4},{1,7},{3,1},{5,3},{7,5},{8,14},{10,8},{12,... | collective-permute-start | bytes 12296 | tf_op jit(solution)/shard_map/ppermute | solution.py:549
  79.9 5.1 %collective-permute-start.6 = (f32[2,512]{1,0:T(2,128)S(1)}, f32[2,512]{1,0:T(2,128)S(1)}, u32[]{:S(2)}, u32[]{:S(2)}) collective-permute-start(f32[2,512]{1,0:T(2,128)S(1)} %add.73), channel_id=1, source_target_pairs={{0,4},{2,6},{4,0},{6,2},{1,5},{3,7},{5,1},{7,3},{8,12},{10,14},{12... | collective-permute-start | bytes 12296 | tf_op jit(solution)/shard_map/ppermute | solution.py:549
  80.7 4.8 %collective-permute-start.5 = (f32[2,512]{1,0:T(2,128)S(1)}, f32[2,512]{1,0:T(2,128)S(1)}, u32[]{:S(2)}, u32[]{:S(2)}) collective-permute-start(f32[2,512]{1,0:T(2,128)S(1)} %add.73), channel_id=1, source_target_pairs={{0,2},{2,4},{4,6},{6,0},{1,3},{3,5},{5,7},{7,1},{8,10},{10,12},{12... | collective-permute-start | bytes 12296 | tf_op jit(solution)/shard_map/ppermute | solution.py:549
  99.1 1.9 collective-permute-start.14
  99.2 5.2 %collective-permute-start.10 = (bf16[448,512]{1,0:T(8,128)(2,1)S(1)}, bf16[448,512]{1,0:T(8,128)(2,1)S(1)}, u32[]{:S(2)}, u32[]{:S(2)}) collective-permute-start(bf16[448,512]{1,0:T(8,128)(2,1)S(1)} %get-tuple-element.62), channel_id=1, source_target_pairs={{0,1},{1,0},{2,3},{3,2},{4,5},{5,4},{6,7},{7,6},{8,9},{9,8},{10,11... | collective-permute-start | bytes 1376264 | tf_op jit(solution)/shard_map/ppermute | solution.py:553
  99.7 4.8 %collective-permute-start.12 = (bf16[448,512]{1,0:T(8,128)(2,1)S(1)}, bf16[448,512]{1,0:T(8,128)(2,1)S(1)}, u32[]{:S(2)}, u32[]{:S(2)}) collective-permute-start(bf16[448,512]{1,0:T(8,128)(2,1)S(1)} %get-tuple-element.64), channel_id=1, source_target_pairs={{0,1},{1,0},{2,3},{3,2},{4,5},{5,4},{6,7},{7,6},{8,9},{9,8},{10,11... | collective-permute-start | bytes 1376264 | tf_op jit(solution)/shard_map/ppermute | solution.py:553
  99.8 15.4 %collective-permute-start.9 = (bf16[448,512]{1,0:T(8,128)(2,1)}, bf16[448,512]{1,0:T(8,128)(2,1)S(1)}, u32[]{:S(2)}, u32[]{:S(2)}) collective-permute-start(bf16[448,512]{1,0:T(8,128)(2,1)} %get-tuple-element.60), channel_id=1, source_target_pairs={{0,1},{1,0},{2,3},{3,2},{4,5},{5,4},{6,7},{7,6},{8,9},{9,8},{10,11... | collective-permute-start | bytes 1376264 | tf_op jit(solution)/shard_map/ppermute | solution.py:553
  101.1 9.7 %collective-permute-start.15 = (bf16[224,512]{1,0:T(8,128)(2,1)S(1)}, bf16[224,512]{1,0:T(8,128)(2,1)S(1)}, u32[]{:S(2)}, u32[]{:S(2)}) collective-permute-start(bf16[224,512]{1,0:T(8,128)(2,1)S(1)} %get-tuple-element.67), channel_id=1, source_target_pairs={{0,2},{2,4},{4,6},{6,0},{1,3},{3,5},{5,7},{7,1},{8,10},{10,12},{12... | collective-permute-start | bytes 688136 | tf_op jit(solution)/shard_map/ppermute | solution.py:549
  101.2 9.8 %collective-permute-start.17 = (bf16[224,512]{1,0:T(8,128)(2,1)S(1)}, bf16[224,512]{1,0:T(8,128)(2,1)S(1)}, u32[]{:S(2)}, u32[]{:S(2)}) collective-permute-start(bf16[224,512]{1,0:T(8,128)(2,1)S(1)} %get-tuple-element.68), channel_id=1, source_target_pairs={{0,6},{2,0},{4,2},{6,4},{1,7},{3,1},{5,3},{7,5},{8,14},{10,8},{12,... | collective-permute-start | bytes 688136 | tf_op jit(solution)/shard_map/ppermute | solution.py:549
  104.4 10.8 %collective-permute-start.11 = (bf16[224,512]{1,0:T(8,128)(2,1)S(1)}, bf16[224,512]{1,0:T(8,128)(2,1)S(1)}, u32[]{:S(2)}, u32[]{:S(2)}) collective-permute-start(bf16[224,512]{1,0:T(8,128)(2,1)S(1)} %add_half.8), channel_id=1, source_target_pairs={{0,6},{2,0},{4,2},{6,4},{1,7},{3,1},{5,3},{7,5},{8,14},{10,8},{12,... | collective-permute-start | bytes 688136 | tf_op jit(solution)/shard_map/ppermute | solution.py:549
  104.6 11.1 %collective-permute-start.13 = (bf16[224,512]{1,0:T(8,128)(2,1)S(1)}, bf16[224,512]{1,0:T(8,128)(2,1)S(1)}, u32[]{:S(2)}, u32[]{:S(2)}) collective-permute-start(bf16[224,512]{1,0:T(8,128)(2,1)S(1)} %add_half.9), channel_id=1, source_target_pairs={{0,2},{2,4},{4,6},{6,0},{1,3},{3,5},{5,7},{7,1},{8,10},{10,12},{12... | collective-permute-start | bytes 688136 | tf_op jit(solution)/shard_map/ppermute | solution.py:549
  110.9 8.9 %collective-permute-start.16 = (bf16[224,512]{1,0:T(8,128)(2,1)S(1)}, bf16[224,512]{1,0:T(8,128)(2,1)S(1)}, u32[]{:S(2)}, u32[]{:S(2)}) collective-permute-start(bf16[224,512]{1,0:T(8,128)(2,1)S(1)} %add_half.10), channel_id=1, source_target_pairs={{0,2},{2,4},{4,6},{6,0},{1,3},{3,5},{5,7},{7,1},{8,10},{10,12},{12... | collective-permute-start | bytes 688136 | tf_op jit(solution)/shard_map/ppermute | solution.py:549
  111.8 8.1 %collective-permute-start.18 = (bf16[224,512]{1,0:T(8,128)(2,1)}, bf16[224,512]{1,0:T(8,128)(2,1)}, u32[]{:S(2)}, u32[]{:S(2)}) collective-permute-start(bf16[224,512]{1,0:T(8,128)(2,1)} %add_half.11), channel_id=1, source_target_pairs={{0,6},{2,0},{4,2},{6,4},{1,7},{3,1},{5,3},{7,5},{8,14},{10,8},{12,... | collective-permute-start | bytes 688136 | tf_op jit(solution)/shard_map/ppermute | solution.py:549
  120.9 11.8 %collective-permute-start.24 = (bf16[448,512]{1,0:T(8,128)(2,1)S(1)}, bf16[448,512]{1,0:T(8,128)(2,1)S(1)}, u32[]{:S(2)}, u32[]{:S(2)}) collective-permute-start(bf16[448,512]{1,0:T(8,128)(2,1)S(1)} %get-tuple-element.70.refs_0_), channel_id=1, source_target_pairs={{0,6},{2,0},{4,2},{6,4},{1,7},{3,1},{5,3},{7,5},{8,14},{10,8},{12,... | collective-permute-start | bytes 1376264 | tf_op jit(solution)/shard_map/ppermute | solution.py:549
  124.1 11.7 %collective-permute-start.20 = (bf16[448,512]{1,0:T(8,128)(2,1)S(1)}, bf16[448,512]{1,0:T(8,128)(2,1)S(1)}, u32[]{:S(2)}, u32[]{:S(2)}) collective-permute-start(bf16[448,512]{1,0:T(8,128)(2,1)S(1)} %get-tuple-element.70.refs_0_), channel_id=1, source_target_pairs={{0,2},{2,4},{4,6},{6,0},{1,3},{3,5},{5,7},{7,1},{8,10},{10,12},{12... | collective-permute-start | bytes 1376264 | tf_op jit(solution)/shard_map/ppermute | solution.py:549
  132.8 6.5 %collective-permute-start.25 = (bf16[224,512]{1,0:T(8,128)(2,1)S(1)}, bf16[224,512]{1,0:T(8,128)(2,1)S(1)}, u32[]{:S(2)}, u32[]{:S(2)}) collective-permute-start(bf16[224,512]{1,0:T(8,128)(2,1)S(1)} %slice.9), channel_id=1, source_target_pairs={{0,6},{2,0},{4,2},{6,4},{1,7},{3,1},{5,3},{7,5},{8,14},{10,8},{12,... | collective-permute-start | bytes 688136 | tf_op jit(solution)/shard_map/ppermute | solution.py:549
  135.8 7.4 %collective-permute-start.22 = (bf16[224,512]{1,0:T(8,128)(2,1)S(1)}, bf16[224,512]{1,0:T(8,128)(2,1)}, u32[]{:S(2)}, u32[]{:S(2)}) collective-permute-start(bf16[224,512]{1,0:T(8,128)(2,1)S(1)} %slice.8), channel_id=1, source_target_pairs={{0,2},{2,4},{4,6},{6,0},{1,3},{3,5},{5,7},{7,1},{8,10},{10,12},{12... | collective-permute-start | bytes 688136 | tf_op jit(solution)/shard_map/ppermute | solution.py:549
  135.9 7.4 %collective-permute-start.19 = (bf16[448,512]{1,0:T(8,128)(2,1)S(1)}, bf16[448,512]{1,0:T(8,128)(2,1)S(1)}, u32[]{:S(2)}, u32[]{:S(2)}) collective-permute-start(bf16[448,512]{1,0:T(8,128)(2,1)S(1)} %get-tuple-element.70.refs_0_), channel_id=1, source_target_pairs={{0,1},{1,0},{2,3},{3,2},{4,5},{5,4},{6,7},{7,6},{8,9},{9,8},{10,11... | collective-permute-start | bytes 1376264 | tf_op jit(solution)/shard_map/ppermute | solution.py:553
  136.0 7.3 %collective-permute-start.27 = (bf16[448,512]{1,0:T(8,128)(2,1)S(1)}, bf16[448,512]{1,0:T(8,128)(2,1)S(1)}, u32[]{:S(2)}, u32[]{:S(2)}) collective-permute-start(bf16[448,512]{1,0:T(8,128)(2,1)S(1)} %collective-permute-done.24.refs_8_), channel_id=1, source_target_pairs={{0,1},{1,0},{2,3},{3,2},{4,5},{5,4},{6,7},{7,6},{8,9},{9,8},{10,11... | collective-permute-start | bytes 1376264 | tf_op jit(solution)/shard_map/ppermute | solution.py:553
  136.4 8.6 %collective-permute-start.21 = (bf16[448,512]{1,0:T(8,128)(2,1)S(1)}, bf16[448,512]{1,0:T(8,128)(2,1)}, u32[]{:S(2)}, u32[]{:S(2)}) collective-permute-start(bf16[448,512]{1,0:T(8,128)(2,1)S(1)} %collective-permute-done.20.refs_2_), channel_id=1, source_target_pairs={{0,1},{1,0},{2,3},{3,2},{4,5},{5,4},{6,7},{7,6},{8,9},{9,8},{10,11... | collective-permute-start | bytes 1376264 | tf_op jit(solution)/shard_map/ppermute | solution.py:553
  139.3 4.0 %collective-permute-start.26 = (bf16[224,512]{1,0:T(8,128)(2,1)S(1)}, bf16[224,512]{1,0:T(8,128)(2,1)}, u32[]{:S(2)}, u32[]{:S(2)}) collective-permute-start(bf16[224,512]{1,0:T(8,128)(2,1)S(1)} %collective-permute-done.25.refs_6_), channel_id=1, source_target_pairs={{0,1},{1,0},{2,3},{3,2},{4,5},{5,4},{6,7},{7,6},{8,9},{9,8},{10,11... | collective-permute-start | bytes 688136 | tf_op jit(solution)/shard_map/ppermute | solution.py:553
  143.2 1.8 collective-permute-start.23
  170.9 1.9 collective-permute-start.33
  171.1 5.2 %collective-permute-start.29 = (bf16[448,512]{1,0:T(8,128)(2,1)S(1)}, bf16[448,512]{1,0:T(8,128)(2,1)S(1)}, u32[]{:S(2)}, u32[]{:S(2)}) collective-permute-start(bf16[448,512]{1,0:T(8,128)(2,1)S(1)} %get-tuple-element.76), channel_id=1, source_target_pairs={{0,1},{1,0},{2,3},{3,2},{4,5},{5,4},{6,7},{7,6},{8,9},{9,8},{10,11... | collective-permute-start | bytes 1376264 | tf_op jit(solution)/shard_map/ppermute | solution.py:553
  171.5 6.4 %collective-permute-start.31 = (bf16[448,512]{1,0:T(8,128)(2,1)S(1)}, bf16[448,512]{1,0:T(8,128)(2,1)S(1)}, u32[]{:S(2)}, u32[]{:S(2)}) collective-permute-start(bf16[448,512]{1,0:T(8,128)(2,1)S(1)} %get-tuple-element.78), channel_id=1, source_target_pairs={{0,1},{1,0},{2,3},{3,2},{4,5},{5,4},{6,7},{7,6},{8,9},{9,8},{10,11... | collective-permute-start | bytes 1376264 | tf_op jit(solution)/shard_map/ppermute | solution.py:553
  171.6 14.5 %collective-permute-start.28 = (bf16[448,512]{1,0:T(8,128)(2,1)S(1)}, bf16[448,512]{1,0:T(8,128)(2,1)S(1)}, u32[]{:S(2)}, u32[]{:S(2)}) collective-permute-start(bf16[448,512]{1,0:T(8,128)(2,1)S(1)} %get-tuple-element.74), channel_id=1, source_target_pairs={{0,1},{1,0},{2,3},{3,2},{4,5},{5,4},{6,7},{7,6},{8,9},{9,8},{10,11... | collective-permute-start | bytes 1376264 | tf_op jit(solution)/shard_map/ppermute | solution.py:553
  172.9 9.6 %collective-permute-start.34 = (bf16[224,512]{1,0:T(8,128)(2,1)S(1)}, bf16[224,512]{1,0:T(8,128)(2,1)S(1)}, u32[]{:S(2)}, u32[]{:S(2)}) collective-permute-start(bf16[224,512]{1,0:T(8,128)(2,1)S(1)} %get-tuple-element.81), channel_id=1, source_target_pairs={{0,2},{2,4},{4,6},{6,0},{1,3},{3,5},{5,7},{7,1},{8,10},{10,12},{12... | collective-permute-start | bytes 688136 | tf_op jit(solution)/shard_map/ppermute | solution.py:549
  174.5 8.6 %collective-permute-start.36 = (bf16[224,512]{1,0:T(8,128)(2,1)S(1)}, bf16[224,512]{1,0:T(8,128)(2,1)S(1)}, u32[]{:S(2)}, u32[]{:S(2)}) collective-permute-start(bf16[224,512]{1,0:T(8,128)(2,1)S(1)} %get-tuple-element.82), channel_id=1, source_target_pairs={{0,6},{2,0},{4,2},{6,4},{1,7},{3,1},{5,3},{7,5},{8,14},{10,8},{12,... | collective-permute-start | bytes 688136 | tf_op jit(solution)/shard_map/ppermute | solution.py:549
  176.3 11.6 %collective-permute-start.30 = (bf16[224,512]{1,0:T(8,128)(2,1)S(1)}, bf16[224,512]{1,0:T(8,128)(2,1)S(1)}, u32[]{:S(2)}, u32[]{:S(2)}) collective-permute-start(bf16[224,512]{1,0:T(8,128)(2,1)S(1)} %add_half.12), channel_id=1, source_target_pairs={{0,6},{2,0},{4,2},{6,4},{1,7},{3,1},{5,3},{7,5},{8,14},{10,8},{12,... | collective-permute-start | bytes 688136 | tf_op jit(solution)/shard_map/ppermute | solution.py:549
  177.9 9.9 %collective-permute-start.32 = (bf16[224,512]{1,0:T(8,128)(2,1)S(1)}, bf16[224,512]{1,0:T(8,128)(2,1)S(1)}, u32[]{:S(2)}, u32[]{:S(2)}) collective-permute-start(bf16[224,512]{1,0:T(8,128)(2,1)S(1)} %add_half.13), channel_id=1, source_target_pairs={{0,2},{2,4},{4,6},{6,0},{1,3},{3,5},{5,7},{7,1},{8,10},{10,12},{12... | collective-permute-start | bytes 688136 | tf_op jit(solution)/shard_map/ppermute | solution.py:549
  182.6 9.1 %collective-permute-start.35 = (bf16[224,512]{1,0:T(8,128)(2,1)S(1)}, bf16[224,512]{1,0:T(8,128)(2,1)S(1)}, u32[]{:S(2)}, u32[]{:S(2)}) collective-permute-start(bf16[224,512]{1,0:T(8,128)(2,1)S(1)} %add_half.14), channel_id=1, source_target_pairs={{0,2},{2,4},{4,6},{6,0},{1,3},{3,5},{5,7},{7,1},{8,10},{10,12},{12... | collective-permute-start | bytes 688136 | tf_op jit(solution)/shard_map/ppermute | solution.py:549
  183.1 8.5 %collective-permute-start.37 = (bf16[224,512]{1,0:T(8,128)(2,1)S(1)}, bf16[224,512]{1,0:T(8,128)(2,1)S(1)}, u32[]{:S(2)}, u32[]{:S(2)}) collective-permute-start(bf16[224,512]{1,0:T(8,128)(2,1)S(1)} %add_half.15), channel_id=1, source_target_pairs={{0,6},{2,0},{4,2},{6,4},{1,7},{3,1},{5,3},{7,5},{8,14},{10,8},{12,... | collective-permute-start | bytes 688136 | tf_op jit(solution)/shard_map/ppermute | solution.py:549
  187.9 14.3 %copy-start.17 = (f32[448]{0:T(512)S(1)}, f32[448]{0:T(512)}, u32[]{:S(2)}) copy-start(f32[448]{0:T(512)} %param.41) | copy-start | bytes 5380
  192.6 1.2 collective-permute-start.38
  193.8 4.3 %collective-permute-start.41 = (f32[1,512]{1,0:T(1,128)S(1)}, f32[1,512]{1,0:T(1,128)S(1)}, u32[]{:S(2)}, u32[]{:S(2)}) collective-permute-start(f32[1,512]{1,0:T(1,128)S(1)} %add.79), channel_id=1, source_target_pairs={{0,6},{2,0},{4,2},{6,4},{1,7},{3,1},{5,3},{7,5},{8,14},{10,8},{12,... | collective-permute-start | bytes 6152 | tf_op jit(solution)/shard_map/ppermute | solution.py:549
  196.7 5.1 %collective-permute-start.40 = (f32[1,512]{1,0:T(1,128)S(1)}, f32[1,512]{1,0:T(1,128)S(1)}, u32[]{:S(2)}, u32[]{:S(2)}) collective-permute-start(f32[1,512]{1,0:T(1,128)S(1)} %add.79), channel_id=1, source_target_pairs={{0,4},{2,6},{4,0},{6,2},{1,5},{3,7},{5,1},{7,3},{8,12},{10,14},{12... | collective-permute-start | bytes 6152 | tf_op jit(solution)/shard_map/ppermute | solution.py:549
  197.3 4.8 %collective-permute-start.39 = (f32[1,512]{1,0:T(1,128)S(1)}, f32[1,512]{1,0:T(1,128)S(1)}, u32[]{:S(2)}, u32[]{:S(2)}) collective-permute-start(f32[1,512]{1,0:T(1,128)S(1)} %add.79), channel_id=1, source_target_pairs={{0,2},{2,4},{4,6},{6,0},{1,3},{3,5},{5,7},{7,1},{8,10},{10,12},{12... | collective-permute-start | bytes 6152 | tf_op jit(solution)/shard_map/ppermute | solution.py:549
  (16 other events, 82.9 us)
Sparse Core Ops, SparseCore 0:
  10.2 140.5 all-gather.2

commit v5 on v4

--- a/solution.py
+++ b/solution.py
@@ -486,6 +486,19 @@
     )(place, rows, inv, weights, weights)
 
 
+def copy_kernel(in_ref, out_ref):
+    out_ref[...] = in_ref[...]
+
+
+def copy_out(value):
+    return pl.pallas_call(
+        copy_kernel,
+        out_shape=jax.ShapeDtypeStruct(value.shape, value.dtype),
+        compiler_params=vmem(4),
+        name="copy_out",
+    )(value)
+
+
 def pages_kernel(table_ref, k_ref, v_ref, out_ref):
     pages = out_ref.shape[2]
     row = lax.broadcasted_iota(jnp.int32, (T, T), 0)
@@ -607,12 +620,11 @@
     )(base, top, low, gain)
 
 
-def hidden_kernel(base_ref, top_ref, low_ref, new_ref, kept_ref, sq_ref):
+def hidden_kernel(base_ref, top_ref, low_ref, kept_ref, sq_ref):
     half = top_ref.shape[0]
     total = jnp.zeros(sq_ref.shape, F32)
     for at, ref in ((slice(0, half), top_ref), (slice(half, 2 * half), low_ref)):
         new = (base_ref[at, :] + ref[...].astype(F32)).astype(BF16)
-        new_ref[at, :] = new
         kept_ref[at, :] = new
         wide = new.astype(F32)
         total = total + jnp.sum(wide * wide, axis=0, keepdims=True)
@@ -623,8 +635,7 @@
     return pl.pallas_call(
         hidden_kernel,
         out_shape=(
-            jax.ShapeDtypeStruct(base.shape, BF16), jax.ShapeDtypeStruct(base.shape, BF16),
-            jax.ShapeDtypeStruct((1, T), F32),
+            jax.ShapeDtypeStruct(base.shape, BF16), jax.ShapeDtypeStruct((1, T), F32)
         ),
         compiler_params=vmem(8),
         name="finish_hidden",
@@ -733,9 +744,8 @@
     blocks = gather_rows(scaled)
     here = jnp.stack([x, core]).astype(jnp.int32)
     rows, inv = prepare(here, blocks, (1.0 / mlp_norm_gain).reshape(4, -1))
-    new_hidden, kept, squares = finish_hidden(
-        *scatter_sum(mlp(place, in_hbm(rows), inv, weights), mixed)
-    )
+    kept, squares = finish_hidden(*scatter_sum(mlp(place, in_hbm(rows), inv, weights), mixed))
+    new_hidden = copy_out(kept)
     widened = kept.astype(F32)
     total_sq = group_sum(squares)
     next_normed = (

time: 212 us -> 211 us (level)
  transfers between devices with their start and end apart: 43 -> 43, of which waited for: 23 -> 22; matrix products, arithmetic and copies ran while one was open for 1% -> 1% of each run, Pallas kernels for 17% -> 17%
where the time goes in v5:
time: 211 us; the launch traced here: 209 us
  waiting for transfers between devices  75.4 us (36%)
  Pallas kernels  59 us (28%)
  starting transfers between devices  50.6 us (24%)
  between operations  14.6 us (7%)
  local copies, waits for them, and re-layouts  6.8 us (3%)
  other arithmetic  2.82 us (1%)
    ppermute x22, waiting for transfers between devices, along(): lax.ppermute(value, 'x', [(i, (i + steps) % count) for i in range(count)])  39.8 us
    ppermute x22, starting transfers between devices, along(): lax.ppermute(value, 'x', [(i, (i + steps) % count) for i in range(count)])  32.3 us
    ppermute x5, waiting for transfers between devices, behind(): return lax.ppermute(value, REQ, pairs)  29.7 us
    pallas_call x1, Pallas kernels, mlp(): pl.pallas_call(mlp_kernel, grid_spec=pltpu.PrefetchScalarGridSpec(num_sca...  20.1 us
    ppermute x5, starting transfers between devices, behind(): return lax.ppermute(value, REQ, pairs)  15.2 us
    pallas_call x1, Pallas kernels, project(): pl.pallas_call(project_kernel, grid_spec=pltpu.PrefetchScalarGridSpec(num...  11.6 us
    unnamed x42, local copies, waits for them, and re-layouts  5.76 us
    ppermute x15, waiting for transfers between devices, swap(): return lax.ppermute(value, 'c', [(0, 1), (1, 0)])  5.62 us
  transfers between devices with their start and end apart: 43, of which 22 were waited for; matrix products, arithmetic and copies ran while one was open for 1% of the time, Pallas kernels for 17%

profile of v5, /device:TPU:96, one launch (start us, length us, event | category | flops | bytes accessed | tf_op | source)
XLA Modules:
  0.0 209.2 jit_solution(8296695654103275170)
XLA Ops:
  7.2 2.1 %stack_three.1 = bf16[3,224,896]{2,1,0:T(8,128)(2,1)} custom-call(bf16[224,896]{1,0:T(8,128)(2,1)} %a_ref.1, bf16[224,896]{1,0:T(8,128)(2,1)} %b_ref.5, bf16[224,896]{1,0:T(8,128)(2,1)} %bitcast.42), custom_call_target="tpu_custom_call" | custom-call | tf_op jit(solution)/shard_map/stack_three/pallas_call | solution.py:543
  9.6 1.0 pad_maximum_fusion
  10.6 3.5 %collective-permute-start.2 = (bf16[912,512]{1,0:T(8,128)(2,1)}, bf16[912,512]{1,0:T(8,128)(2,1)}, u32[]{:S(2)}, u32[]{:S(2)}) collective-permute-start(bf16[912,512]{1,0:T(8,128)(2,1)} %pad_maximum_fusion), channel_id=1, source_target_pairs={{0,8},{8,16},{16,24},{24,32},{32,40},{40,48},{48,56},{56,64},{64,7... | collective-permute-start | bytes 2801672 | tf_op jit(solution)/shard_map/ppermute | solution.py:557
  14.9 4.5 %collective-permute-start.1 = (bf16[464,512]{1,0:T(8,128)(2,1)}, bf16[464,512]{1,0:T(8,128)(2,1)}, u32[]{:S(2)}, u32[]{:S(2)}) collective-permute-start(bf16[464,512]{1,0:T(8,128)(2,1)} %pad_maximum_fusion.1), channel_id=1, source_target_pairs={{8,0},{16,8},{24,16},{32,24},{40,32},{48,40},{56,48},{64,56},{72,6... | collective-permute-start | bytes 1425416 | tf_op jit(solution)/shard_map/ppermute | solution.py:557
  19.4 2.1 %leaving_state.1 = (bf16[80,896]{1,0:T(8,128)(2,1)S(1)}, f32[16,512]{1,0:T(8,128)S(1)}, f32[512,128]{1,0:T(8,128)S(1)}) custom-call(f32[14,512]{1,0:T(8,128)S(1)} %bitcast.38, f32[14,1]{1,0:T(8,128)S(1)} %copy.32.rate_ref, s32[1,512]{1,0:T(1,128)S(1)} %bitcast.33, bf16[512,896]{1,0:T(8,128)(2,1)S(1)} %copy-done.3, bf16[512,128]{1,0:T(8,128)(2,1)S(1)} %copy-done.8), custom_call_target="tpu_custom_call" | custom-call | tf_op jit(solution)/shard_map/leaving_state/pallas_call | solution.py:83
  21.6 1.9 collective-permute-start
  24.0 1.7 cache_pages.1
  25.7 1.3 attend_own.1
  27.0 1.0 copy-done.6
  28.0 4.0 %mamba_local.1.y_ref = f32[512,896]{1,0:T(8,128)S(1)} custom-call(bf16[512,896]{1,0:T(8,128)(2,1)S(1)} %copy-done.3, bf16[512,128]{1,0:T(8,128)(2,1)S(1)} %copy-done.8, bf16[512,128]{1,0:T(8,128)(2,1)S(1)} %copy-done.9, f32[16,512]{1,0:T(8,128)S(1)} %get-tuple-element.46.row_ref, f32[512,128]{1,0:T(8,128)S(1)} %get-tuple-element.47.col_ref, ...), custom_call_target="tpu_custom_call" | custom-call | tf_op jit(solution)/shard_map/mamba_local/pallas_call | solution.py:155
  31.9 1.3 copy-done
  33.4 3.9 %collective-permute-done.1.q_ref = bf16[464,512]{1,0:T(8,128)(2,1)} collective-permute-done((bf16[464,512]{1,0:T(8,128)(2,1)}, bf16[464,512]{1,0:T(8,128)(2,1)}, u32[]{:S(2)}, u32[]{:S(2)}) %collective-permute-start.1) | collective-permute-done | bytes 475168 | tf_op jit(solution)/shard_map/ppermute | solution.py:557
  37.2 13.3 %collective-permute-done.2.kv_ref = bf16[912,512]{1,0:T(8,128)(2,1)} collective-permute-done((bf16[912,512]{1,0:T(8,128)(2,1)}, bf16[912,512]{1,0:T(8,128)(2,1)}, u32[]{:S(2)}, u32[]{:S(2)}) %collective-permute-start.2) | collective-permute-done | bytes 933920 | tf_op jit(solution)/shard_map/ppermute | solution.py:557
  50.5 4.5 %attend_next.1 = bf16[464,512]{1,0:T(8,128)(2,1)} custom-call(bf16[464,512]{1,0:T(8,128)(2,1)} %collective-permute-done.1.q_ref, bf16[448,512]{1,0:T(8,128)(2,1)S(1)} %bitcast.25, bf16[448,512]{1,0:T(8,128)(2,1)S(1)} %bitcast.29, bf16[912,512]{1,0:T(8,128)(2,1)} %collective-permute-done.2.kv_ref, s32[512,1]{1,0:T(8,128)S(1)} %copy.34.segc_ref), custom_call_target="tpu_custom_call" | custom-call | tf_op jit(solution)/shard_map/attend_next/pallas_call | solution.py:284
  55.0 1.9 collective-permute-start.8
  57.0 3.4 %collective-permute-start.3 = (bf16[80,896]{1,0:T(8,128)(2,1)S(1)}, bf16[80,896]{1,0:T(8,128)(2,1)S(1)}, u32[]{:S(2)}, u32[]{:S(2)}) collective-permute-start(bf16[80,896]{1,0:T(8,128)(2,1)S(1)} %pass_through.1), channel_id=1, source_target_pairs={{0,8},{8,16},{16,24},{24,32},{32,40},{40,48},{48,56},{56,64},{64,7... | collective-permute-start | bytes 430088 | tf_op jit(solution)/shard_map/ppermute | solution.py:557
  60.4 12.5 %collective-permute-done.3.carry_ref = bf16[80,896]{1,0:T(8,128)(2,1)S(1)} collective-permute-done((bf16[80,896]{1,0:T(8,128)(2,1)S(1)}, bf16[80,896]{1,0:T(8,128)(2,1)S(1)}, u32[]{:S(2)}, u32[]{:S(2)}) %collective-permute-start.3) | collective-permute-done | bytes 143392 | tf_op jit(solution)/shard_map/ppermute | solution.py:557
  72.9 2.9 %mamba_finish.1 = (f32[512,896]{1,0:T(8,128)S(1)}, f32[2,512]{1,0:T(2,128)S(1)}) custom-call(f32[512,896]{1,0:T(8,128)} %copy-done, bf16[512,896]{1,0:T(8,128)(2,1)S(1)} %copy-done.7, bf16[512,128]{1,0:T(8,128)(2,1)S(1)} %copy-done.9, f32[512,128]{1,0:T(8,128)S(1)} %get-tuple-element.47.col_ref, s32[512,1]{1,0:T(8,128)S(1)} %copy.31.segc_ref, ...), custom_call_target="tpu_custom_call" | custom-call | tf_op jit(solution)/shard_map/mamba_finish/pallas_call | solution.py:191
  76.0 1.2 collective-permute-done.4
  77.1 2.8 %collective-permute-start.7 = (f32[2,512]{1,0:T(2,128)S(1)}, f32[2,512]{1,0:T(2,128)S(1)}, u32[]{:S(2)}, u32[]{:S(2)}) collective-permute-start(f32[2,512]{1,0:T(2,128)S(1)} %add.73), channel_id=1, source_target_pairs={{0,6},{2,0},{4,2},{6,4},{1,7},{3,1},{5,3},{7,5},{8,14},{10,8},{12,... | collective-permute-start | bytes 12296 | tf_op jit(solution)/shard_map/ppermute | solution.py:562
  81.7 3.3 %collective-permute-done.6 = f32[2,512]{1,0:T(2,128)S(1)} collective-permute-done((f32[2,512]{1,0:T(2,128)S(1)}, f32[2,512]{1,0:T(2,128)S(1)}, u32[]{:S(2)}, u32[]{:S(2)}) %collective-permute-start.6) | collective-permute-done | bytes 4128 | tf_op jit(solution)/shard_map/ppermute | solution.py:562
  86.1 1.4 merge.1.att_ref
  87.5 11.6 %project.1 = (f32[448,512]{1,0:T(8,128)S(1)}, bf16[448,512]{1,0:T(8,128)(2,1)S(1)}, f32[448,512]{1,0:T(8,128)S(1)}, bf16[448,512]{1,0:T(8,128)(2,1)S(1)}, f32[44...) custom-call(s32[5]{0:T(128)S(1)} %stack.30.place_ref, ...), custom_call_target="tpu_custom_call" | custom-call | tf_op jit(solution)/shard_map/project/pallas_call | solution.py:369
  101.2 3.2 %collective-permute-start.17 = (bf16[224,512]{1,0:T(8,128)(2,1)S(1)}, bf16[224,512]{1,0:T(8,128)(2,1)S(1)}, u32[]{:S(2)}, u32[]{:S(2)}) collective-permute-start(bf16[224,512]{1,0:T(8,128)(2,1)S(1)} %get-tuple-element.67), channel_id=1, source_target_pairs={{0,6},{2,0},{4,2},{6,4},{1,7},{3,1},{5,3},{7,5},{8,14},{10,8},{12,... | collective-permute-start | bytes 688136 | tf_op jit(solution)/shard_map/ppermute | solution.py:562
  104.6 2.1 collective-permute-start.13
  106.7 4.1 %collective-permute-done.15.refs_0_ = bf16[224,512]{1,0:T(8,128)(2,1)S(1)} collective-permute-done((bf16[224,512]{1,0:T(8,128)(2,1)S(1)}, bf16[224,512]{1,0:T(8,128)(2,1)S(1)}, u32[]{:S(2)}, u32[]{:S(2)}) %collective-permute-start.15) | collective-permute-done | bytes 229408 | tf_op jit(solution)/shard_map/ppermute | solution.py:562
  111.8 3.2 %collective-permute-start.18 = (bf16[224,512]{1,0:T(8,128)(2,1)}, bf16[224,512]{1,0:T(8,128)(2,1)}, u32[]{:S(2)}, u32[]{:S(2)}) collective-permute-start(bf16[224,512]{1,0:T(8,128)(2,1)} %add_half.11), channel_id=1, source_target_pairs={{0,6},{2,0},{4,2},{6,4},{1,7},{3,1},{5,3},{7,5},{8,14},{10,8},{12,... | collective-permute-start | bytes 688136 | tf_op jit(solution)/shard_map/ppermute | solution.py:562
  115.9 3.9 %collective-permute-done.16.top_ref = bf16[224,512]{1,0:T(8,128)(2,1)S(1)} collective-permute-done((bf16[224,512]{1,0:T(8,128)(2,1)S(1)}, bf16[224,512]{1,0:T(8,128)(2,1)S(1)}, u32[]{:S(2)}, u32[]{:S(2)}) %collective-permute-start.16) | collective-permute-done | bytes 229408 | tf_op jit(solution)/shard_map/ppermute | solution.py:562
  119.8 1.1 finish_mixed.1
  120.9 3.1 %collective-permute-start.24 = (bf16[448,512]{1,0:T(8,128)(2,1)S(1)}, bf16[448,512]{1,0:T(8,128)(2,1)S(1)}, u32[]{:S(2)}, u32[]{:S(2)}) collective-permute-start(bf16[448,512]{1,0:T(8,128)(2,1)S(1)} %get-tuple-element.69.refs_0_), channel_id=1, source_target_pairs={{0,6},{2,0},{4,2},{6,4},{1,7},{3,1},{5,3},{7,5},{8,14},{10,8},{12,... | collective-permute-start | bytes 1376264 | tf_op jit(solution)/shard_map/ppermute | solution.py:562
  124.1 8.7 %collective-permute-done.24.refs_8_ = bf16[448,512]{1,0:T(8,128)(2,1)S(1)} collective-permute-done((bf16[448,512]{1,0:T(8,128)(2,1)S(1)}, bf16[448,512]{1,0:T(8,128)(2,1)S(1)}, u32[]{:S(2)}, u32[]{:S(2)}) %collective-permute-start.24) | collective-permute-done | bytes 458784 | tf_op jit(solution)/shard_map/ppermute | solution.py:562
  132.8 3.0 %collective-permute-start.25 = (bf16[224,512]{1,0:T(8,128)(2,1)S(1)}, bf16[224,512]{1,0:T(8,128)(2,1)S(1)}, u32[]{:S(2)}, u32[]{:S(2)}) collective-permute-start(bf16[224,512]{1,0:T(8,128)(2,1)S(1)} %slice.9), channel_id=1, source_target_pairs={{0,6},{2,0},{4,2},{6,4},{1,7},{3,1},{5,3},{7,5},{8,14},{10,8},{12,... | collective-permute-start | bytes 688136 | tf_op jit(solution)/shard_map/ppermute | solution.py:562
  136.5 2.7 %collective-permute-done.25.refs_6_ = bf16[224,512]{1,0:T(8,128)(2,1)S(1)} collective-permute-done((bf16[224,512]{1,0:T(8,128)(2,1)S(1)}, bf16[224,512]{1,0:T(8,128)(2,1)S(1)}, u32[]{:S(2)}, u32[]{:S(2)}) %collective-permute-start.25) | collective-permute-done | bytes 229408 | tf_op jit(solution)/shard_map/ppermute | solution.py:562
  140.0 3.2 %collective-permute-done.22.refs_4_ = bf16[224,512]{1,0:T(8,128)(2,1)} collective-permute-done((bf16[224,512]{1,0:T(8,128)(2,1)S(1)}, bf16[224,512]{1,0:T(8,128)(2,1)}, u32[]{:S(2)}, u32[]{:S(2)}) %collective-permute-start.22) | collective-permute-done | bytes 229408 | tf_op jit(solution)/shard_map/ppermute | solution.py:562
  143.3 1.7 collective-permute-done.23.refs_5_
  146.0 2.7 %prepare.1 = (bf16[512,3584]{1,0:T(8,128)(2,1)S(1)}, f32[512,128]{1,0:T(8,128)S(1)}) custom-call(s32[2]{0:T(128)S(1)} %pad_add_fusion.place_ref, bf16[448,512]{1,0:T(8,128)(2,1)S(1)} %get-tuple-element.69.refs_0_, bf16[448,512]{1,0:T(8,128)(2,1)S(1)} %collective-permute-done.19.refs_1_, bf16[448,512]{1,0:T(8,128)(2,1)S(1)} %collective-permute-done.20.refs_2_, ...), custom_call_target="tpu_custom_call" | custom-call | tf_op jit(solution)/shard_map/prepare/pallas_call | solution.py:417
  148.7 1.8 copy-done.4
  150.8 20.1 %mlp.1 = (f32[448,512]{1,0:T(8,128)S(1)}, bf16[448,512]{1,0:T(8,128)(2,1)S(1)}, f32[448,512]{1,0:T(8,128)S(1)}, bf16[448,512]{1,0:T(8,128)(2,1)S(1)}, f32[448,51...) custom-call(s32[5]{0:T(128)S(1)} %stack.30.place_ref, ...), custom_call_target="tpu_custom_call" | custom-call | tf_op jit(solution)/shard_map/mlp/pallas_call | solution.py:465
  172.9 1.6 collective-permute-start.34
  174.5 1.7 collective-permute-start.36
  176.3 1.6 collective-permute-start.30
  178.5 4.0 %collective-permute-done.34.refs_0_ = bf16[224,512]{1,0:T(8,128)(2,1)S(1)} collective-permute-done((bf16[224,512]{1,0:T(8,128)(2,1)S(1)}, bf16[224,512]{1,0:T(8,128)(2,1)S(1)}, u32[]{:S(2)}, u32[]{:S(2)}) %collective-permute-start.34) | collective-permute-done | bytes 229408 | tf_op jit(solution)/shard_map/ppermute | solution.py:562
  183.1 2.9 %collective-permute-start.37 = (bf16[224,512]{1,0:T(8,128)(2,1)S(1)}, bf16[224,512]{1,0:T(8,128)(2,1)S(1)}, u32[]{:S(2)}, u32[]{:S(2)}) collective-permute-start(bf16[224,512]{1,0:T(8,128)(2,1)S(1)} %add_half.15), channel_id=1, source_target_pairs={{0,6},{2,0},{4,2},{6,4},{1,7},{3,1},{5,3},{7,5},{8,14},{10,8},{12,... | collective-permute-start | bytes 688136 | tf_op jit(solution)/shard_map/ppermute | solution.py:562
  186.1 1.8 collective-permute-done.30.top_ref
  188.1 3.5 %collective-permute-done.35.top_ref = bf16[224,512]{1,0:T(8,128)(2,1)S(1)} collective-permute-done((bf16[224,512]{1,0:T(8,128)(2,1)S(1)}, bf16[224,512]{1,0:T(8,128)(2,1)S(1)}, u32[]{:S(2)}, u32[]{:S(2)}) %collective-permute-start.35) | collective-permute-done | bytes 229408 | tf_op jit(solution)/shard_map/ppermute | solution.py:562
  191.9 1.1 collective-permute-done.38
  193.1 3.0 %collective-permute-start.41 = (f32[1,512]{1,0:T(1,128)S(1)}, f32[1,512]{1,0:T(1,128)S(1)}, u32[]{:S(2)}, u32[]{:S(2)}) collective-permute-start(f32[1,512]{1,0:T(1,128)S(1)} %add.79), channel_id=1, source_target_pairs={{0,6},{2,0},{4,2},{6,4},{1,7},{3,1},{5,3},{7,5},{8,14},{10,8},{12,... | collective-permute-start | bytes 6152 | tf_op jit(solution)/shard_map/ppermute | solution.py:562
  198.0 3.1 %collective-permute-done.40 = f32[1,512]{1,0:T(1,128)S(1)} collective-permute-done((f32[1,512]{1,0:T(1,128)S(1)}, f32[1,512]{1,0:T(1,128)S(1)}, u32[]{:S(2)}, u32[]{:S(2)}) %collective-permute-start.40) | collective-permute-done | bytes 2080 | tf_op jit(solution)/shard_map/ppermute | solution.py:562
  (134 shorter events, 18.5 us)
Async XLA Ops:
  7.2 143.6 %all-gather.3.cloned.1.call-start = ((), (), s32[]{:S(2)}) async-start(), calls=%async_computation | async-start | bytes 20471808 | tf_op jit(solution)/shard_map/all_gather | solution.py:703
  9.5 14.0 %copy-start.19 = (f32[14]{0:T(128)S(1)}, f32[14]{0:T(128)}, u32[]{:S(2)}) copy-start(f32[14]{0:T(128)} %param.33) | copy-start | bytes 172
  9.6 14.1 %copy-start.20 = (s32[1,32]{1,0:T(1,128)S(1)}, s32[1,32]{1,0:T(1,128)}, u32[]{:S(2)}) copy-start(s32[1,32]{1,0:T(1,128)} %param.26) | copy-start | bytes 388
  10.6 40.0 %collective-permute-start.2 = (bf16[912,512]{1,0:T(8,128)(2,1)}, bf16[912,512]{1,0:T(8,128)(2,1)}, u32[]{:S(2)}, u32[]{:S(2)}) collective-permute-start(bf16[912,512]{1,0:T(8,128)(2,1)} %pad_maximum_fusion), channel_id=1, source_target_pairs={{0,8},{8,16},{16,24},{24,32},{32,40},{40,48},{48,56},{56,64},{64,7... | collective-permute-start | bytes 2801672 | tf_op jit(solution)/shard_map/ppermute | solution.py:557
  14.9 22.4 %collective-permute-start.1 = (bf16[464,512]{1,0:T(8,128)(2,1)}, bf16[464,512]{1,0:T(8,128)(2,1)}, u32[]{:S(2)}, u32[]{:S(2)}) collective-permute-start(bf16[464,512]{1,0:T(8,128)(2,1)} %pad_maximum_fusion.1), channel_id=1, source_target_pairs={{8,0},{16,8},{24,16},{32,24},{40,32},{48,40},{56,48},{64,56},{72,6... | collective-permute-start | bytes 1425416 | tf_op jit(solution)/shard_map/ppermute | solution.py:557
  21.6 35.3 %collective-permute-start = (bf16[80,896]{1,0:T(8,128)(2,1)S(1)}, bf16[80,896]{1,0:T(8,128)(2,1)S(1)}, u32[]{:S(2)}, u32[]{:S(2)}) collective-permute-start(bf16[80,896]{1,0:T(8,128)(2,1)S(1)} %get-tuple-element.51.state_ref), channel_id=1, source_target_pairs={{0,8},{8,16},{16,24},{24,32},{32,40},{40,48},{48,56},{56,64},{64,7... | collective-permute-start | bytes 430088 | tf_op jit(solution)/shard_map/ppermute | solution.py:557
  33.4 39.6 %copy-start.7 = (bf16[512,896]{1,0:T(8,128)(2,1)S(1)}, bf16[512,896]{1,0:T(8,128)(2,1)}, u32[]{:S(2)}) copy-start(bf16[512,896]{1,0:T(8,128)(2,1)} %z_ref.1) | copy-start | bytes 2752516
  55.0 31.1 %collective-permute-start.8 = (bf16[464,512]{1,0:T(8,128)(2,1)}, bf16[464,512]{1,0:T(8,128)(2,1)S(1)}, u32[]{:S(2)}, u32[]{:S(2)}) collective-permute-start(bf16[464,512]{1,0:T(8,128)(2,1)} %attend_next.1), channel_id=1, source_target_pairs={{0,8},{8,16},{16,24},{24,32},{32,40},{40,48},{48,56},{56,64},{64,7... | collective-permute-start | bytes 1425416 | tf_op jit(solution)/shard_map/ppermute | solution.py:557
  57.0 24.6 %copy-start.16 = (f32[896]{0:T(1024)S(1)}, f32[896]{0:T(1024)}, u32[]{:S(2)}) copy-start(f32[896]{0:T(1024)} %param.34) | copy-start | bytes 10756
  57.0 16.0 %collective-permute-start.3 = (bf16[80,896]{1,0:T(8,128)(2,1)S(1)}, bf16[80,896]{1,0:T(8,128)(2,1)S(1)}, u32[]{:S(2)}, u32[]{:S(2)}) collective-permute-start(bf16[80,896]{1,0:T(8,128)(2,1)S(1)} %pass_through.1), channel_id=1, source_target_pairs={{0,8},{8,16},{16,24},{24,32},{32,40},{40,48},{48,56},{56,64},{64,7... | collective-permute-start | bytes 430088 | tf_op jit(solution)/shard_map/ppermute | solution.py:557
  75.9 1.2 collective-permute-start.4
  77.1 4.5 %collective-permute-start.7 = (f32[2,512]{1,0:T(2,128)S(1)}, f32[2,512]{1,0:T(2,128)S(1)}, u32[]{:S(2)}, u32[]{:S(2)}) collective-permute-start(f32[2,512]{1,0:T(2,128)S(1)} %add.73), channel_id=1, source_target_pairs={{0,6},{2,0},{4,2},{6,4},{1,7},{3,1},{5,3},{7,5},{8,14},{10,8},{12,... | collective-permute-start | bytes 12296 | tf_op jit(solution)/shard_map/ppermute | solution.py:562
  79.9 5.1 %collective-permute-start.6 = (f32[2,512]{1,0:T(2,128)S(1)}, f32[2,512]{1,0:T(2,128)S(1)}, u32[]{:S(2)}, u32[]{:S(2)}) collective-permute-start(f32[2,512]{1,0:T(2,128)S(1)} %add.73), channel_id=1, source_target_pairs={{0,4},{2,6},{4,0},{6,2},{1,5},{3,7},{5,1},{7,3},{8,12},{10,14},{12... | collective-permute-start | bytes 12296 | tf_op jit(solution)/shard_map/ppermute | solution.py:562
  80.7 4.8 %collective-permute-start.5 = (f32[2,512]{1,0:T(2,128)S(1)}, f32[2,512]{1,0:T(2,128)S(1)}, u32[]{:S(2)}, u32[]{:S(2)}) collective-permute-start(f32[2,512]{1,0:T(2,128)S(1)} %add.73), channel_id=1, source_target_pairs={{0,2},{2,4},{4,6},{6,0},{1,3},{3,5},{5,7},{7,1},{8,10},{10,12},{12... | collective-permute-start | bytes 12296 | tf_op jit(solution)/shard_map/ppermute | solution.py:562
  99.1 1.9 collective-permute-start.14
  99.2 5.2 %collective-permute-start.10 = (bf16[448,512]{1,0:T(8,128)(2,1)S(1)}, bf16[448,512]{1,0:T(8,128)(2,1)S(1)}, u32[]{:S(2)}, u32[]{:S(2)}) collective-permute-start(bf16[448,512]{1,0:T(8,128)(2,1)S(1)} %get-tuple-element.61), channel_id=1, source_target_pairs={{0,1},{1,0},{2,3},{3,2},{4,5},{5,4},{6,7},{7,6},{8,9},{9,8},{10,11... | collective-permute-start | bytes 1376264 | tf_op jit(solution)/shard_map/ppermute | solution.py:566
  99.7 4.8 %collective-permute-start.12 = (bf16[448,512]{1,0:T(8,128)(2,1)S(1)}, bf16[448,512]{1,0:T(8,128)(2,1)S(1)}, u32[]{:S(2)}, u32[]{:S(2)}) collective-permute-start(bf16[448,512]{1,0:T(8,128)(2,1)S(1)} %get-tuple-element.63), channel_id=1, source_target_pairs={{0,1},{1,0},{2,3},{3,2},{4,5},{5,4},{6,7},{7,6},{8,9},{9,8},{10,11... | collective-permute-start | bytes 1376264 | tf_op jit(solution)/shard_map/ppermute | solution.py:566
  99.8 15.4 %collective-permute-start.9 = (bf16[448,512]{1,0:T(8,128)(2,1)}, bf16[448,512]{1,0:T(8,128)(2,1)S(1)}, u32[]{:S(2)}, u32[]{:S(2)}) collective-permute-start(bf16[448,512]{1,0:T(8,128)(2,1)} %get-tuple-element.59), channel_id=1, source_target_pairs={{0,1},{1,0},{2,3},{3,2},{4,5},{5,4},{6,7},{7,6},{8,9},{9,8},{10,11... | collective-permute-start | bytes 1376264 | tf_op jit(solution)/shard_map/ppermute | solution.py:566
  101.1 9.7 %collective-permute-start.15 = (bf16[224,512]{1,0:T(8,128)(2,1)S(1)}, bf16[224,512]{1,0:T(8,128)(2,1)S(1)}, u32[]{:S(2)}, u32[]{:S(2)}) collective-permute-start(bf16[224,512]{1,0:T(8,128)(2,1)S(1)} %get-tuple-element.66), channel_id=1, source_target_pairs={{0,2},{2,4},{4,6},{6,0},{1,3},{3,5},{5,7},{7,1},{8,10},{10,12},{12... | collective-permute-start | bytes 688136 | tf_op jit(solution)/shard_map/ppermute | solution.py:562
  101.2 9.8 %collective-permute-start.17 = (bf16[224,512]{1,0:T(8,128)(2,1)S(1)}, bf16[224,512]{1,0:T(8,128)(2,1)S(1)}, u32[]{:S(2)}, u32[]{:S(2)}) collective-permute-start(bf16[224,512]{1,0:T(8,128)(2,1)S(1)} %get-tuple-element.67), channel_id=1, source_target_pairs={{0,6},{2,0},{4,2},{6,4},{1,7},{3,1},{5,3},{7,5},{8,14},{10,8},{12,... | collective-permute-start | bytes 688136 | tf_op jit(solution)/shard_map/ppermute | solution.py:562
  104.4 10.8 %collective-permute-start.11 = (bf16[224,512]{1,0:T(8,128)(2,1)S(1)}, bf16[224,512]{1,0:T(8,128)(2,1)S(1)}, u32[]{:S(2)}, u32[]{:S(2)}) collective-permute-start(bf16[224,512]{1,0:T(8,128)(2,1)S(1)} %add_half.8), channel_id=1, source_target_pairs={{0,6},{2,0},{4,2},{6,4},{1,7},{3,1},{5,3},{7,5},{8,14},{10,8},{12,... | collective-permute-start | bytes 688136 | tf_op jit(solution)/shard_map/ppermute | solution.py:562
  104.6 11.1 %collective-permute-start.13 = (bf16[224,512]{1,0:T(8,128)(2,1)S(1)}, bf16[224,512]{1,0:T(8,128)(2,1)S(1)}, u32[]{:S(2)}, u32[]{:S(2)}) collective-permute-start(bf16[224,512]{1,0:T(8,128)(2,1)S(1)} %add_half.9), channel_id=1, source_target_pairs={{0,2},{2,4},{4,6},{6,0},{1,3},{3,5},{5,7},{7,1},{8,10},{10,12},{12... | collective-permute-start | bytes 688136 | tf_op jit(solution)/shard_map/ppermute | solution.py:562
  110.9 8.9 %collective-permute-start.16 = (bf16[224,512]{1,0:T(8,128)(2,1)S(1)}, bf16[224,512]{1,0:T(8,128)(2,1)S(1)}, u32[]{:S(2)}, u32[]{:S(2)}) collective-permute-start(bf16[224,512]{1,0:T(8,128)(2,1)S(1)} %add_half.10), channel_id=1, source_target_pairs={{0,2},{2,4},{4,6},{6,0},{1,3},{3,5},{5,7},{7,1},{8,10},{10,12},{12... | collective-permute-start | bytes 688136 | tf_op jit(solution)/shard_map/ppermute | solution.py:562
  111.8 8.1 %collective-permute-start.18 = (bf16[224,512]{1,0:T(8,128)(2,1)}, bf16[224,512]{1,0:T(8,128)(2,1)}, u32[]{:S(2)}, u32[]{:S(2)}) collective-permute-start(bf16[224,512]{1,0:T(8,128)(2,1)} %add_half.11), channel_id=1, source_target_pairs={{0,6},{2,0},{4,2},{6,4},{1,7},{3,1},{5,3},{7,5},{8,14},{10,8},{12,... | collective-permute-start | bytes 688136 | tf_op jit(solution)/shard_map/ppermute | solution.py:562
  120.9 11.8 %collective-permute-start.24 = (bf16[448,512]{1,0:T(8,128)(2,1)S(1)}, bf16[448,512]{1,0:T(8,128)(2,1)S(1)}, u32[]{:S(2)}, u32[]{:S(2)}) collective-permute-start(bf16[448,512]{1,0:T(8,128)(2,1)S(1)} %get-tuple-element.69.refs_0_), channel_id=1, source_target_pairs={{0,6},{2,0},{4,2},{6,4},{1,7},{3,1},{5,3},{7,5},{8,14},{10,8},{12,... | collective-permute-start | bytes 1376264 | tf_op jit(solution)/shard_map/ppermute | solution.py:562
  124.1 11.7 %collective-permute-start.20 = (bf16[448,512]{1,0:T(8,128)(2,1)S(1)}, bf16[448,512]{1,0:T(8,128)(2,1)S(1)}, u32[]{:S(2)}, u32[]{:S(2)}) collective-permute-start(bf16[448,512]{1,0:T(8,128)(2,1)S(1)} %get-tuple-element.69.refs_0_), channel_id=1, source_target_pairs={{0,2},{2,4},{4,6},{6,0},{1,3},{3,5},{5,7},{7,1},{8,10},{10,12},{12... | collective-permute-start | bytes 1376264 | tf_op jit(solution)/shard_map/ppermute | solution.py:562
  132.8 6.5 %collective-permute-start.25 = (bf16[224,512]{1,0:T(8,128)(2,1)S(1)}, bf16[224,512]{1,0:T(8,128)(2,1)S(1)}, u32[]{:S(2)}, u32[]{:S(2)}) collective-permute-start(bf16[224,512]{1,0:T(8,128)(2,1)S(1)} %slice.9), channel_id=1, source_target_pairs={{0,6},{2,0},{4,2},{6,4},{1,7},{3,1},{5,3},{7,5},{8,14},{10,8},{12,... | collective-permute-start | bytes 688136 | tf_op jit(solution)/shard_map/ppermute | solution.py:562
  135.8 7.4 %collective-permute-start.22 = (bf16[224,512]{1,0:T(8,128)(2,1)S(1)}, bf16[224,512]{1,0:T(8,128)(2,1)}, u32[]{:S(2)}, u32[]{:S(2)}) collective-permute-start(bf16[224,512]{1,0:T(8,128)(2,1)S(1)} %slice.8), channel_id=1, source_target_pairs={{0,2},{2,4},{4,6},{6,0},{1,3},{3,5},{5,7},{7,1},{8,10},{10,12},{12... | collective-permute-start | bytes 688136 | tf_op jit(solution)/shard_map/ppermute | solution.py:562
  135.9 7.4 %collective-permute-start.19 = (bf16[448,512]{1,0:T(8,128)(2,1)S(1)}, bf16[448,512]{1,0:T(8,128)(2,1)S(1)}, u32[]{:S(2)}, u32[]{:S(2)}) collective-permute-start(bf16[448,512]{1,0:T(8,128)(2,1)S(1)} %get-tuple-element.69.refs_0_), channel_id=1, source_target_pairs={{0,1},{1,0},{2,3},{3,2},{4,5},{5,4},{6,7},{7,6},{8,9},{9,8},{10,11... | collective-permute-start | bytes 1376264 | tf_op jit(solution)/shard_map/ppermute | solution.py:566
  136.0 7.3 %collective-permute-start.27 = (bf16[448,512]{1,0:T(8,128)(2,1)S(1)}, bf16[448,512]{1,0:T(8,128)(2,1)S(1)}, u32[]{:S(2)}, u32[]{:S(2)}) collective-permute-start(bf16[448,512]{1,0:T(8,128)(2,1)S(1)} %collective-permute-done.24.refs_8_), channel_id=1, source_target_pairs={{0,1},{1,0},{2,3},{3,2},{4,5},{5,4},{6,7},{7,6},{8,9},{9,8},{10,11... | collective-permute-start | bytes 1376264 | tf_op jit(solution)/shard_map/ppermute | solution.py:566
  136.4 8.6 %collective-permute-start.21 = (bf16[448,512]{1,0:T(8,128)(2,1)S(1)}, bf16[448,512]{1,0:T(8,128)(2,1)}, u32[]{:S(2)}, u32[]{:S(2)}) collective-permute-start(bf16[448,512]{1,0:T(8,128)(2,1)S(1)} %collective-permute-done.20.refs_2_), channel_id=1, source_target_pairs={{0,1},{1,0},{2,3},{3,2},{4,5},{5,4},{6,7},{7,6},{8,9},{9,8},{10,11... | collective-permute-start | bytes 1376264 | tf_op jit(solution)/shard_map/ppermute | solution.py:566
  139.3 4.0 %collective-permute-start.26 = (bf16[224,512]{1,0:T(8,128)(2,1)S(1)}, bf16[224,512]{1,0:T(8,128)(2,1)}, u32[]{:S(2)}, u32[]{:S(2)}) collective-permute-start(bf16[224,512]{1,0:T(8,128)(2,1)S(1)} %collective-permute-done.25.refs_6_), channel_id=1, source_target_pairs={{0,1},{1,0},{2,3},{3,2},{4,5},{5,4},{6,7},{7,6},{8,9},{9,8},{10,11... | collective-permute-start | bytes 688136 | tf_op jit(solution)/shard_map/ppermute | solution.py:566
  143.2 1.8 collective-permute-start.23
  170.9 1.9 collective-permute-start.33
  171.1 5.2 %collective-permute-start.29 = (bf16[448,512]{1,0:T(8,128)(2,1)S(1)}, bf16[448,512]{1,0:T(8,128)(2,1)S(1)}, u32[]{:S(2)}, u32[]{:S(2)}) collective-permute-start(bf16[448,512]{1,0:T(8,128)(2,1)S(1)} %get-tuple-element.75), channel_id=1, source_target_pairs={{0,1},{1,0},{2,3},{3,2},{4,5},{5,4},{6,7},{7,6},{8,9},{9,8},{10,11... | collective-permute-start | bytes 1376264 | tf_op jit(solution)/shard_map/ppermute | solution.py:566
  171.5 6.4 %collective-permute-start.31 = (bf16[448,512]{1,0:T(8,128)(2,1)S(1)}, bf16[448,512]{1,0:T(8,128)(2,1)S(1)}, u32[]{:S(2)}, u32[]{:S(2)}) collective-permute-start(bf16[448,512]{1,0:T(8,128)(2,1)S(1)} %get-tuple-element.77), channel_id=1, source_target_pairs={{0,1},{1,0},{2,3},{3,2},{4,5},{5,4},{6,7},{7,6},{8,9},{9,8},{10,11... | collective-permute-start | bytes 1376264 | tf_op jit(solution)/shard_map/ppermute | solution.py:566
  171.6 14.5 %collective-permute-start.28 = (bf16[448,512]{1,0:T(8,128)(2,1)S(1)}, bf16[448,512]{1,0:T(8,128)(2,1)S(1)}, u32[]{:S(2)}, u32[]{:S(2)}) collective-permute-start(bf16[448,512]{1,0:T(8,128)(2,1)S(1)} %get-tuple-element.73), channel_id=1, source_target_pairs={{0,1},{1,0},{2,3},{3,2},{4,5},{5,4},{6,7},{7,6},{8,9},{9,8},{10,11... | collective-permute-start | bytes 1376264 | tf_op jit(solution)/shard_map/ppermute | solution.py:566
  172.9 9.6 %collective-permute-start.34 = (bf16[224,512]{1,0:T(8,128)(2,1)S(1)}, bf16[224,512]{1,0:T(8,128)(2,1)S(1)}, u32[]{:S(2)}, u32[]{:S(2)}) collective-permute-start(bf16[224,512]{1,0:T(8,128)(2,1)S(1)} %get-tuple-element.80), channel_id=1, source_target_pairs={{0,2},{2,4},{4,6},{6,0},{1,3},{3,5},{5,7},{7,1},{8,10},{10,12},{12... | collective-permute-start | bytes 688136 | tf_op jit(solution)/shard_map/ppermute | solution.py:562
  174.5 8.6 %collective-permute-start.36 = (bf16[224,512]{1,0:T(8,128)(2,1)S(1)}, bf16[224,512]{1,0:T(8,128)(2,1)S(1)}, u32[]{:S(2)}, u32[]{:S(2)}) collective-permute-start(bf16[224,512]{1,0:T(8,128)(2,1)S(1)} %get-tuple-element.81), channel_id=1, source_target_pairs={{0,6},{2,0},{4,2},{6,4},{1,7},{3,1},{5,3},{7,5},{8,14},{10,8},{12,... | collective-permute-start | bytes 688136 | tf_op jit(solution)/shard_map/ppermute | solution.py:562
  176.3 11.6 %collective-permute-start.30 = (bf16[224,512]{1,0:T(8,128)(2,1)S(1)}, bf16[224,512]{1,0:T(8,128)(2,1)S(1)}, u32[]{:S(2)}, u32[]{:S(2)}) collective-permute-start(bf16[224,512]{1,0:T(8,128)(2,1)S(1)} %add_half.12), channel_id=1, source_target_pairs={{0,6},{2,0},{4,2},{6,4},{1,7},{3,1},{5,3},{7,5},{8,14},{10,8},{12,... | collective-permute-start | bytes 688136 | tf_op jit(solution)/shard_map/ppermute | solution.py:562
  177.9 9.9 %collective-permute-start.32 = (bf16[224,512]{1,0:T(8,128)(2,1)S(1)}, bf16[224,512]{1,0:T(8,128)(2,1)S(1)}, u32[]{:S(2)}, u32[]{:S(2)}) collective-permute-start(bf16[224,512]{1,0:T(8,128)(2,1)S(1)} %add_half.13), channel_id=1, source_target_pairs={{0,2},{2,4},{4,6},{6,0},{1,3},{3,5},{5,7},{7,1},{8,10},{10,12},{12... | collective-permute-start | bytes 688136 | tf_op jit(solution)/shard_map/ppermute | solution.py:562
  182.6 9.1 %collective-permute-start.35 = (bf16[224,512]{1,0:T(8,128)(2,1)S(1)}, bf16[224,512]{1,0:T(8,128)(2,1)S(1)}, u32[]{:S(2)}, u32[]{:S(2)}) collective-permute-start(bf16[224,512]{1,0:T(8,128)(2,1)S(1)} %add_half.14), channel_id=1, source_target_pairs={{0,2},{2,4},{4,6},{6,0},{1,3},{3,5},{5,7},{7,1},{8,10},{10,12},{12... | collective-permute-start | bytes 688136 | tf_op jit(solution)/shard_map/ppermute | solution.py:562
  183.1 8.5 %collective-permute-start.37 = (bf16[224,512]{1,0:T(8,128)(2,1)S(1)}, bf16[224,512]{1,0:T(8,128)(2,1)S(1)}, u32[]{:S(2)}, u32[]{:S(2)}) collective-permute-start(bf16[224,512]{1,0:T(8,128)(2,1)S(1)} %add_half.15), channel_id=1, source_target_pairs={{0,6},{2,0},{4,2},{6,4},{1,7},{3,1},{5,3},{7,5},{8,14},{10,8},{12,... | collective-permute-start | bytes 688136 | tf_op jit(solution)/shard_map/ppermute | solution.py:562
  188.1 13.4 %copy-start.17 = (f32[448]{0:T(512)S(1)}, f32[448]{0:T(512)}, u32[]{:S(2)}) copy-start(f32[448]{0:T(512)} %param.41) | copy-start | bytes 5380
  191.9 1.2 collective-permute-start.38
  193.1 4.9 %collective-permute-start.41 = (f32[1,512]{1,0:T(1,128)S(1)}, f32[1,512]{1,0:T(1,128)S(1)}, u32[]{:S(2)}, u32[]{:S(2)}) collective-permute-start(f32[1,512]{1,0:T(1,128)S(1)} %add.79), channel_id=1, source_target_pairs={{0,6},{2,0},{4,2},{6,4},{1,7},{3,1},{5,3},{7,5},{8,14},{10,8},{12,... | collective-permute-start | bytes 6152 | tf_op jit(solution)/shard_map/ppermute | solution.py:562
  196.0 5.1 %collective-permute-start.40 = (f32[1,512]{1,0:T(1,128)S(1)}, f32[1,512]{1,0:T(1,128)S(1)}, u32[]{:S(2)}, u32[]{:S(2)}) collective-permute-start(f32[1,512]{1,0:T(1,128)S(1)} %add.79), channel_id=1, source_target_pairs={{0,4},{2,6},{4,0},{6,2},{1,5},{3,7},{5,1},{7,3},{8,12},{10,14},{12... | collective-permute-start | bytes 6152 | tf_op jit(solution)/shard_map/ppermute | solution.py:562
  196.6 4.8 %collective-permute-start.39 = (f32[1,512]{1,0:T(1,128)S(1)}, f32[1,512]{1,0:T(1,128)S(1)}, u32[]{:S(2)}, u32[]{:S(2)}) collective-permute-start(f32[1,512]{1,0:T(1,128)S(1)} %add.79), channel_id=1, source_target_pairs={{0,2},{2,4},{4,6},{6,0},{1,3},{3,5},{5,7},{7,1},{8,10},{10,12},{12... | collective-permute-start | bytes 6152 | tf_op jit(solution)/shard_map/ppermute | solution.py:562
  (16 other events, 82.9 us)
Sparse Core Ops, SparseCore 0:
  10.2 140.5 all-gather.2
